TPU v7x, 32 devices: a whole 2x2x4 slice. The times are simulated.
32 devices in a mesh: ta: 4 (over z), ha: 4 (over y, x), wa: 2 (over core).
Axes of the slice: x: 2, y: 2, z: 4, core: 2. Of those that a mesh axis runs over, the one named last changes fastest.
Arguments:
- queries: bfloat16 [16, 16, 4, 4, 1536], P('ta', 'ha', 'wa'), may hold values from -4.5 to 4.5
- key_states: bfloat16 [16, 16, 4, 4, 1536], P('ta', 'ha', 'wa'), may hold values from -4.5 to 4.5
- value_states: bfloat16 [16, 16, 4, 4, 1536], P('ta', 'ha', 'wa'), may hold values from -6 to 6
- output_cotangent: bfloat16 [16, 16, 4, 4, 1536], P('ta', 'ha', 'wa'), may hold values from -48 to 48
- tile_valid: int32 [16, 16, 4], replicated, may hold values from 0 to 1, as said below
- window_radius: int32 [12, 3], replicated, may hold values from 0 to 1
Outputs:
- query_gradient: bfloat16 [16, 16, 4, 4, 1536], P('ta', 'ha', 'wa')
- key_gradient: bfloat16 [16, 16, 4, 4, 1536], P('ta', 'ha', 'wa')
- value_gradient: bfloat16 [16, 16, 4, 4, 1536], P('ta', 'ha', 'wa')
Inputs may be any that keep to these rules, and one draw needn't show every extreme that they name: `tile_valid`: 0 exactly on the first zero or one and the last zero to two tile layers along each axis (padding at the clip's borders), with at least one such layer in all, 1 everywhere else.
All inputs are finite; a program needn't handle non-finite values.
Results may differ from a plain program's by a relative error of at most 0.0084.
Values may be sent and summed in bfloat16 or wider, within the bound.
No kernel may reach another device: no remote copies, remote signals or barrier semaphores. Data moves between devices by JAX's collectives and lax.ppermute only.
A program may use at most 64 MiB of HBM per device.

v0:
```python
import math

import jax
import jax.numpy as jnp
from jax import lax
from jax.sharding import PartitionSpec as P

NEG_FILL = -1e30


def with_halo(x, sides, width):
    for axis, dim in sides:
        devices, length = (lax.axis_size(axis), x.shape[dim])
        up = [(i, (i + 1) % devices) for i in range(devices - 1)]
        down = [(j, i) for i, j in up]
        last = lax.slice_in_dim(x, length - width, length, axis=dim)
        first = lax.slice_in_dim(x, 0, width, axis=dim)
        before = lax.ppermute(last, axis, up)
        after = lax.ppermute(first, axis, down)
        x = jnp.concatenate([before, x, after], axis=dim)
    return x


def axis_window(query_coords, key_coords, radius, grid_length):
    window_start = query_coords[None, :] - radius[:, None]
    window_span = 2 * radius + 1
    above_start = key_coords[None, None, :] >= window_start[:, :, None]
    below_end = key_coords[None, None, :] < window_start[:, :, None] + window_span[:, None, None]
    inside = (query_coords >= 0) & (query_coords < grid_length)
    key_inside = (key_coords >= 0) & (key_coords < grid_length)
    return above_start & below_end & inside[None, :, None] & key_inside[None, None, :]


def tile_mask(query_coords, key_coords, window_radius, grid_sizes, key_valid):
    time_window = axis_window(query_coords[0], key_coords[0], window_radius[:, 0], grid_sizes[0])
    row_window = axis_window(query_coords[1], key_coords[1], window_radius[:, 1], grid_sizes[1])
    column_window = axis_window(query_coords[2], key_coords[2], window_radius[:, 2], grid_sizes[2])
    within = (
        time_window[:, :, None, None, :, None, None]
        & row_window[:, None, :, None, None, :, None]
        & column_window[:, None, None, :, None, None, :]
    )
    time_same = query_coords[0][:, None] == key_coords[0][None, :]
    row_same = query_coords[1][:, None] == key_coords[1][None, :]
    column_same = query_coords[2][:, None] == key_coords[2][None, :]
    same_tile = (
        time_same[:, None, None, :, None, None]
        & row_same[None, :, None, None, :, None]
        & column_same[None, None, :, None, None, :]
    )
    usable = key_valid[None, None, None, :, :, :] | same_tile
    allowed = within & usable[None]
    head_count = window_radius.shape[0]
    query_tiles = query_coords[0].shape[0] * query_coords[1].shape[0] * query_coords[2].shape[0]
    key_tiles = key_coords[0].shape[0] * key_coords[1].shape[0] * key_coords[2].shape[0]
    return allowed.reshape(head_count, query_tiles, key_tiles)


def expand_mask(scores, allowed, tile_cells):
    group_count, row_count, column_count = scores.shape
    shaped = scores.reshape(
        group_count, row_count // tile_cells, tile_cells, column_count // tile_cells, tile_cells
    )
    shaped = jnp.where(allowed[:, :, None, :, None], shaped, NEG_FILL)
    return shaped.reshape(group_count, row_count, column_count)


def query_side(
    own_queries, own_cotangent, outer_keys, outer_values, allowed, tile_cells, score_scale
):
    scores = (
        jnp.einsum("qhd,khd->hqk", own_queries, outer_keys, preferred_element_type=jnp.float32)
        * score_scale
    )
    scores = expand_mask(scores, allowed, tile_cells)
    row_peak = jnp.max(scores, axis=2, keepdims=True)
    logsum = row_peak + jnp.log(jnp.sum(jnp.exp(scores - row_peak), axis=2, keepdims=True))
    attention = jnp.exp(scores - logsum)
    weights_low = attention.astype(jnp.bfloat16)
    output = jnp.einsum(
        "hqk,khd->qhd", weights_low, outer_values, preferred_element_type=jnp.float32
    )
    drift = jnp.sum(own_cotangent.astype(jnp.float32) * output, axis=2)
    weight_grads = jnp.einsum(
        "qhd,khd->hqk", own_cotangent, outer_values, preferred_element_type=jnp.float32
    )
    score_grads = (attention * (weight_grads - drift.T[:, :, None])).astype(jnp.bfloat16)
    query_gradient = (
        jnp.einsum("hqk,khd->qhd", score_grads, outer_keys, preferred_element_type=jnp.float32)
        * score_scale
    )
    return (logsum[:, :, 0].T, drift, weights_low, score_grads, query_gradient)


def key_side(
    outer_queries,
    outer_cotangent,
    outer_logsum,
    outer_drift,
    own_keys,
    own_values,
    allowed,
    tile_cells,
    score_scale,
):
    scores = (
        jnp.einsum("qhd,khd->hqk", outer_queries, own_keys, preferred_element_type=jnp.float32)
        * score_scale
    )
    scores = expand_mask(scores, allowed, tile_cells)
    attention = jnp.exp(scores - outer_logsum.T[:, :, None])
    weights_low = attention.astype(jnp.bfloat16)
    weight_grads = jnp.einsum(
        "qhd,khd->hqk", outer_cotangent, own_values, preferred_element_type=jnp.float32
    )
    score_grads = (attention * (weight_grads - outer_drift.T[:, :, None])).astype(jnp.bfloat16)
    key_gradient = (
        jnp.einsum("hqk,qhd->khd", score_grads, outer_queries, preferred_element_type=jnp.float32)
        * score_scale
    )
    value_gradient = jnp.einsum(
        "hqk,qhd->khd", weights_low, outer_cotangent, preferred_element_type=jnp.float32
    )
    return (key_gradient, value_gradient)


def per_device(queries, key_states, value_states, output_cotangent, tile_valid, window_radius):
    tiles_time, tiles_rows, tiles_columns, tile_cells, full_width = queries.shape
    head_count = window_radius.shape[0]
    head_depth = full_width // head_count
    score_scale = 1.0 / math.sqrt(head_depth)
    head_group = math.gcd(head_count, 4)
    grid_sizes = (
        tiles_time * lax.axis_size("ta"),
        tiles_rows * lax.axis_size("ha"),
        tiles_columns * lax.axis_size("wa"),
    )
    anchor_time = lax.axis_index("ta") * tiles_time
    anchor_rows = lax.axis_index("ha") * tiles_rows
    anchor_columns = lax.axis_index("wa") * tiles_columns
    own_rows_coords = anchor_rows + jnp.arange(tiles_rows, dtype=jnp.int32)
    own_column_coords = anchor_columns + jnp.arange(tiles_columns, dtype=jnp.int32)
    outer_rows_coords = anchor_rows - 1 + jnp.arange(tiles_rows + 2, dtype=jnp.int32)
    outer_column_coords = anchor_columns - 1 + jnp.arange(tiles_columns + 2, dtype=jnp.int32)
    valid_padded = jnp.pad(tile_valid, 1)
    outer_valid = (
        lax.dynamic_slice(
            valid_padded,
            (anchor_time, anchor_rows, anchor_columns),
            (tiles_time + 2, tiles_rows + 2, tiles_columns + 2),
        )
        > 0
    )
    own_valid = (
        lax.dynamic_slice(
            tile_valid,
            (anchor_time, anchor_rows, anchor_columns),
            (tiles_time, tiles_rows, tiles_columns),
        )
        > 0
    )
    slab_rows = tiles_rows * tiles_columns * tile_cells
    slab_shape = (tiles_rows, tiles_columns, tile_cells, full_width)
    slab_ids = jnp.arange(tiles_time, dtype=jnp.int32)
    rim_pair = with_halo(
        jnp.stack([key_states, value_states]), (("ta", 1), ("ha", 2), ("wa", 3)), 1
    )

    def own_time(slab):
        return anchor_time + slab + jnp.arange(1, dtype=jnp.int32)

    def outer_time(slab):
        return anchor_time - 1 + slab + jnp.arange(3, dtype=jnp.int32)

    def query_inputs(slab):
        own_queries = lax.dynamic_index_in_dim(queries, slab, 0, keepdims=False).reshape(
            slab_rows, head_count, head_depth
        )
        own_cotangent = lax.dynamic_index_in_dim(output_cotangent, slab, 0, keepdims=False).reshape(
            slab_rows, head_count, head_depth
        )
        keys_slab = lax.dynamic_slice_in_dim(rim_pair[0], slab, 3, 0).reshape(
            -1, head_count, head_depth
        )
        values_slab = lax.dynamic_slice_in_dim(rim_pair[1], slab, 3, 0).reshape(
            -1, head_count, head_depth
        )
        valid_slab = lax.dynamic_slice_in_dim(outer_valid, slab, 3, 0)
        forward_mask = tile_mask(
            (own_time(slab), own_rows_coords, own_column_coords),
            (outer_time(slab), outer_rows_coords, outer_column_coords),
            window_radius,
            grid_sizes,
            valid_slab,
        )
        return (own_queries, own_cotangent, keys_slab, values_slab, forward_mask)

    query_pair = with_halo(
        jnp.stack([queries, output_cotangent]), (("ta", 1), ("ha", 2), ("wa", 3)), 1
    )
    stat_slab_shape = (tiles_rows, tiles_columns, tile_cells, head_count)

    def query_step(slab):
        own_queries, own_cotangent, keys_slab, values_slab, forward_mask = query_inputs(slab)
        query_pieces = []
        logsum_pieces = []
        drift_pieces = []
        for begin_head in range(0, head_count, head_group):
            end_head = begin_head + head_group
            logsum, drift, weights_low, score_grads, query_piece = query_side(
                own_queries[:, begin_head:end_head],
                own_cotangent[:, begin_head:end_head],
                keys_slab[:, begin_head:end_head],
                values_slab[:, begin_head:end_head],
                forward_mask[begin_head:end_head],
                tile_cells,
                score_scale,
            )
            query_pieces.append(query_piece)
            logsum_pieces.append(logsum)
            drift_pieces.append(drift)
        return (
            jnp.concatenate(query_pieces, axis=1).reshape(slab_shape).astype(jnp.bfloat16),
            jnp.concatenate(logsum_pieces, axis=1).reshape(stat_slab_shape),
            jnp.concatenate(drift_pieces, axis=1).reshape(stat_slab_shape),
        )

    query_gradient, logsum_all, drift_all = lax.map(query_step, slab_ids)
    statistics = jnp.stack([logsum_all, drift_all])
    outer_stats = with_halo(statistics, (("ta", 1), ("ha", 2), ("wa", 3)), 1)

    def key_step(slab):
        own_keys = lax.dynamic_index_in_dim(key_states, slab, 0, keepdims=False).reshape(
            slab_rows, head_count, head_depth
        )
        own_values = lax.dynamic_index_in_dim(value_states, slab, 0, keepdims=False).reshape(
            slab_rows, head_count, head_depth
        )
        outer_queries = lax.dynamic_slice_in_dim(query_pair[0], slab, 3, 0).reshape(
            -1, head_count, head_depth
        )
        outer_cotangent = lax.dynamic_slice_in_dim(query_pair[1], slab, 3, 0).reshape(
            -1, head_count, head_depth
        )
        outer_logsum = lax.dynamic_slice_in_dim(outer_stats[0], slab, 3, 0).reshape(-1, head_count)
        outer_drift = lax.dynamic_slice_in_dim(outer_stats[1], slab, 3, 0).reshape(-1, head_count)
        valid_slab = lax.dynamic_slice_in_dim(own_valid, slab, 1, 0)
        backward_mask = tile_mask(
            (outer_time(slab), outer_rows_coords, outer_column_coords),
            (own_time(slab), own_rows_coords, own_column_coords),
            window_radius,
            grid_sizes,
            valid_slab,
        )
        key_pieces = []
        value_pieces = []
        for begin_head in range(0, head_count, head_group):
            end_head = begin_head + head_group
            key_piece, value_piece = key_side(
                outer_queries[:, begin_head:end_head],
                outer_cotangent[:, begin_head:end_head],
                outer_logsum[:, begin_head:end_head],
                outer_drift[:, begin_head:end_head],
                own_keys[:, begin_head:end_head],
                own_values[:, begin_head:end_head],
                backward_mask[begin_head:end_head],
                tile_cells,
                score_scale,
            )
            key_pieces.append(key_piece)
            value_pieces.append(value_piece)
        return (
            jnp.concatenate(key_pieces, axis=1).reshape(slab_shape).astype(jnp.bfloat16),
            jnp.concatenate(value_pieces, axis=1).reshape(slab_shape).astype(jnp.bfloat16),
        )

    key_gradient, value_gradient = lax.map(key_step, slab_ids)
    return (query_gradient, key_gradient, value_gradient)


def solution(mesh):
    return jax.shard_map(
        per_device,
        mesh=mesh,
        in_specs=(
            P("ta", "ha", "wa", None, None),
            P("ta", "ha", "wa", None, None),
            P("ta", "ha", "wa", None, None),
            P("ta", "ha", "wa", None, None),
            P(),
            P(),
        ),
        out_specs=(
            P("ta", "ha", "wa", None, None),
            P("ta", "ha", "wa", None, None),
            P("ta", "ha", "wa", None, None),
        ),
        check_vma=False,
    )
```

profile of v0, /device:TPU:21, one launch (start us, length us, event | category | flops | bytes accessed | tf_op | source)
XLA Modules:
  0.0 849.9 jit_solution(2197075619087802944)
XLA Ops:
  4.3 3.2 collective-permute-start
  11.7 3.2 collective-permute-start.6
  16.4 3.0 collective-permute-start.3
  23.0 3.9 collective-permute-start.9
  33.9 6.9 collective-permute-start.5
  48.5 5.5 collective-permute-start.11
  55.4 3.1 pad_maximum_fusion.5
  59.9 361.3 %while.32 = (s32[]{:T(128)}, bf16[4,4,2,4,1536]{4,3,2,1,0:T(4,128)(2,1)}, f32[4,4,2,4,12]{4,3,2,1,0:T(4,128)}, f32[4,4,2,4,12]{4,3,2,1,0:T(4,128)}, bf16[2,6,6,4...) while((s32[]{:T(128)}, ...), condition=%wide.region_10.11_spmd.clone, body=%wide.region_0.10_spmd.clone.sunk | while | flops 114825952 | bytes 34916652 | solution.py:228
  59.9 4.1 fusion.251
  69.8 2.7 reshape.1105
  72.5 2.7 fusion.252
  76.5 2.8 reshape.1106
  97.7 3.3 broadcast_in_dim.242
  120.5 3.3 broadcast_in_dim.245
  131.5 3.3 broadcast_in_dim.248
  150.2 4.1 fusion.251
  160.1 2.7 reshape.1105
  162.8 2.7 fusion.252
  166.8 2.8 reshape.1106
  188.0 3.3 broadcast_in_dim.242
  210.8 3.3 broadcast_in_dim.245
  221.8 3.3 broadcast_in_dim.248
  240.5 4.1 fusion.251
  250.4 2.7 reshape.1105
  253.1 2.7 fusion.252
  257.1 2.8 reshape.1106
  278.3 3.3 broadcast_in_dim.242
  301.1 3.3 broadcast_in_dim.245
  312.1 3.3 broadcast_in_dim.248
  330.8 4.1 fusion.251
  340.7 2.7 reshape.1105
  347.4 2.8 reshape.1106
  368.7 3.3 broadcast_in_dim.242
  391.4 3.3 broadcast_in_dim.245
  402.5 3.3 broadcast_in_dim.248
  424.0 3.2 collective-permute-start.12
  431.4 3.6 collective-permute-start.14
  438.1 6.5 collective-permute-start.17
  446.2 5.5 pad_maximum_fusion.6
  455.1 394.9 %while.33 = (s32[]{:T(128)}, bf16[4,4,2,4,1536]{4,3,2,1,0:T(4,128)(2,1)}, bf16[4,4,2,4,1536]{4,3,2,1,0:T(4,128)(2,1)}, bf16[2,6,6,4,4,1536]{5,4,3,2,1,0:T(4,128)...) while((s32[]{:T(128)}, ...), condition=%wide.region_12.13_spmd.clone, body=%wide.region_11.12_spmd.clone.sunk | while | flops 114382960 | bytes 28493196 | solution.py:277
  455.1 4.1 fusion.287
  464.6 2.7 reshape.1109
  487.9 3.3 broadcast_in_dim.254
  493.6 2.8 reshape.1110
  512.4 3.3 broadcast_in_dim.257
  522.7 3.3 broadcast_in_dim.260
  553.8 4.1 fusion.287
  563.3 2.7 reshape.1109
  586.6 3.3 broadcast_in_dim.254
  592.4 2.8 reshape.1110
  611.1 3.3 broadcast_in_dim.257
  621.4 3.3 broadcast_in_dim.260
  652.5 4.1 fusion.287
  662.0 2.7 reshape.1109
  685.3 3.3 broadcast_in_dim.254
  691.0 2.8 reshape.1110
  709.8 3.3 broadcast_in_dim.257
  720.1 3.3 broadcast_in_dim.260
  751.2 4.1 fusion.287
  760.7 2.7 reshape.1109
  784.1 3.3 broadcast_in_dim.254
  789.8 2.8 reshape.1110
  808.6 3.3 broadcast_in_dim.257
  818.9 3.3 broadcast_in_dim.260
  (807 shorter events, 600.5 us)
Async XLA Ops:
  0.6 14.5 %copy-start.7 = (bf16[4,4,2,4,1536]{4,3,2,1,0:T(4,128)(2,1)S(1)}, bf16[4,4,2,4,1536]{4,3,2,1,0:T(4,128)(2,1)}, u32[]{:S(2)}) copy-start(bf16[4,4,2,4,1536]{4,3,2,1,0:T(4,128)(2,1)} %param.12) | copy-start | bytes 1179652
  0.6 14.5 %copy-start.9 = (bf16[4,4,2,4,1536]{4,3,2,1,0:T(4,128)(2,1)S(1)}, bf16[4,4,2,4,1536]{4,3,2,1,0:T(4,128)(2,1)}, u32[]{:S(2)}) copy-start(bf16[4,4,2,4,1536]{4,3,2,1,0:T(4,128)(2,1)} %param.11) | copy-start | bytes 1179652
  0.7 14.2 %copy-start.41 = (s32[16,16,4]{1,2,0:T(4,128)S(1)}, s32[16,16,4]{1,2,0:T(4,128)}, u32[]{:S(2)}) copy-start(s32[16,16,4]{1,2,0:T(4,128)} %param.14) | copy-start | bytes 12292
  2.1 20.3 %copy-start.5 = (bf16[4,4,2,4,1536]{4,3,2,1,0:T(4,128)(2,1)S(1)}, bf16[4,4,2,4,1536]{4,3,2,1,0:T(4,128)(2,1)}, u32[]{:S(2)}) copy-start(bf16[4,4,2,4,1536]{4,3,2,1,0:T(4,128)(2,1)} %param.10) | copy-start | bytes 1179652
  2.1 20.3 %copy-start.6 = (bf16[4,4,2,4,1536]{4,3,2,1,0:T(4,128)(2,1)S(1)}, bf16[4,4,2,4,1536]{4,3,2,1,0:T(4,128)(2,1)}, u32[]{:S(2)}) copy-start(bf16[4,4,2,4,1536]{4,3,2,1,0:T(4,128)(2,1)} %param.13) | copy-start | bytes 1179652
  2.1 13.0 %collective-permute-start.1 = (bf16[2,1,4,2,4,1536]{5,4,3,2,1,0:T(4,128)(2,1)S(1)}, bf16[2,1,4,2,4,1536]{5,4,3,2,1,0:T(4,128)(2,1)S(1)}, u32[]{:S(2)}, u32[]{:S(2)}) collective-permute-start(bf16[2,1,4,2,4,1536]{5,4,3,2,1,0:T(4,128)(2,1)S(1)} %get-tuple-element.592), channel_id=1, source_target_pairs={{8,0},{16,8},{24,16},{9,1},{17,9},{25,17},{10,2},{18,10},{26,18},{... | collective-permute-start | bytes 589832 | tf_op jit(solution)/shard_map/ppermute | solution.py:19
  4.3 10.8 %collective-permute-start = (bf16[2,1,4,2,4,1536]{5,4,3,2,1,0:T(4,128)(2,1)S(1)}, bf16[2,1,4,2,4,1536]{5,4,3,2,1,0:T(4,128)(2,1)S(1)}, u32[]{:S(2)}, u32[]{:S(2)}) collective-permute-start(bf16[2,1,4,2,4,1536]{5,4,3,2,1,0:T(4,128)(2,1)S(1)} %get-tuple-element.591), channel_id=1, source_target_pairs={{0,8},{8,16},{16,24},{1,9},{9,17},{17,25},{2,10},{10,18},{18,26},{... | collective-permute-start | bytes 589832 | tf_op jit(solution)/shard_map/ppermute | solution.py:18
  9.6 12.8 %collective-permute-start.7 = (bf16[2,1,4,2,4,1536]{5,4,3,2,1,0:T(4,128)(2,1)}, bf16[2,1,4,2,4,1536]{5,4,3,2,1,0:T(4,128)(2,1)S(1)}, u32[]{:S(2)}, u32[]{:S(2)}) collective-permute-start(bf16[2,1,4,2,4,1536]{5,4,3,2,1,0:T(4,128)(2,1)} %get-tuple-element.590), channel_id=1, source_target_pairs={{8,0},{16,8},{24,16},{9,1},{17,9},{25,17},{10,2},{18,10},{26,18},{... | collective-permute-start | bytes 589832 | tf_op jit(solution)/shard_map/ppermute | solution.py:19
  11.7 10.7 %collective-permute-start.6 = (bf16[2,1,4,2,4,1536]{5,4,3,2,1,0:T(4,128)(2,1)}, bf16[2,1,4,2,4,1536]{5,4,3,2,1,0:T(4,128)(2,1)S(1)}, u32[]{:S(2)}, u32[]{:S(2)}) collective-permute-start(bf16[2,1,4,2,4,1536]{5,4,3,2,1,0:T(4,128)(2,1)} %get-tuple-element.589), channel_id=1, source_target_pairs={{0,8},{8,16},{16,24},{1,9},{9,17},{17,25},{2,10},{10,18},{18,26},{... | collective-permute-start | bytes 589832 | tf_op jit(solution)/shard_map/ppermute | solution.py:18
  15.1 7.9 copy-start.29
  15.1 16.4 %copy-start.16 = (bf16[2,1,4,2,4,1536]{5,4,3,2,1,0:T(4,128)(2,1)}, bf16[2,1,4,2,4,1536]{5,4,3,2,1,0:T(4,128)(2,1)S(1)}, u32[]{:S(2)}) copy-start(bf16[2,1,4,2,4,1536]{5,4,3,2,1,0:T(4,128)(2,1)S(1)} %collective-permute-done.1) | copy-start | bytes 589828
  15.1 16.4 %copy-start.18 = (bf16[2,1,4,2,4,1536]{5,4,3,2,1,0:T(4,128)(2,1)}, bf16[2,1,4,2,4,1536]{5,4,3,2,1,0:T(4,128)(2,1)S(1)}, u32[]{:S(2)}) copy-start(bf16[2,1,4,2,4,1536]{5,4,3,2,1,0:T(4,128)(2,1)S(1)} %collective-permute-done) | copy-start | bytes 589828
  16.4 12.5 %collective-permute-start.3 = (bf16[2,6,1,2,4,1536]{5,4,3,2,1,0:T(4,128)(2,1)}, bf16[2,6,1,2,4,1536]{5,4,3,2,1,0:T(4,128)(2,1)S(1)}, u32[]{:S(2)}, u32[]{:S(2)}) collective-permute-start(bf16[2,6,1,2,4,1536]{5,4,3,2,1,0:T(4,128)(2,1)} %get-tuple-element.588), channel_id=1, source_target_pairs={{2,0},{4,2},{6,4},{3,1},{5,3},{7,5},{10,8},{12,10},{14,12},{11,9},... | collective-permute-start | bytes 884744 | tf_op jit(solution)/shard_map/ppermute | solution.py:19
  19.5 12.1 %collective-permute-start.2 = (bf16[2,6,1,2,4,1536]{5,4,3,2,1,0:T(4,128)(2,1)S(1)}, bf16[2,6,1,2,4,1536]{5,4,3,2,1,0:T(4,128)(2,1)S(1)}, u32[]{:S(2)}, u32[]{:S(2)}) collective-permute-start(bf16[2,6,1,2,4,1536]{5,4,3,2,1,0:T(4,128)(2,1)S(1)} %get-tuple-element.587), channel_id=1, source_target_pairs={{0,2},{2,4},{4,6},{1,3},{3,5},{5,7},{8,10},{10,12},{12,14},{9,11},... | collective-permute-start | bytes 884744 | tf_op jit(solution)/shard_map/ppermute | solution.py:18
  22.4 21.8 %copy-start.14 = (bf16[2,1,4,2,4,1536]{5,4,3,2,1,0:T(4,128)(2,1)}, bf16[2,1,4,2,4,1536]{5,4,3,2,1,0:T(4,128)(2,1)S(1)}, u32[]{:S(2)}) copy-start(bf16[2,1,4,2,4,1536]{5,4,3,2,1,0:T(4,128)(2,1)S(1)} %collective-permute-done.7) | copy-start | bytes 589828
  22.4 21.7 %copy-start.15 = (bf16[2,1,4,2,4,1536]{5,4,3,2,1,0:T(4,128)(2,1)}, bf16[2,1,4,2,4,1536]{5,4,3,2,1,0:T(4,128)(2,1)S(1)}, u32[]{:S(2)}) copy-start(bf16[2,1,4,2,4,1536]{5,4,3,2,1,0:T(4,128)(2,1)S(1)} %collective-permute-done.6) | copy-start | bytes 589828
  23.0 19.1 %collective-permute-start.9 = (bf16[2,6,1,2,4,1536]{5,4,3,2,1,0:T(4,128)(2,1)S(1)}, bf16[2,6,1,2,4,1536]{5,4,3,2,1,0:T(4,128)(2,1)S(1)}, u32[]{:S(2)}, u32[]{:S(2)}) collective-permute-start(bf16[2,6,1,2,4,1536]{5,4,3,2,1,0:T(4,128)(2,1)S(1)} %get-tuple-element.586), channel_id=1, source_target_pairs={{2,0},{4,2},{6,4},{3,1},{5,3},{7,5},{10,8},{12,10},{14,12},{11,9},... | collective-permute-start | bytes 884744 | tf_op jit(solution)/shard_map/ppermute | solution.py:19
  27.0 17.2 %collective-permute-start.8 = (bf16[2,6,1,2,4,1536]{5,4,3,2,1,0:T(4,128)(2,1)S(1)}, bf16[2,6,1,2,4,1536]{5,4,3,2,1,0:T(4,128)(2,1)S(1)}, u32[]{:S(2)}, u32[]{:S(2)}) collective-permute-start(bf16[2,6,1,2,4,1536]{5,4,3,2,1,0:T(4,128)(2,1)S(1)} %get-tuple-element.585), channel_id=1, source_target_pairs={{0,2},{2,4},{4,6},{1,3},{3,5},{5,7},{8,10},{10,12},{12,14},{9,11},... | collective-permute-start | bytes 884744 | tf_op jit(solution)/shard_map/ppermute | solution.py:18
  28.9 4.4 copy-start.22
  33.9 21.4 %collective-permute-start.5 = (bf16[2,6,6,1,4,1536]{5,4,3,2,1,0:T(4,128)(2,1)S(1)}, bf16[2,6,6,1,4,1536]{5,4,3,2,1,0:T(4,128)(2,1)S(1)}, u32[]{:S(2)}, u32[]{:S(2)}) collective-permute-start(bf16[2,6,6,1,4,1536]{5,4,3,2,1,0:T(4,128)(2,1)S(1)} %get-tuple-element.584), channel_id=1, source_target_pairs={{1,0},{3,2},{5,4},{7,6},{9,8},{11,10},{13,12},{15,14},{17,16},{19,... | collective-permute-start | bytes 2654216 | tf_op jit(solution)/shard_map/ppermute | solution.py:19
  40.8 14.5 %collective-permute-start.4 = (bf16[2,6,6,1,4,1536]{5,4,3,2,1,0:T(4,128)(2,1)S(1)}, bf16[2,6,6,1,4,1536]{5,4,3,2,1,0:T(4,128)(2,1)S(1)}, u32[]{:S(2)}, u32[]{:S(2)}) collective-permute-start(bf16[2,6,6,1,4,1536]{5,4,3,2,1,0:T(4,128)(2,1)S(1)} %get-tuple-element.583), channel_id=1, source_target_pairs={{0,1},{2,3},{4,5},{6,7},{8,9},{10,11},{12,13},{14,15},{16,17},{18,... | collective-permute-start | bytes 2654216 | tf_op jit(solution)/shard_map/ppermute | solution.py:18
  46.6 8.7 %copy-start.8 = (bf16[4,4,2,4,1536]{4,3,2,1,0:T(4,128)(2,1)S(1)}, bf16[4,4,2,4,1536]{4,3,2,1,0:T(4,128)(2,1)}, u32[]{:S(2)}) copy-start(bf16[4,4,2,4,1536]{4,3,2,1,0:T(4,128)(2,1)} %param.12) | copy-start | bytes 1179652
  46.6 8.7 %copy-start.10 = (bf16[4,4,2,4,1536]{4,3,2,1,0:T(4,128)(2,1)S(1)}, bf16[4,4,2,4,1536]{4,3,2,1,0:T(4,128)(2,1)}, u32[]{:S(2)}) copy-start(bf16[4,4,2,4,1536]{4,3,2,1,0:T(4,128)(2,1)} %param.11) | copy-start | bytes 1179652
  46.6 8.7 %copy-start.17 = (bf16[2,1,4,2,4,1536]{5,4,3,2,1,0:T(4,128)(2,1)S(1)}, bf16[2,1,4,2,4,1536]{5,4,3,2,1,0:T(4,128)(2,1)}, u32[]{:S(2)}) copy-start(bf16[2,1,4,2,4,1536]{5,4,3,2,1,0:T(4,128)(2,1)} %copy-done.16) | copy-start | bytes 589828
  46.6 8.7 %copy-start.19 = (bf16[2,1,4,2,4,1536]{5,4,3,2,1,0:T(4,128)(2,1)S(1)}, bf16[2,1,4,2,4,1536]{5,4,3,2,1,0:T(4,128)(2,1)}, u32[]{:S(2)}) copy-start(bf16[2,1,4,2,4,1536]{5,4,3,2,1,0:T(4,128)(2,1)} %copy-done.18) | copy-start | bytes 589828
  46.6 8.7 %copy-start.23 = (bf16[2,6,1,2,4,1536]{5,4,3,2,1,0:T(4,128)(2,1)S(1)}, bf16[2,6,1,2,4,1536]{5,4,3,2,1,0:T(4,128)(2,1)}, u32[]{:S(2)}) copy-start(bf16[2,6,1,2,4,1536]{5,4,3,2,1,0:T(4,128)(2,1)} %copy-done.22) | copy-start | bytes 884740
  46.6 8.7 %copy-start.25 = (bf16[2,6,1,2,4,1536]{5,4,3,2,1,0:T(4,128)(2,1)S(1)}, bf16[2,6,1,2,4,1536]{5,4,3,2,1,0:T(4,128)(2,1)}, u32[]{:S(2)}) copy-start(bf16[2,6,1,2,4,1536]{5,4,3,2,1,0:T(4,128)(2,1)} %copy-done.24) | copy-start | bytes 884740
  48.5 397.6 %collective-permute-start.11 = (bf16[2,6,6,1,4,1536]{5,4,3,2,1,0:T(4,128)(2,1)}, bf16[2,6,6,1,4,1536]{5,4,3,2,1,0:T(4,128)(2,1)}, u32[]{:S(2)}, u32[]{:S(2)}) collective-permute-start(bf16[2,6,6,1,4,1536]{5,4,3,2,1,0:T(4,128)(2,1)} %get-tuple-element.582), channel_id=1, source_target_pairs={{1,0},{3,2},{5,4},{7,6},{9,8},{11,10},{13,12},{15,14},{17,16},{19,... | collective-permute-start | bytes 2654216 | tf_op jit(solution)/shard_map/ppermute | solution.py:19
  54.0 392.2 %collective-permute-start.10 = (bf16[2,6,6,1,4,1536]{5,4,3,2,1,0:T(4,128)(2,1)}, bf16[2,6,6,1,4,1536]{5,4,3,2,1,0:T(4,128)(2,1)}, u32[]{:S(2)}, u32[]{:S(2)}) collective-permute-start(bf16[2,6,6,1,4,1536]{5,4,3,2,1,0:T(4,128)(2,1)} %get-tuple-element.581), channel_id=1, source_target_pairs={{0,1},{2,3},{4,5},{6,7},{8,9},{10,11},{12,13},{14,15},{16,17},{18,... | collective-permute-start | bytes 2654216 | tf_op jit(solution)/shard_map/ppermute | solution.py:18
  72.5 2.7 copy-start
  109.2 8.9 %copy-start.34 = (f32[4,32]{1,0:T(4,128)}, f32[4,32]{1,0:T(4,128)S(1)}, u32[]{:S(2)}) copy-start(f32[4,32]{1,0:T(4,128)S(1)} %log_add_fusion.6) | copy-start | bytes 1540 | tf_op jit(solution)/shard_map/while
  125.2 3.9 copy-start.35
  136.2 8.5 %copy-start.36 = (f32[4,32]{1,0:T(4,128)}, f32[4,32]{1,0:T(4,128)S(1)}, u32[]{:S(2)}) copy-start(f32[4,32]{1,0:T(4,128)S(1)} %log_add_fusion.8) | copy-start | bytes 1540 | tf_op jit(solution)/shard_map/while
  162.8 2.7 copy-start
  199.6 8.9 %copy-start.34 = (f32[4,32]{1,0:T(4,128)}, f32[4,32]{1,0:T(4,128)S(1)}, u32[]{:S(2)}) copy-start(f32[4,32]{1,0:T(4,128)S(1)} %log_add_fusion.6) | copy-start | bytes 1540 | tf_op jit(solution)/shard_map/while
  215.5 3.9 copy-start.35
  226.6 8.5 %copy-start.36 = (f32[4,32]{1,0:T(4,128)}, f32[4,32]{1,0:T(4,128)S(1)}, u32[]{:S(2)}) copy-start(f32[4,32]{1,0:T(4,128)S(1)} %log_add_fusion.8) | copy-start | bytes 1540 | tf_op jit(solution)/shard_map/while
  253.1 2.7 copy-start
  289.9 8.9 %copy-start.34 = (f32[4,32]{1,0:T(4,128)}, f32[4,32]{1,0:T(4,128)S(1)}, u32[]{:S(2)}) copy-start(f32[4,32]{1,0:T(4,128)S(1)} %log_add_fusion.6) | copy-start | bytes 1540 | tf_op jit(solution)/shard_map/while
  305.9 3.9 copy-start.35
  316.9 8.5 %copy-start.36 = (f32[4,32]{1,0:T(4,128)}, f32[4,32]{1,0:T(4,128)S(1)}, u32[]{:S(2)}) copy-start(f32[4,32]{1,0:T(4,128)S(1)} %log_add_fusion.8) | copy-start | bytes 1540 | tf_op jit(solution)/shard_map/while
  343.5 2.7 copy-start
  380.2 8.9 %copy-start.34 = (f32[4,32]{1,0:T(4,128)}, f32[4,32]{1,0:T(4,128)S(1)}, u32[]{:S(2)}) copy-start(f32[4,32]{1,0:T(4,128)S(1)} %log_add_fusion.6) | copy-start | bytes 1540 | tf_op jit(solution)/shard_map/while
  396.2 3.9 copy-start.35
  407.2 8.5 %copy-start.36 = (f32[4,32]{1,0:T(4,128)}, f32[4,32]{1,0:T(4,128)S(1)}, u32[]{:S(2)}) copy-start(f32[4,32]{1,0:T(4,128)S(1)} %log_add_fusion.8) | copy-start | bytes 1540 | tf_op jit(solution)/shard_map/while
  421.9 5.3 collective-permute-start.13
  424.0 4.7 collective-permute-start.12
  427.2 18.9 %copy-start.30 = (f32[2,1,4,2,4,12]{5,4,3,2,1,0:T(4,128)}, f32[2,1,4,2,4,12]{5,4,3,2,1,0:T(4,128)S(1)}, u32[]{:S(2)}) copy-start(f32[2,1,4,2,4,12]{5,4,3,2,1,0:T(4,128)S(1)} %collective-permute-done.13) | copy-start | bytes 9220
  428.6 17.5 %copy-start.32 = (f32[2,1,4,2,4,12]{5,4,3,2,1,0:T(4,128)}, f32[2,1,4,2,4,12]{5,4,3,2,1,0:T(4,128)S(1)}, u32[]{:S(2)}) copy-start(f32[2,1,4,2,4,12]{5,4,3,2,1,0:T(4,128)S(1)} %collective-permute-done.12) | copy-start | bytes 9220
  429.5 6.9 collective-permute-start.15
  431.4 5.7 collective-permute-start.14
  436.4 9.8 %copy-start.37 = (f32[2,6,1,2,4,12]{5,4,3,2,1,0:T(4,128)}, f32[2,6,1,2,4,12]{5,4,3,2,1,0:T(4,128)S(1)}, u32[]{:S(2)}) copy-start(f32[2,6,1,2,4,12]{5,4,3,2,1,0:T(4,128)S(1)} %collective-permute-done.15) | copy-start | bytes 13828
  437.1 9.1 %copy-start.39 = (f32[2,6,1,2,4,12]{5,4,3,2,1,0:T(4,128)}, f32[2,6,1,2,4,12]{5,4,3,2,1,0:T(4,128)S(1)}, u32[]{:S(2)}) copy-start(f32[2,6,1,2,4,12]{5,4,3,2,1,0:T(4,128)S(1)} %collective-permute-done.14) | copy-start | bytes 13828
  438.1 13.6 %collective-permute-start.17 = (f32[2,6,6,1,4,12]{5,4,3,2,1,0:T(4,128)S(1)}, f32[2,6,6,1,4,12]{5,4,3,2,1,0:T(4,128)S(1)}, u32[]{:S(2)}, u32[]{:S(2)}) collective-permute-start(f32[2,6,6,1,4,12]{5,4,3,2,1,0:T(4,128)S(1)} %get-tuple-element.594), channel_id=1, source_target_pairs={{1,0},{3,2},{5,4},{7,6},{9,8},{11,10},{13,12},{15,14},{17,16},{19,... | collective-permute-start | bytes 41480 | tf_op jit(solution)/shard_map/ppermute | solution.py:19
  444.7 7.1 copy-start.26
  444.7 7.1 copy-start.27
  444.7 7.1 collective-permute-start.16
  446.2 5.6 copy-start.31
  446.2 5.6 copy-start.33
  446.2 5.6 copy-start.38
  446.2 5.6 copy-start.40
  496.4 2.6 copy-start.1
  595.1 2.6 copy-start.1
  693.8 2.6 copy-start.1
  (52 other events, 39.5 us)
where the time goes:
time: 862 us; the launch traced here: 850 us
  local copies, waits for them, and re-layouts  529 us (61%)
  matrix products  115 us (13%)
  other arithmetic  105 us (12%)
  starting transfers between devices  55.5 us (6%)
  loops' own time  36.8 us (4%)
    broadcast_in_dim x72, local copies, waits for them, and re-layouts, expand_mask(): shaped = jnp.where(allowed[:, :, None, :, None], shaped, NEG_FILL)  135 us
    ppermute x9, starting transfers between devices, with_halo(): after = lax.ppermute(first, axis, down)  34.1 us
    dot_general x12, matrix products, key_side(): jnp.einsum('hqk,qhd->khd', score_grads, outer_queries, preferred_element_...  25.5 us
    dot_general x12, matrix products, query_side(): jnp.einsum('hqk,khd->qhd', score_grads, outer_keys, preferred_element_typ...  25.4 us
    while x136, local copies, waits for them, and re-layouts  25 us
    ppermute x9, starting transfers between devices, with_halo(): before = lax.ppermute(last, axis, up)  21.4 us
    another operation x1, loops' own time, per_device(): query_gradient, logsum_all, drift_all = lax.map(query_step, slab_ids)  20.1 us
    dot_general x12, matrix products, key_side(): jnp.einsum('hqk,qhd->khd', weights_low, outer_cotangent, preferred_elemen...  18.5 us
  transfers between devices with their start and end apart: 18, of which 4 were waited for; matrix products, arithmetic and copies ran while one was open for 42% of the time, Pallas kernels for 0%

commit v1 on v0

v1 whole, which is shorter than its diff:
```python
import functools
import math

import jax
import jax.numpy as jnp
import numpy as np
from jax import lax
from jax.experimental import pallas as pl
from jax.experimental.pallas import tpu as pltpu
from jax.sharding import PartitionSpec as P

NEG = -1e30
LOG2E = 1.4426950408889634
EVEN, ODD = 1000, 1001
AXES = ("ta", "ha", "wa")


def matchings(n):
    even = [(i, i ^ 1) for i in range(n) if (i ^ 1) < n]
    odd = [(i, ((i + 1) ^ 1) - 1) for i in range(n) if 0 <= ((i + 1) ^ 1) - 1 < n]
    return [m for m in (even, odd) if m]


def exchange(axis, first, last):
    n = lax.axis_size(axis)
    is_odd = lax.rem(lax.axis_index(axis), 2) == 1
    pieces = []
    for k, pairs in enumerate(matchings(n)):
        flip = is_odd if k == 0 else jnp.logical_not(is_odd)
        pieces.append(lax.ppermute(jnp.where(flip, first, last), axis, pairs))
    return pieces


def halo(own, block):
    T, H, W, C = block
    k, _, width = own.shape
    grid = own.reshape(k, W, T, H, C, width)
    ha = exchange(
        "ha",
        grid[:, :, :, 0].reshape(k, W * T * C, width),
        grid[:, :, :, H - 1].reshape(k, W * T * C, width),
    )
    own_t = own.reshape(k, W, T, H * C, width)
    ha_t = [p.reshape(k, W, T, C, width) for p in ha]

    def time_layer(t):
        return jnp.concatenate([own_t[:, :, t]] + [p[:, :, t] for p in ha_t], axis=2).reshape(
            k, -1, width
        )

    ta = exchange("ta", time_layer(0), time_layer(T - 1))

    def column(w):
        return jnp.concatenate(
            [p.reshape(k, W, -1, width)[:, w] for p in [own] + ha + ta], axis=1
        )

    wa = exchange("wa", column(0), column(W - 1))
    return ha + ta + wa


def piece_coords(block, counts):
    T, H, W, C = block
    marks = (EVEN, ODD)

    def rows(cells):
        return [np.repeat(np.array(cells, np.int32), C, axis=0)]

    own = [[[(t, h, w) for h in range(H)] for t in range(T)] for w in range(W)]
    pieces = [np.array(own, np.int32).reshape(W, -1, 3)]
    for m in marks[: counts[1]]:
        pieces.append(np.array([[(t, m, w) for t in range(T)] for w in range(W)], np.int32))
    hs = list(range(H)) + list(marks[: counts[1]])
    for m in marks[: counts[0]]:
        pieces.append(np.array([[(m, h, w) for h in hs] for w in range(W)], np.int32))
    column = np.concatenate([p[0] for p in pieces], axis=0)
    out = [p.reshape(-1, 3) for p in pieces]
    for m in marks[: counts[2]]:
        c = column.copy()
        c[:, 2] = m
        out.append(c)
    return np.repeat(np.concatenate(out, axis=0), C, axis=0)


def build_code(oc_ref, kc_ref, bounds_ref, code_ref, block, grids, own_is_query):
    bad = None
    same = None
    valid = None
    code = None
    for a, axis in enumerate(AXES):
        index = lax.axis_index(axis)
        length = block[a]
        odd = lax.rem(index, 2)
        at_even = jnp.where(odd == 1, -1, length)
        at_odd = jnp.where(odd == 1, length, -1)
        own = oc_ref[:, a : a + 1]
        outer = kc_ref[a : a + 1, :]
        outer = jnp.where(outer == EVEN, at_even, jnp.where(outer == ODD, at_odd, outer))
        place = outer + index * length
        inside = (place >= 0) & (place < grids[a])
        low, high = bounds_ref[2 * a], bounds_ref[2 * a + 1]
        checked = own + index * length if not own_is_query else place
        ok = (checked >= low) & (checked <= high)
        apart = jnp.abs(own - outer)
        here_bad = jnp.where((apart > 1) | jnp.logical_not(inside), 8, 0)
        here_code = jnp.where(apart == 1, 1 << a, 0)
        code = here_code if code is None else code | here_code
        bad = here_bad if bad is None else bad | here_bad
        valid = jnp.where(ok, 0, 8) if valid is None else valid | jnp.where(ok, 0, 8)
        same = apart if same is None else same | apart
    blocked = jnp.where(same == 0, 0, jnp.broadcast_to(valid, same.shape))
    code_ref[...] = code | bad | blocked


def forbidden(radius_ref, h):
    bits = 8
    for a in range(3):
        bits = bits + (1 - radius_ref[h, a]) * (1 << a)
    return bits


NT = (((1,), (1,)), ((), ()))
NN = (((1,), (0,)), ((), ()))


def dot(a, b, dims):
    return lax.dot_general(a, b, dims, preferred_element_type=jnp.float32)


def gather(refs, which, cols, pad):
    parts = [r[which, :, cols] for r in refs]
    if pad:
        parts.append(jnp.zeros((pad, parts[0].shape[1]), parts[0].dtype))
    return jnp.concatenate(parts, axis=0)


def query_kernel(cfg, radius_ref, bounds_ref, oc_ref, kc_ref, qd_ref, *rest):
    block, grids, heads, depth, pad, count = cfg
    kv = rest[:count]
    dq_ref, stat_ref, code_ref = rest[count:]
    build_code(oc_ref, kc_ref, bounds_ref, code_ref, block, grids, True)
    scale = 1.0 / math.sqrt(depth)
    rows = qd_ref.shape[1]
    lane = lax.broadcasted_iota(jnp.int32, (rows, stat_ref.shape[1]), 1)
    stats = jnp.zeros((rows, stat_ref.shape[1]), jnp.float32)
    for h in range(heads):
        cols = slice(h * depth, (h + 1) * depth)
        keys = gather(kv, 0, cols, pad)
        values = gather(kv, 1, cols, pad)
        allowed = (code_ref[...] & forbidden(radius_ref, h)) == 0
        scores = dot(qd_ref[0, :, cols], keys, NT) * (scale * LOG2E)
        scores = jnp.where(allowed, scores, NEG)
        peak = jnp.max(scores, axis=1, keepdims=True)
        raised = jnp.exp2(scores - peak)
        logsum = peak + jnp.log2(jnp.sum(raised, axis=1, keepdims=True))
        attention = jnp.exp2(scores - logsum)
        grads = dot(qd_ref[1, :, cols], values, NT)
        low = attention.astype(jnp.bfloat16).astype(jnp.float32)
        drift = jnp.sum(low * grads, axis=1, keepdims=True)
        score_grads = (attention * (grads - drift)).astype(jnp.bfloat16)
        dq_ref[:, cols] = (dot(score_grads, keys, NN) * scale).astype(jnp.bfloat16)
        stats = jnp.where(lane == h, logsum, stats)
        stats = jnp.where(lane == heads + h, drift, stats)
    stat_ref[...] = stats


def key_kernel(cfg, radius_ref, bounds_ref, oc_ref, kc_ref, kv_ref, *rest):
    block, grids, heads, depth, pad, count = cfg
    qd = rest[:count]
    st = rest[count : 2 * count]
    dk_ref, dv_ref, code_ref, row_ref = rest[2 * count :]
    build_code(oc_ref, kc_ref, bounds_ref, code_ref, block, grids, False)
    scale = 1.0 / math.sqrt(depth)
    parts = [r[0] for r in st]
    if pad:
        parts.append(jnp.zeros((pad, parts[0].shape[1]), jnp.float32))
    row_ref[...] = jnp.concatenate(parts, axis=0).T
    for h in range(heads):
        cols = slice(h * depth, (h + 1) * depth)
        queries = gather(qd, 0, cols, pad)
        cotangent = gather(qd, 1, cols, pad)
        allowed = (code_ref[...] & forbidden(radius_ref, h)) == 0
        scores = dot(kv_ref[0, :, cols], queries, NT) * (scale * LOG2E)
        scores = jnp.where(allowed, scores, NEG)
        attention = jnp.exp2(scores - row_ref[h : h + 1, :])
        grads = dot(kv_ref[1, :, cols], cotangent, NT)
        score_grads = (attention * (grads - row_ref[heads + h : heads + h + 1, :])).astype(
            jnp.bfloat16
        )
        dk_ref[:, cols] = (dot(score_grads, queries, NN) * scale).astype(jnp.bfloat16)
        dv_ref[:, cols] = dot(attention.astype(jnp.bfloat16), cotangent, NN).astype(jnp.bfloat16)


def per_device(queries, key_states, value_states, output_cotangent, tile_valid, window_radius):
    T, H, W, C, width = queries.shape
    block = (T, H, W, C)
    heads = window_radius.shape[0]
    depth = width // heads
    sizes = tuple(lax.axis_size(a) for a in AXES)
    grids = tuple(n * b for n, b in zip(sizes, block))
    counts = tuple(len(matchings(n)) for n in sizes)
    rows = T * H * W * C

    def rowwise(x):
        return x.transpose(2, 0, 1, 3, 4).reshape(rows, width)

    def tilewise(x):
        return x.reshape(W, T, H, C, width).transpose(1, 2, 0, 3, 4)

    kv = jnp.stack([rowwise(key_states), rowwise(value_states)])
    qd = jnp.stack([rowwise(queries), rowwise(output_cotangent)])
    kv_pieces = [kv] + halo(kv, block)
    qd_pieces = [qd] + halo(qd, block)

    lines = (tile_valid[:, 1, 1], tile_valid[1, :, 1], tile_valid[1, 1, :])
    bounds = jnp.stack(
        [b for v in lines for b in (1 - v[0], v.shape[0] - 3 + v[-1] + v[-2])]
    ).astype(jnp.int32)

    coords = piece_coords(block, counts)
    total = coords.shape[0]
    padded = -(-total // 128) * 128
    pad = padded - total
    outer = np.full((8, padded), -(1 << 20), np.int32)
    outer[:3, :total] = coords.T
    inner = np.zeros((rows, 8), np.int32)
    inner[:, :3] = coords[:rows]
    cfg = (block, grids, heads, depth, pad, len(kv_pieces))
    smem = pl.BlockSpec(memory_space=pltpu.SMEM)
    vmem = pl.BlockSpec(memory_space=pltpu.VMEM)
    lanes = -(-2 * heads // 128) * 128
    params = pltpu.CompilerParams(vmem_limit_bytes=48 << 20)

    query_gradient, stats = pl.pallas_call(
        functools.partial(query_kernel, cfg),
        out_shape=(
            jax.ShapeDtypeStruct((rows, width), jnp.bfloat16),
            jax.ShapeDtypeStruct((rows, lanes), jnp.float32),
        ),
        in_specs=[smem] * 2 + [vmem] * (3 + len(kv_pieces)),
        out_specs=(vmem, vmem),
        scratch_shapes=[pltpu.VMEM((rows, padded), jnp.int32)],
        compiler_params=params,
        name="query_side",
    )(window_radius, bounds, inner, outer, qd, *kv_pieces)

    stats = stats[None]
    stat_pieces = [stats] + halo(stats, block)

    key_gradient, value_gradient = pl.pallas_call(
        functools.partial(key_kernel, cfg),
        out_shape=(jax.ShapeDtypeStruct((rows, width), jnp.bfloat16),) * 2,
        in_specs=[smem] * 2 + [vmem] * (3 + 2 * len(kv_pieces)),
        out_specs=(vmem, vmem),
        scratch_shapes=[
            pltpu.VMEM((rows, padded), jnp.int32),
            pltpu.VMEM((lanes, padded), jnp.float32),
        ],
        compiler_params=params,
        name="key_side",
    )(window_radius, bounds, inner, outer, kv, *qd_pieces, *stat_pieces)

    return (tilewise(query_gradient), tilewise(key_gradient), tilewise(value_gradient))


def solution(mesh):
    split = P("ta", "ha", "wa", None, None)
    return jax.shard_map(
        per_device,
        mesh=mesh,
        in_specs=(split, split, split, split, P(), P()),
        out_specs=(split, split, split),
        check_vma=False,
    )
```

time: 862 us -> 89.7 us (0.10); the launches traced: 850 us -> 88.8 us
  local copies, waits for them, and re-layouts: 529 us -> 33.1 us
  matrix products: 115 us -> 0 us
  other arithmetic: 105 us -> 6.94 us
  loops' own time: 36.8 us -> 0 us
  starting transfers between devices: 55.5 us -> 24 us
  Pallas kernels: 0 us -> 11.3 us
    broadcast_in_dim x72 -> x0, local copies, waits for them, and re-layouts: 135 us -> none  [expand_mask(): shaped = jnp.where(allowed[:, :, None, :, None], shaped, NEG_FILL)]
    slice x63 -> x1, local copies, waits for them, and re-layouts: 120 us -> 1.59 us  [per_device(): v[-2]]
    dot_general x72 -> x0, matrix products: 115 us -> none  [the longest x12 25.5 us: key_side(): jnp.einsum('hqk,qhd->khd', score_grads, outer_queries, preferred_element_...]
    dynamic_slice x52 -> x0, local copies, waits for them, and re-layouts: 76.2 us -> none  [the longest x4 10 us: query_inputs(): lax.dynamic_slice_in_dim(rim_pair[1], slab, 3, 0)]
    reshape x32 -> x10, local copies, waits for them, and re-layouts: 69.6 us -> 4.16 us  [the longest x6 3.95 us: tilewise(): return x.reshape(W, T, H, C, width).transpose(1, 2, 0, 3, 4)]
    another operation x2 -> x0, loops' own time: 36.8 us -> none  [the longest x1 20.1 us: per_device(): query_gradient, logsum_all, drift_all = lax.map(query_step, slab_ids)]
    and x88 -> x0, other arithmetic: 33.6 us -> none  [the longest x24 16.6 us: axis_window(): above_start & below_end & inside[None, :, None] & key_inside[None, None, :]]
    ppermute x18 -> x15, starting transfers between devices: 55.5 us -> 24 us  [exchange(): pieces.append(lax.ppermute(jnp.where(flip, first, last), axis, pairs))]
  transfers between devices with their start and end apart: 18 -> 15, of which waited for: 4 -> 5; matrix products, arithmetic and copies ran while one was open for 42% -> 32% of each run, Pallas kernels for 0% -> 8%
where the time goes in v1:
time: 89.7 us; the launch traced here: 88.8 us
  local copies, waits for them, and re-layouts  33.1 us (37%)
  starting transfers between devices  24 us (27%)
  Pallas kernels  11.3 us (13%)
  other arithmetic  6.94 us (8%)
  between operations  6.85 us (8%)
  waiting for transfers between devices  6.68 us (7%)
    ppermute x15, starting transfers between devices, exchange(): pieces.append(lax.ppermute(jnp.where(flip, first, last), axis, pairs))  24 us
    unnamed x73, local copies, waits for them, and re-layouts  13 us
    pallas_call x1, Pallas kernels, per_device(): pl.pallas_call(functools.partial(query_kernel, cfg), out_shape=(jax.Shape...  6.86 us
    ppermute x15, waiting for transfers between devices, exchange(): pieces.append(lax.ppermute(jnp.where(flip, first, last), axis, pairs))  6.68 us
    select_n x11, other arithmetic, exchange(): pieces.append(lax.ppermute(jnp.where(flip, first, last), axis, pairs))  6.28 us
    pallas_call x1, Pallas kernels, per_device(): pl.pallas_call(functools.partial(key_kernel, cfg), out_shape=(jax.ShapeDt...  4.46 us
    transpose x8, local copies, waits for them, and re-layouts, rowwise(): return x.transpose(2, 0, 1, 3, 4).reshape(rows, width)  4.05 us
    reshape x6, local copies, waits for them, and re-layouts, tilewise(): return x.reshape(W, T, H, C, width).transpose(1, 2, 0, 3, 4)  3.95 us
  transfers between devices with their start and end apart: 15, of which 5 were waited for; matrix products, arithmetic and copies ran while one was open for 32% of the time, Pallas kernels for 8%

profile of v1, /device:TPU:21, one launch (start us, length us, event | category | flops | bytes accessed | tf_op | source)
XLA Modules:
  0.0 88.8 jit_solution(8919991672357686699)
XLA Ops:
  0.6 1.4 %broadcast_select_fusion.7 = (bf16[2,2,4,1,4,1536]{5,4,1,3,2,0:T(4,128)(2,1)S(1)}, bf16[2,2,4,1,4,1536]{5,4,1,3,2,0:T(4,128)(2,1)S(1)}, bf16[2,2,4,1,4,1536]{5,4,1,3,2,0:T(4,128)(2,1)S(1)}) fusion(pred[]{:T(512)S(6)} %not.4, bf16[1,2,4,4,4,1536]{5,4,1,3,2,0:T(4,128)(2,1)} %bitcast.320, bf16[1,2,4,4,4,1536]{5,4,1,3,2,0:T(4,128)(2,1)} %bitcast.317), kind=kLoop, calls=%fused_computation.36 | loop fusion | flops 294912 | bytes 1376257 | tf_op jit(solution)/shard_map/jit(_where)/select_n | solution.py:30
  2.1 0.7 select_n.170
  2.9 1.2 %collective-permute-start = (bf16[2,32,1536]{2,1,0:T(8,128)(2,1)}, bf16[2,32,1536]{2,1,0:T(8,128)(2,1)S(1)}, u32[]{:S(2)}, u32[]{:S(2)}) collective-permute-start(bf16[2,32,1536]{2,1,0:T(8,128)(2,1)} %select_n.170), channel_id=1, source_target_pairs={{0,2},{2,0},{4,6},{6,4},{1,3},{3,1},{5,7},{7,5},{8,10},{10,8},{12,... | collective-permute-start | bytes 589832 | tf_op jit(solution)/shard_map/ppermute | solution.py:30
  4.1 0.7 select_n.173
  4.9 2.1 %collective-permute-start.1 = (bf16[2,32,1536]{2,1,0:T(8,128)(2,1)}, bf16[2,32,1536]{2,1,0:T(8,128)(2,1)S(1)}, u32[]{:S(2)}, u32[]{:S(2)}) collective-permute-start(bf16[2,32,1536]{2,1,0:T(8,128)(2,1)} %select_n.173), channel_id=1, source_target_pairs={{2,4},{4,2},{3,5},{5,3},{10,12},{12,10},{11,13},{13,11},{18,20},{2... | collective-permute-start | bytes 589832 | tf_op jit(solution)/shard_map/ppermute | solution.py:30
  7.0 0.3 broadcast_select_fusion.6
  7.5 0.7 select_n.183
  8.3 0.7 select_n.185
  9.0 4.1 %collective-permute-start.6 = (bf16[2,32,1536]{2,1,0:T(8,128)(2,1)}, bf16[2,32,1536]{2,1,0:T(8,128)(2,1)S(1)}, u32[]{:S(2)}, u32[]{:S(2)}) collective-permute-start(bf16[2,32,1536]{2,1,0:T(8,128)(2,1)} %select_n.185), channel_id=1, source_target_pairs={{2,4},{4,2},{3,5},{5,3},{10,12},{12,10},{11,13},{13,11},{18,20},{2... | collective-permute-start | bytes 589832 | tf_op jit(solution)/shard_map/ppermute | solution.py:30
  13.1 1.1 %copy.161 = bf16[2,4,4,4,1536]{4,1,3,2,0:T(4,128)(2,1)} copy(bf16[2,4,4,4,1536]{4,3,0,2,1:T(4,128)(2,1)S(1)} %bitcast.318) | data formatting | bytes 786432 | tf_op jit(solution)/shard_map/transpose | solution.py:205
  14.3 0.9 copy-done.10
  15.1 1.1 %copy.162 = bf16[2,4,4,4,1536]{4,1,3,2,0:T(4,128)(2,1)} copy(bf16[2,4,4,4,1536]{4,3,0,2,1:T(4,128)(2,1)S(1)} %bitcast.321) | data formatting | bytes 786432 | tf_op jit(solution)/shard_map/transpose | solution.py:205
  16.4 0.9 stack.78
  17.3 0.8 stack.79
  18.2 0.8 stack_reshape.15
  19.1 0.3 copy.181
  19.5 0.1 copy.156
  19.6 1.1 %copy.182 = bf16[2,4,4,4,1536]{4,1,3,2,0:T(4,128)(2,1)} copy(bf16[2,4,4,4,1536]{4,3,0,2,1:T(4,128)(2,1)S(1)} %bitcast.328) | data formatting | bytes 786432 | tf_op jit(solution)/shard_map/transpose | solution.py:205
  20.9 0.8 stack_reshape.13
  21.7 0.9 stack.88
  22.6 0.2 copy-done.18
  22.7 1.0 %copy-done.19 = bf16[1,2,64,1536]{3,2,0,1:T(8,128)(2,1)S(1)} copy-done((bf16[1,2,64,1536]{3,2,0,1:T(8,128)(2,1)S(1)}, bf16[1,2,64,1536]{3,2,0,1:T(8,128)(2,1)}, u32[]{:S(2)}) %copy-start.19) | copy-done | bytes 393240
  23.7 1.0 %fusion.3 = (bf16[2,144,1536]{2,1,0:T(8,128)(2,1)}, bf16[2,144,1536]{2,1,0:T(8,128)(2,1)}) fusion(bf16[2,2,64,1536]{3,2,0,1:T(8,128)(2,1)S(1)} %constant_dynamic-update-slice_fusion.4), kind=kLoop, calls=%fused_computation.10 | loop fusion | bytes 1572864
  24.7 1.6 %fusion.25 = (s32[1,1,1]{1,2,0:T(1,128)}, s32[1,1,1]{1,2,0:T(1,128)}, s32[1,1,1]{1,2,0:T(1,128)}, s32[1,1,1]{1,2,0:T(1,128)}, s32[1,1,1]{1,2,0:T(1,128)}, /*inde...) fusion(s32[16,16,4]{1,2,0:T(4,128)} %param.12), kind=kLoop, calls=%fused_computation.122 | loop fusion | bytes 72 | tf_op jit(solution)/shard_map/slice | solution.py:217
  30.0 0.6 copy-done.26
  30.8 0.9 %copy-done.17 = bf16[2,4,4,4,1536]{4,1,3,2,0:T(4,128)(2,1)S(1)} copy-done((bf16[2,4,4,4,1536]{4,1,3,2,0:T(4,128)(2,1)S(1)}, bf16[2,4,4,4,1536]{4,1,3,2,0:T(4,128)(2,1)}, u32[]{:S(2)}) %copy-start.17) | copy-done | bytes 393240
  31.8 0.8 slice_bitcast_fusion.5
  32.6 1.0 %copy-done.16 = bf16[1,2,64,1536]{3,2,0,1:T(8,128)(2,1)S(1)} copy-done((bf16[1,2,64,1536]{3,2,0,1:T(8,128)(2,1)S(1)}, bf16[1,2,64,1536]{3,2,0,1:T(8,128)(2,1)}, u32[]{:S(2)}) %copy-start.16) | copy-done | bytes 393240
  33.6 0.9 %fusion.1 = (bf16[2,144,1536]{2,1,0:T(8,128)(2,1)}, bf16[2,144,1536]{2,1,0:T(8,128)(2,1)}) fusion(bf16[2,2,64,1536]{3,2,0,1:T(8,128)(2,1)S(1)} %constant_dynamic-update-slice_fusion.6), kind=kLoop, calls=%fused_computation.6 | loop fusion | bytes 1572864
  34.7 0.3 copy-done.23
  35.0 0.7 fusion
  38.1 1.0 %broadcast_select_fusion.3 = (bf16[2,2,24,1536]{3,2,1,0:T(8,128)(2,1)}, bf16[2,2,24,1536]{3,2,1,0:T(8,128)(2,1)}) fusion(pred[]{:T(512)S(6)} %not.5, bf16[2,2,4,1536]{3,2,1,0:T(4,128)(2,1)S(1)} %get-tuple-element.52, bf16[2,2,4,1536]{3,2,1,0:T(4,128)(2,1)S(1)} %get-tuple-element.50, bf16[2,2,16,1536]{3,2,1,0:T(8,128)(2,1)S(1)} %get-tuple-element.82, ...), kind=kLoop, calls=%fused_computation.24 | loop fusion | flops 2064384 | bytes 1179650 | tf_op jit(solution)/shard_map/jit(_where)/select_n | solution.py:30
  39.1 1.3 %collective-permute-start.2 = (bf16[2,48,1536]{2,1,0:T(8,128)(2,1)}, bf16[2,48,1536]{2,1,0:T(8,128)(2,1)S(1)}, u32[]{:S(2)}, u32[]{:S(2)}) collective-permute-start(bf16[2,48,1536]{2,1,0:T(8,128)(2,1)} %bitcast.18), channel_id=1, source_target_pairs={{0,8},{8,0},{16,24},{24,16},{1,9},{9,1},{17,25},{25,17},{2,10},{10... | collective-permute-start | bytes 884744 | tf_op jit(solution)/shard_map/ppermute | solution.py:30
  40.4 1.9 %collective-permute-start.3 = (bf16[2,48,1536]{2,1,0:T(8,128)(2,1)}, bf16[2,48,1536]{2,1,0:T(8,128)(2,1)S(1)}, u32[]{:S(2)}, u32[]{:S(2)}) collective-permute-start(bf16[2,48,1536]{2,1,0:T(8,128)(2,1)} %bitcast.19), channel_id=1, source_target_pairs={{8,16},{16,8},{9,17},{17,9},{10,18},{18,10},{11,19},{19,11},{12,20... | collective-permute-start | bytes 884744 | tf_op jit(solution)/shard_map/ppermute | solution.py:30
  42.4 0.7 slice_bitcast_fusion.25
  43.2 0.8 copy-done.24
  44.1 1.1 %broadcast_select_fusion.2 = (bf16[2,2,24,1536]{3,2,1,0:T(8,128)(2,1)S(1)}, bf16[2,2,24,1536]{3,2,1,0:T(8,128)(2,1)S(1)}) fusion(pred[]{:T(512)S(6)} %not.5, bf16[2,2,4,1536]{3,2,1,0:T(4,128)(2,1)S(1)} %get-tuple-element.44, bf16[2,2,4,1536]{3,2,1,0:T(4,128)(2,1)} %get-tuple-element.42, bf16[2,2,16,1536]{3,2,1,0:T(8,128)(2,1)S(1)} %copy-done.25, ...), kind=kLoop, calls=%fused_computation.23 | loop fusion | flops 2064384 | bytes 1179650 | tf_op jit(solution)/shard_map/jit(_where)/select_n | solution.py:30
  45.3 3.5 %collective-permute-start.8 = (bf16[2,48,1536]{2,1,0:T(8,128)(2,1)S(1)}, bf16[2,48,1536]{2,1,0:T(8,128)(2,1)S(1)}, u32[]{:S(2)}, u32[]{:S(2)}) collective-permute-start(bf16[2,48,1536]{2,1,0:T(8,128)(2,1)S(1)} %bitcast.342), channel_id=1, source_target_pairs={{8,16},{16,8},{9,17},{17,9},{10,18},{18,10},{11,19},{19,11},{12,20... | collective-permute-start | bytes 884744 | tf_op jit(solution)/shard_map/ppermute | solution.py:30
  48.8 0.6 fusion.18
  49.5 0.7 fusion.17
  50.1 0.7 fusion.14
  50.8 0.7 fusion.13
  51.5 0.7 fusion.10
  52.2 0.7 fusion.9
  52.8 1.3 %broadcast_select_fusion.1 = bf16[2,144,1536]{2,1,0:T(8,128)(2,1)S(1)} fusion(bf16[2,144,1536]{2,1,0:T(8,128)(2,1)} %get-tuple-element.34, bf16[2,144,1536]{2,1,0:T(8,128)(2,1)S(1)} %get-tuple-element.33, pred[]{:T(512)S(6)} %eq.8), kind=kLoop, calls=%fused_computation.1 | loop fusion | flops 442368 | bytes 2654209 | tf_op jit(solution)/shard_map/jit(_where)/select_n | solution.py:30
  54.2 1.2 %collective-permute-start.4 = (bf16[2,144,1536]{2,1,0:T(8,128)(2,1)S(1)}, bf16[2,144,1536]{2,1,0:T(8,128)(2,1)S(1)}, u32[]{:S(2)}, u32[]{:S(2)}) collective-permute-start(bf16[2,144,1536]{2,1,0:T(8,128)(2,1)S(1)} %broadcast_select_fusion.1), channel_id=1, source_target_pairs={{0,1},{1,0},{2,3},{3,2},{4,5},{5,4},{6,7},{7,6},{8,9},{9,8},{10,11... | collective-permute-start | bytes 2654216 | tf_op jit(solution)/shard_map/ppermute | solution.py:30
  55.4 0.8 collective-permute-done.8.rest_4_
  56.2 1.1 %broadcast_select_fusion = bf16[2,144,1536]{2,1,0:T(8,128)(2,1)} fusion(bf16[2,144,1536]{2,1,0:T(8,128)(2,1)S(1)} %get-tuple-element.30, bf16[2,144,1536]{2,1,0:T(8,128)(2,1)S(1)} %get-tuple-element.29, pred[]{:T(512)S(6)} %eq.8), kind=kLoop, calls=%fused_computation | loop fusion | flops 442368 | bytes 2654209 | tf_op jit(solution)/shard_map/jit(_where)/select_n | solution.py:30
  57.3 2.1 %collective-permute-start.9 = (bf16[2,144,1536]{2,1,0:T(8,128)(2,1)}, bf16[2,144,1536]{2,1,0:T(8,128)(2,1)}, u32[]{:S(2)}, u32[]{:S(2)}) collective-permute-start(bf16[2,144,1536]{2,1,0:T(8,128)(2,1)} %broadcast_select_fusion), channel_id=1, source_target_pairs={{0,1},{1,0},{2,3},{3,2},{4,5},{5,4},{6,7},{7,6},{8,9},{9,8},{10,11... | collective-permute-start | bytes 2654216 | tf_op jit(solution)/shard_map/ppermute | solution.py:30
  59.4 6.9 %query_side.1 = (bf16[128,1536]{1,0:T(8,128)(2,1)S(1)}, f32[128,128]{1,0:T(8,128)S(1)}) custom-call(s32[12,3]{1,0:T(8,128)S(1)} %copy.177.radius_ref, s32[6]{0:T(128)S(1)} %stack.69.bounds_ref, s32[128,8]{1,0:T(8,128)S(1)} %copy-done.3, s32[8,512]{1,0:T(8,128)S(1)} %copy-done.7, bf16[2,128,1536]{2,1,0:T(8,128)(2,1)S(1)} %get-tuple-element.84.qd_ref.rest_0_, ...), custom_call_target="tpu_custom_call" | custom-call | tf_op jit(solution)/shard_map/query_side/pallas_call | solution.py:234
  66.4 2.1 %collective-permute-start.11 = (f32[1,32,128]{2,1,0:T(8,128)S(1)}, f32[1,32,128]{2,1,0:T(8,128)S(1)}, u32[]{:S(2)}, u32[]{:S(2)}) collective-permute-start(f32[1,32,128]{2,1,0:T(8,128)S(1)} %bitcast.346), channel_id=1, source_target_pairs={{2,4},{4,2},{3,5},{5,3},{10,12},{12,10},{11,13},{13,11},{18,20},{2... | collective-permute-start | bytes 49160 | tf_op jit(solution)/shard_map/ppermute | solution.py:30
  68.5 0.4 collective-permute-done.10.rest_7_
  68.9 2.8 %collective-permute-done.11.rest_8_ = f32[1,32,128]{2,1,0:T(8,128)S(1)} collective-permute-done((f32[1,32,128]{2,1,0:T(8,128)S(1)}, f32[1,32,128]{2,1,0:T(8,128)S(1)}, u32[]{:S(2)}, u32[]{:S(2)}) %collective-permute-start.11) | collective-permute-done | bytes 16416 | tf_op jit(solution)/shard_map/ppermute | solution.py:30
  71.8 1.9 %collective-permute-start.13 = (f32[1,48,128]{2,1,0:T(8,128)S(1)}, f32[1,48,128]{2,1,0:T(8,128)S(1)}, u32[]{:S(2)}, u32[]{:S(2)}) collective-permute-start(f32[1,48,128]{2,1,0:T(8,128)S(1)} %bitcast.344), channel_id=1, source_target_pairs={{8,16},{16,8},{9,17},{17,9},{10,18},{18,10},{11,19},{19,11},{12,20... | collective-permute-start | bytes 73736 | tf_op jit(solution)/shard_map/ppermute | solution.py:30
  73.8 0.7 collective-permute-done.12.rest_9_
  74.5 1.9 %collective-permute-done.13.rest_10_ = f32[1,48,128]{2,1,0:T(8,128)S(1)} collective-permute-done((f32[1,48,128]{2,1,0:T(8,128)S(1)}, f32[1,48,128]{2,1,0:T(8,128)S(1)}, u32[]{:S(2)}, u32[]{:S(2)}) %collective-permute-start.13) | collective-permute-done | bytes 24608 | tf_op jit(solution)/shard_map/ppermute | solution.py:30
  76.4 2.4 %collective-permute-start.14 = (f32[1,144,128]{2,1,0:T(8,128)S(1)}, f32[1,144,128]{2,1,0:T(8,128)S(1)}, u32[]{:S(2)}, u32[]{:S(2)}) collective-permute-start(f32[1,144,128]{2,1,0:T(8,128)S(1)} %broadcast_select_fusion.10), channel_id=1, source_target_pairs={{0,1},{1,0},{2,3},{3,2},{4,5},{5,4},{6,7},{7,6},{8,9},{9,8},{10,11... | collective-permute-start | bytes 221192 | tf_op jit(solution)/shard_map/ppermute | solution.py:30
  78.8 1.1 %reshape.432 = bf16[2,4,4,4,1536]{4,3,2,1,0:T(4,128)(2,1)S(1)} reshape(bf16[128,1536]{1,0:T(8,128)(2,1)} %copy-done.2) | data formatting | bytes 786432 | tf_op jit(solution)/shard_map/reshape | solution.py:208
  79.9 0.9 %copy.253 = bf16[2,4,4,4,1536]{4,3,0,2,1:T(4,128)(2,1)} copy(bf16[2,4,4,4,1536]{4,3,2,1,0:T(4,128)(2,1)S(1)} %reshape.432) | data formatting | bytes 786432 | tf_op jit(solution)/shard_map/reshape | solution.py:208
  80.8 0.6 copy-done.5
  81.5 0.9 copy-done.6
  82.4 4.5 %key_side.1 = (bf16[128,1536]{1,0:T(8,128)(2,1)S(1)}, bf16[128,1536]{1,0:T(8,128)(2,1)S(1)}) custom-call(s32[12,3]{1,0:T(8,128)S(1)} %copy.177.radius_ref, s32[6]{0:T(128)S(1)} %stack.69.bounds_ref, s32[128,8]{1,0:T(8,128)S(1)} %copy-done.4, s32[8,512]{1,0:T(8,128)S(1)} %copy-done.8, bf16[2,128,1536]{2,1,0:T(8,128)(2,1)S(1)} %get-tuple-element.85.rest_0_.kv_ref, ...), custom_call_target="tpu_custom_call" | custom-call | tf_op jit(solution)/shard_map/key_side/pallas_call | solution.py:250
  86.9 0.9 %copy.251 = bf16[2,4,4,4,1536]{4,3,0,2,1:T(4,128)(2,1)} copy(bf16[2,4,4,4,1536]{4,3,2,1,0:T(4,128)(2,1)S(1)} %reshape.446) | data formatting | bytes 786432 | tf_op jit(solution)/shard_map/reshape | solution.py:208
  87.9 0.9 %copy.252 = bf16[2,4,4,4,1536]{4,3,0,2,1:T(4,128)(2,1)} copy(bf16[2,4,4,4,1536]{4,3,2,1,0:T(4,128)(2,1)S(1)} %reshape.445) | data formatting | bytes 786432 | tf_op jit(solution)/shard_map/reshape | solution.py:208
  (104 shorter events, 2.8 us)
Async XLA Ops:
  2.9 35.0 %collective-permute-start = (bf16[2,32,1536]{2,1,0:T(8,128)(2,1)}, bf16[2,32,1536]{2,1,0:T(8,128)(2,1)S(1)}, u32[]{:S(2)}, u32[]{:S(2)}) collective-permute-start(bf16[2,32,1536]{2,1,0:T(8,128)(2,1)} %select_n.170), channel_id=1, source_target_pairs={{0,2},{2,0},{4,6},{6,4},{1,3},{3,1},{5,7},{7,5},{8,10},{10,8},{12,... | collective-permute-start | bytes 589832 | tf_op jit(solution)/shard_map/ppermute | solution.py:30
  4.1 2.9 %copy-start.11 = (bf16[4,4,2,4,1536]{4,3,2,1,0:T(4,128)(2,1)S(1)}, bf16[4,4,2,4,1536]{4,3,2,1,0:T(4,128)(2,1)}, u32[]{:S(2)}) copy-start(bf16[4,4,2,4,1536]{4,3,2,1,0:T(4,128)(2,1)} %param.8) | copy-start | bytes 1179652
  4.1 2.9 %copy-start.12 = (bf16[4,4,2,4,1536]{4,3,2,1,0:T(4,128)(2,1)S(1)}, bf16[4,4,2,4,1536]{4,3,2,1,0:T(4,128)(2,1)}, u32[]{:S(2)}) copy-start(bf16[4,4,2,4,1536]{4,3,2,1,0:T(4,128)(2,1)} %param.11) | copy-start | bytes 1179652
  4.9 33.1 %collective-permute-start.1 = (bf16[2,32,1536]{2,1,0:T(8,128)(2,1)}, bf16[2,32,1536]{2,1,0:T(8,128)(2,1)S(1)}, u32[]{:S(2)}, u32[]{:S(2)}) collective-permute-start(bf16[2,32,1536]{2,1,0:T(8,128)(2,1)} %select_n.173), channel_id=1, source_target_pairs={{2,4},{4,2},{3,5},{5,3},{10,12},{12,10},{11,13},{13,11},{18,20},{2... | collective-permute-start | bytes 589832 | tf_op jit(solution)/shard_map/ppermute | solution.py:30
  8.2 34.1 %collective-permute-start.5 = (bf16[2,32,1536]{2,1,0:T(8,128)(2,1)}, bf16[2,32,1536]{2,1,0:T(8,128)(2,1)S(1)}, u32[]{:S(2)}, u32[]{:S(2)}) collective-permute-start(bf16[2,32,1536]{2,1,0:T(8,128)(2,1)} %select_n.183), channel_id=1, source_target_pairs={{0,2},{2,0},{4,6},{6,4},{1,3},{3,1},{5,7},{7,5},{8,10},{10,8},{12,... | collective-permute-start | bytes 589832 | tf_op jit(solution)/shard_map/ppermute | solution.py:30
  8.2 4.9 %copy-start.9 = (bf16[4,4,2,4,1536]{4,3,2,1,0:T(4,128)(2,1)S(1)}, bf16[4,4,2,4,1536]{4,3,2,1,0:T(4,128)(2,1)}, u32[]{:S(2)}) copy-start(bf16[4,4,2,4,1536]{4,3,2,1,0:T(4,128)(2,1)} %param.9) | copy-start | bytes 1179652
  9.0 34.1 %collective-permute-start.6 = (bf16[2,32,1536]{2,1,0:T(8,128)(2,1)}, bf16[2,32,1536]{2,1,0:T(8,128)(2,1)S(1)}, u32[]{:S(2)}, u32[]{:S(2)}) collective-permute-start(bf16[2,32,1536]{2,1,0:T(8,128)(2,1)} %select_n.185), channel_id=1, source_target_pairs={{2,4},{4,2},{3,5},{5,3},{10,12},{12,10},{11,13},{13,11},{18,20},{2... | collective-permute-start | bytes 589832 | tf_op jit(solution)/shard_map/ppermute | solution.py:30
  14.2 1.0 %copy-start.10 = (bf16[4,4,2,4,1536]{4,3,2,1,0:T(4,128)(2,1)S(1)}, bf16[4,4,2,4,1536]{4,3,2,1,0:T(4,128)(2,1)}, u32[]{:S(2)}) copy-start(bf16[4,4,2,4,1536]{4,3,2,1,0:T(4,128)(2,1)} %param.10) | copy-start | bytes 1179652
  21.7 1.0 %copy-start.18 = (bf16[1,2,64,1536]{3,2,0,1:T(8,128)(2,1)S(1)}, bf16[1,2,64,1536]{3,2,0,1:T(8,128)(2,1)}, u32[]{:S(2)}) copy-start(bf16[1,2,64,1536]{3,2,0,1:T(8,128)(2,1)} %stack.78) | copy-start | bytes 1179652
  22.7 1.0 %copy-start.19 = (bf16[1,2,64,1536]{3,2,0,1:T(8,128)(2,1)S(1)}, bf16[1,2,64,1536]{3,2,0,1:T(8,128)(2,1)}, u32[]{:S(2)}) copy-start(bf16[1,2,64,1536]{3,2,0,1:T(8,128)(2,1)} %stack.79) | copy-start | bytes 1179652
  30.0 0.7 copy-start.26
  30.7 1.0 %copy-start.17 = (bf16[2,4,4,4,1536]{4,1,3,2,0:T(4,128)(2,1)S(1)}, bf16[2,4,4,4,1536]{4,1,3,2,0:T(4,128)(2,1)}, u32[]{:S(2)}) copy-start(bf16[2,4,4,4,1536]{4,1,3,2,0:T(4,128)(2,1)} %copy.182) | copy-start | bytes 1179652
  32.6 1.0 %copy-start.16 = (bf16[1,2,64,1536]{3,2,0,1:T(8,128)(2,1)S(1)}, bf16[1,2,64,1536]{3,2,0,1:T(8,128)(2,1)}, u32[]{:S(2)}) copy-start(bf16[1,2,64,1536]{3,2,0,1:T(8,128)(2,1)} %stack.88) | copy-start | bytes 1179652
  33.6 1.1 %copy-start.22 = (bf16[2,4,4,4,1536]{4,1,3,2,0:T(4,128)(2,1)S(1)}, bf16[2,4,4,4,1536]{4,1,3,2,0:T(4,128)(2,1)}, u32[]{:S(2)}) copy-start(bf16[2,4,4,4,1536]{4,1,3,2,0:T(4,128)(2,1)} %copy.161) | copy-start | bytes 1179652
  33.6 1.4 %copy-start.23 = (bf16[2,4,4,4,1536]{4,1,3,2,0:T(4,128)(2,1)S(1)}, bf16[2,4,4,4,1536]{4,1,3,2,0:T(4,128)(2,1)}, u32[]{:S(2)}) copy-start(bf16[2,4,4,4,1536]{4,1,3,2,0:T(4,128)(2,1)} %copy.162) | copy-start | bytes 1179652
  35.7 2.2 %copy-start.20 = (bf16[1,128,1536]{2,1,0:T(8,128)(2,1)S(1)}, bf16[1,128,1536]{2,1,0:T(8,128)(2,1)}, u32[]{:S(2)}) copy-start(bf16[1,128,1536]{2,1,0:T(8,128)(2,1)} %stack_reshape.15) | copy-start | bytes 1179652
  35.7 2.2 %copy-start.21 = (bf16[1,128,1536]{2,1,0:T(8,128)(2,1)S(1)}, bf16[1,128,1536]{2,1,0:T(8,128)(2,1)}, u32[]{:S(2)}) copy-start(bf16[1,128,1536]{2,1,0:T(8,128)(2,1)} %stack_reshape.13) | copy-start | bytes 1179652
  39.1 12.3 %collective-permute-start.2 = (bf16[2,48,1536]{2,1,0:T(8,128)(2,1)}, bf16[2,48,1536]{2,1,0:T(8,128)(2,1)S(1)}, u32[]{:S(2)}, u32[]{:S(2)}) collective-permute-start(bf16[2,48,1536]{2,1,0:T(8,128)(2,1)} %bitcast.18), channel_id=1, source_target_pairs={{0,8},{8,0},{16,24},{24,16},{1,9},{9,1},{17,25},{25,17},{2,10},{10... | collective-permute-start | bytes 884744 | tf_op jit(solution)/shard_map/ppermute | solution.py:30
  40.4 11.7 %collective-permute-start.3 = (bf16[2,48,1536]{2,1,0:T(8,128)(2,1)}, bf16[2,48,1536]{2,1,0:T(8,128)(2,1)S(1)}, u32[]{:S(2)}, u32[]{:S(2)}) collective-permute-start(bf16[2,48,1536]{2,1,0:T(8,128)(2,1)} %bitcast.19), channel_id=1, source_target_pairs={{8,16},{16,8},{9,17},{17,9},{10,18},{18,10},{11,19},{19,11},{12,20... | collective-permute-start | bytes 884744 | tf_op jit(solution)/shard_map/ppermute | solution.py:30
  43.1 0.9 %copy-start.24 = (bf16[2,2,16,1536]{3,2,1,0:T(8,128)(2,1)S(1)}, bf16[2,2,16,1536]{3,2,1,0:T(8,128)(2,1)}, u32[]{:S(2)}) copy-start(bf16[2,2,16,1536]{3,2,1,0:T(8,128)(2,1)} %get-tuple-element.19) | copy-start | bytes 589828
  43.1 1.0 %copy-start.25 = (bf16[2,2,16,1536]{3,2,1,0:T(8,128)(2,1)S(1)}, bf16[2,2,16,1536]{3,2,1,0:T(8,128)(2,1)}, u32[]{:S(2)}) copy-start(bf16[2,2,16,1536]{3,2,1,0:T(8,128)(2,1)} %get-tuple-element.20) | copy-start | bytes 589828
  43.1 5.7 %copy-start.13 = (bf16[2,144,1536]{2,1,0:T(8,128)(2,1)S(1)}, bf16[2,144,1536]{2,1,0:T(8,128)(2,1)}, u32[]{:S(2)}) copy-start(bf16[2,144,1536]{2,1,0:T(8,128)(2,1)} %get-tuple-element.21) | copy-start | bytes 2654212
  44.1 6.0 %copy-start.14 = (bf16[2,144,1536]{2,1,0:T(8,128)(2,1)S(1)}, bf16[2,144,1536]{2,1,0:T(8,128)(2,1)}, u32[]{:S(2)}) copy-start(bf16[2,144,1536]{2,1,0:T(8,128)(2,1)} %get-tuple-element.17) | copy-start | bytes 2654212
  45.2 10.2 %collective-permute-start.7 = (bf16[2,48,1536]{2,1,0:T(8,128)(2,1)S(1)}, bf16[2,48,1536]{2,1,0:T(8,128)(2,1)S(1)}, u32[]{:S(2)}, u32[]{:S(2)}) collective-permute-start(bf16[2,48,1536]{2,1,0:T(8,128)(2,1)S(1)} %bitcast.343), channel_id=1, source_target_pairs={{0,8},{8,0},{16,24},{24,16},{1,9},{9,1},{17,25},{25,17},{2,10},{10... | collective-permute-start | bytes 884744 | tf_op jit(solution)/shard_map/ppermute | solution.py:30
  45.3 10.9 %collective-permute-start.8 = (bf16[2,48,1536]{2,1,0:T(8,128)(2,1)S(1)}, bf16[2,48,1536]{2,1,0:T(8,128)(2,1)S(1)}, u32[]{:S(2)}, u32[]{:S(2)}) collective-permute-start(bf16[2,48,1536]{2,1,0:T(8,128)(2,1)S(1)} %bitcast.342), channel_id=1, source_target_pairs={{8,16},{16,8},{9,17},{17,9},{10,18},{18,10},{11,19},{19,11},{12,20... | collective-permute-start | bytes 884744 | tf_op jit(solution)/shard_map/ppermute | solution.py:30
  52.8 2.5 %copy-start.15 = (bf16[2,144,1536]{2,1,0:T(8,128)(2,1)S(1)}, bf16[2,144,1536]{2,1,0:T(8,128)(2,1)}, u32[]{:S(2)}) copy-start(bf16[2,144,1536]{2,1,0:T(8,128)(2,1)} %get-tuple-element.38) | copy-start | bytes 2654212
  54.2 5.2 %collective-permute-start.4 = (bf16[2,144,1536]{2,1,0:T(8,128)(2,1)S(1)}, bf16[2,144,1536]{2,1,0:T(8,128)(2,1)S(1)}, u32[]{:S(2)}, u32[]{:S(2)}) collective-permute-start(bf16[2,144,1536]{2,1,0:T(8,128)(2,1)S(1)} %broadcast_select_fusion.1), channel_id=1, source_target_pairs={{0,1},{1,0},{2,3},{3,2},{4,5},{5,4},{6,7},{7,6},{8,9},{9,8},{10,11... | collective-permute-start | bytes 2654216 | tf_op jit(solution)/shard_map/ppermute | solution.py:30
  56.2 3.2 %copy-start.3 = (s32[128,8]{1,0:T(8,128)S(1)}, s32[128,8]{1,0:T(8,128)}, u32[]{:S(2)}) copy-start(s32[128,8]{1,0:T(8,128)} %constant.34.clone.oc_ref) | copy-start | bytes 12292
  56.2 3.1 %copy-start.7 = (s32[8,512]{1,0:T(8,128)S(1)}, s32[8,512]{1,0:T(8,128)}, u32[]{:S(2)}) copy-start(s32[8,512]{1,0:T(8,128)} %constant.35.clone.kc_ref) | copy-start | bytes 49156
  57.3 23.6 %collective-permute-start.9 = (bf16[2,144,1536]{2,1,0:T(8,128)(2,1)}, bf16[2,144,1536]{2,1,0:T(8,128)(2,1)}, u32[]{:S(2)}, u32[]{:S(2)}) collective-permute-start(bf16[2,144,1536]{2,1,0:T(8,128)(2,1)} %broadcast_select_fusion), channel_id=1, source_target_pairs={{0,1},{1,0},{2,3},{3,2},{4,5},{5,4},{6,7},{7,6},{8,9},{9,8},{10,11... | collective-permute-start | bytes 2654216 | tf_op jit(solution)/shard_map/ppermute | solution.py:30
  66.2 2.3 %copy-start = (f32[128,128]{1,0:T(8,128)}, f32[128,128]{1,0:T(8,128)S(1)}, u32[]{:S(2)}) copy-start(f32[128,128]{1,0:T(8,128)S(1)} %get-tuple-element.8) | copy-start | bytes 196612
  66.2 10.2 %copy-start.2 = (bf16[128,1536]{1,0:T(8,128)(2,1)}, bf16[128,1536]{1,0:T(8,128)(2,1)S(1)}, u32[]{:S(2)}) copy-start(bf16[128,1536]{1,0:T(8,128)(2,1)S(1)} %get-tuple-element.7) | copy-start | bytes 1179652
  66.3 2.7 %collective-permute-start.10 = (f32[1,32,128]{2,1,0:T(8,128)S(1)}, f32[1,32,128]{2,1,0:T(8,128)S(1)}, u32[]{:S(2)}, u32[]{:S(2)}) collective-permute-start(f32[1,32,128]{2,1,0:T(8,128)S(1)} %bitcast.347), channel_id=1, source_target_pairs={{0,2},{2,0},{4,6},{6,4},{1,3},{3,1},{5,7},{7,5},{8,10},{10,8},{12,... | collective-permute-start | bytes 49160 | tf_op jit(solution)/shard_map/ppermute | solution.py:30
  66.4 5.4 %collective-permute-start.11 = (f32[1,32,128]{2,1,0:T(8,128)S(1)}, f32[1,32,128]{2,1,0:T(8,128)S(1)}, u32[]{:S(2)}, u32[]{:S(2)}) collective-permute-start(f32[1,32,128]{2,1,0:T(8,128)S(1)} %bitcast.346), channel_id=1, source_target_pairs={{2,4},{4,2},{3,5},{5,3},{10,12},{12,10},{11,13},{13,11},{18,20},{2... | collective-permute-start | bytes 49160 | tf_op jit(solution)/shard_map/ppermute | solution.py:30
  71.8 2.7 %collective-permute-start.12 = (f32[1,48,128]{2,1,0:T(8,128)S(1)}, f32[1,48,128]{2,1,0:T(8,128)S(1)}, u32[]{:S(2)}, u32[]{:S(2)}) collective-permute-start(f32[1,48,128]{2,1,0:T(8,128)S(1)} %bitcast.345), channel_id=1, source_target_pairs={{0,8},{8,0},{16,24},{24,16},{1,9},{9,1},{17,25},{25,17},{2,10},{10... | collective-permute-start | bytes 73736 | tf_op jit(solution)/shard_map/ppermute | solution.py:30
  71.8 4.6 %collective-permute-start.13 = (f32[1,48,128]{2,1,0:T(8,128)S(1)}, f32[1,48,128]{2,1,0:T(8,128)S(1)}, u32[]{:S(2)}, u32[]{:S(2)}) collective-permute-start(f32[1,48,128]{2,1,0:T(8,128)S(1)} %bitcast.344), channel_id=1, source_target_pairs={{8,16},{16,8},{9,17},{17,9},{10,18},{18,10},{11,19},{19,11},{12,20... | collective-permute-start | bytes 73736 | tf_op jit(solution)/shard_map/ppermute | solution.py:30
  76.4 4.4 %collective-permute-start.14 = (f32[1,144,128]{2,1,0:T(8,128)S(1)}, f32[1,144,128]{2,1,0:T(8,128)S(1)}, u32[]{:S(2)}, u32[]{:S(2)}) collective-permute-start(f32[1,144,128]{2,1,0:T(8,128)S(1)} %broadcast_select_fusion.10), channel_id=1, source_target_pairs={{0,1},{1,0},{2,3},{3,2},{4,5},{5,4},{6,7},{7,6},{8,9},{9,8},{10,11... | collective-permute-start | bytes 221192 | tf_op jit(solution)/shard_map/ppermute | solution.py:30
  79.9 1.6 %copy-start.1 = (f32[128,128]{1,0:T(8,128)S(1)}, f32[128,128]{1,0:T(8,128)}, u32[]{:S(2)}) copy-start(f32[128,128]{1,0:T(8,128)} %copy-done) | copy-start | bytes 196612
  79.9 1.6 %copy-start.4 = (s32[128,8]{1,0:T(8,128)S(1)}, s32[128,8]{1,0:T(8,128)}, u32[]{:S(2)}) copy-start(s32[128,8]{1,0:T(8,128)} %constant.34.clone.oc_ref) | copy-start | bytes 12292
  79.9 1.6 %copy-start.8 = (s32[8,512]{1,0:T(8,128)S(1)}, s32[8,512]{1,0:T(8,128)}, u32[]{:S(2)}) copy-start(s32[8,512]{1,0:T(8,128)} %constant.35.clone.kc_ref) | copy-start | bytes 49156
  80.8 0.6 copy-start.5
  81.5 0.9 copy-start.6

commit v2 on v1

v2 whole, which is shorter than its diff:
```python
import functools
import math

import jax
import jax.numpy as jnp
import numpy as np
from jax import lax
from jax.experimental import pallas as pl
from jax.experimental.pallas import tpu as pltpu
from jax.sharding import PartitionSpec as P


NEG = -1e30
LOG2E = 1.4426950408889634
EVEN, ODD = 1000, 1001
AXES = ("ta", "ha", "wa")


def matchings(n):
    even = [(i, i ^ 1) for i in range(n) if (i ^ 1) < n]
    odd = [(i, ((i + 1) ^ 1) - 1) for i in range(n) if 0 <= ((i + 1) ^ 1) - 1 < n]
    return [m for m in (even, odd) if m]


def swap(axis, sends):
    got = []
    for k, pairs in enumerate(matchings(lax.axis_size(axis))):
        got.append(lax.ppermute(sends[k], axis, pairs))
    return got


def sent_layer(axis, k, length):
    odd = lax.rem(lax.axis_index(axis), 2)
    return (1 - odd if k == 0 else odd) * (length - 1)


def by_parity(axis, count, length, put):
    odd = lax.rem(lax.axis_index(axis), 2)

    @pl.when(odd == 0)
    def _():
        for k in range(count):
            put(k, length - 1 if k == 0 else 0)

    @pl.when(odd == 1)
    def _():
        for k in range(count):
            put(k, 0 if k == 0 else length - 1)


def prepare_kernel(block, count, *refs):
    T, H, W, C = block
    args, refs = refs[:4], refs[4:]
    faces, wholes, (buf, sems) = refs[: 2 * count], refs[2 * count : 2 * count + 2], refs[-2:]
    copies = [
        [pltpu.make_async_copy(args[a].at[t], buf.at[a, t], sems.at[a, t]) for t in range(T)]
        for a in range(4)
    ]
    for a in range(4):
        for copy in copies[a]:
            copy.start()
    width = buf.shape[-1]
    for a in range(4):
        for copy in copies[a]:
            copy.wait()
        whole = wholes[a // 2]
        for k in range(count):
            layer = sent_layer("ha", k, H)
            out = faces[(a // 2) * count + k]
            for w in range(W):
                out[a % 2, w * T * C : (w + 1) * T * C, :] = buf[a, :, layer, w].reshape(
                    T * C, width
                )
        for w in range(W):
            for t in range(T):
                r = (w * T + t) * H * C
                whole[a % 2, r : r + H * C, :] = buf[a, t, :, w].reshape(H * C, width)


def time_kernel(block, near, count, own_ref, *refs):
    T, H, W, C = block
    ha, outs = refs[:near], refs[near:]

    def put(k, t):
        for a in range(own_ref.shape[0]):
            for w in range(W):
                i = w * T + t
                parts = [own_ref[a, i * H * C : (i + 1) * H * C, :]]
                parts += [r[a, i * C : (i + 1) * C, :] for r in ha]
                n = (H + near) * C
                outs[k][a, w * n : (w + 1) * n, :] = jnp.concatenate(parts, axis=0)

    by_parity("ta", count, T, put)


def column_kernel(block, count, *refs):
    _, _, W, _ = block
    pieces, outs = refs[: len(refs) - count], refs[len(refs) - count :]

    def put(k, w):
        for a in range(outs[k].shape[0]):
            at = 0
            for r in pieces:
                n = r.shape[1] // W
                outs[k][a, at : at + n, :] = r[a, w * n : (w + 1) * n, :]
                at += n

    by_parity("wa", count, W, put)


def local(kernel, out_shape, operands, space=pltpu.VMEM, **kw):
    place = pl.BlockSpec(memory_space=space)
    return pl.pallas_call(
        kernel,
        out_shape=out_shape,
        in_specs=[place] * len(operands),
        out_specs=[pl.BlockSpec(memory_space=pltpu.VMEM)] * len(out_shape),
        compiler_params=pltpu.CompilerParams(vmem_limit_bytes=16 << 20),
        **kw,
    )(*operands)


def spread(own, ha, block, counts, name):
    _, H, W, C = block
    k, _, width = own.shape
    kind = pltpu.VMEM
    n = W * (H + counts[1]) * C
    ta = swap(
        "ta",
        local(
            functools.partial(time_kernel, block, counts[1], counts[0]),
            [kind((k, n, width), own.dtype)] * counts[0],
            [own] + ha,
            name=name + "_time",
        ),
    )
    n = sum(p.shape[1] for p in [own] + ha + ta) // W
    wa = swap(
        "wa",
        local(
            functools.partial(column_kernel, block, counts[2]),
            [kind((k, n, width), own.dtype)] * counts[2],
            [own] + ha + ta,
            name=name + "_column",
        ),
    )
    return ha + ta + wa


def stat_halo(own, block):
    T, H, W, C = block
    k, _, width = own.shape

    def exchange(axis, first, last):
        odd = lax.rem(lax.axis_index(axis), 2) == 1
        return swap(axis, [jnp.where(odd, first, last), jnp.where(odd, last, first)])

    grid = own.reshape(k, W, T, H, C, width)
    ha = exchange(
        "ha",
        grid[:, :, :, 0].reshape(k, W * T * C, width),
        grid[:, :, :, H - 1].reshape(k, W * T * C, width),
    )
    own_t = own.reshape(k, W, T, H * C, width)
    ha_t = [p.reshape(k, W, T, C, width) for p in ha]

    def time_layer(t):
        layers = [own_t[:, :, t]] + [p[:, :, t] for p in ha_t]
        return jnp.concatenate(layers, axis=2).reshape(k, -1, width)

    ta = exchange("ta", time_layer(0), time_layer(T - 1))

    def column(w):
        return jnp.concatenate(
            [p.reshape(k, W, -1, width)[:, w] for p in [own] + ha + ta], axis=1
        )

    return ha + ta + exchange("wa", column(0), column(W - 1))


def piece_coords(block, counts):
    T, H, W, C = block
    marks = (EVEN, ODD)

    own = [[[(t, h, w) for h in range(H)] for t in range(T)] for w in range(W)]
    pieces = [np.array(own, np.int32).reshape(W, -1, 3)]
    for m in marks[: counts[1]]:
        pieces.append(np.array([[(t, m, w) for t in range(T)] for w in range(W)], np.int32))
    hs = list(range(H)) + list(marks[: counts[1]])
    for m in marks[: counts[0]]:
        pieces.append(np.array([[(m, h, w) for h in hs] for w in range(W)], np.int32))
    column = np.concatenate([p[0] for p in pieces], axis=0)
    out = [p.reshape(-1, 3) for p in pieces]
    for m in marks[: counts[2]]:
        c = column.copy()
        c[:, 2] = m
        out.append(c)
    return np.repeat(np.concatenate(out, axis=0), C, axis=0)


def codes_kernel(block, grids, *refs):
    sources, outs, bufs, sems = refs[:4], refs[4:7], refs[7:11], refs[11]
    copies = [pltpu.make_async_copy(s, b, sems.at[i]) for i, (s, b) in enumerate(zip(sources, bufs))]
    for copy in copies:
        copy.start()
    for copy in copies:
        copy.wait()
    oc_ref, kc_ref, valid_ref, radius_ref = bufs
    query_ref, key_ref, closed_ref = outs
    r = radius_ref[...]
    closed = 8 + (1 - r[0:1]) + 2 * (1 - r[1:2]) + 4 * (1 - r[2:3])
    closed_ref[...] = jnp.broadcast_to(closed, closed_ref.shape)
    code = same = 0
    bad_key = bad_own = 0
    for a, axis in enumerate(AXES):
        length, grid = block[a], grids[a]

        def line(i):
            i = i % grid
            if a == 0:
                return valid_ref[i, 1:2, 1:2]
            if a == 1:
                return valid_ref[1, 1:2, i : i + 1]
            return valid_ref[1, i : i + 1, 1:2]

        low = 1 - line(0)
        high = grid - 3 + line(-1) + line(-2)
        index = lax.axis_index(axis)
        odd = lax.rem(index, 2)
        at_even = jnp.where(odd == 1, -1, length)
        at_odd = jnp.where(odd == 1, length, -1)
        own = oc_ref[:, a : a + 1]
        outer = kc_ref[a : a + 1, :]
        outer = jnp.where(outer == EVEN, at_even, jnp.where(outer == ODD, at_odd, outer))
        place = outer + index * length
        here = own + index * length
        outside = jnp.where((place >= 0) & (place < grid), 0, 8)
        apart = jnp.abs(own - outer)
        same = same | apart
        code = code | jnp.where(apart > 1, 8, apart << a) | outside
        bad_key = bad_key | jnp.where((place >= low) & (place <= high), 0, 8)
        bad_own = bad_own | jnp.where((here >= low) & (here <= high), 0, 8)
    query_ref[...] = code | jnp.where(same == 0, 0, bad_key)
    key_ref[...] = code | jnp.where(same == 0, 0, bad_own)


NT = (((1,), (1,)), ((), ()))
NN = (((1,), (0,)), ((), ()))


def dot(a, b, dims):
    return lax.dot_general(a, b, dims, preferred_element_type=jnp.float32)


def gather(refs, which, cols, pad):
    parts = [r[which, :, cols] for r in refs]
    if pad:
        parts.append(jnp.zeros((pad, parts[0].shape[1]), parts[0].dtype))
    return jnp.concatenate(parts, axis=0)


def put_tiles(ref, value, cols):
    T, H, W, C, _ = ref.shape
    value = value.astype(ref.dtype)
    for w in range(W):
        for t in range(T):
            r = (w * T + t) * H * C
            ref[t, :, w, :, cols] = value[r : r + H * C].reshape(H, C, value.shape[1])


def query_kernel(cfg, closed_ref, code_ref, qd_ref, *rest):
    heads, depth, pad, count = cfg
    kv = rest[:count]
    dq_ref, stat_ref, s_ref, g_ref, d_ref = rest[count:]
    scale = 1.0 / math.sqrt(depth)
    rows = qd_ref.shape[1]
    step = math.gcd(rows, 32)
    stat_ref[...] = jnp.zeros(stat_ref.shape, jnp.float32)

    def columns(h):
        return slice(h * depth, (h + 1) * depth)

    def products(h):
        cols = columns(h)
        s_ref[h % 2] = dot(qd_ref[0, :, cols], gather(kv, 0, cols, pad), NT)
        g_ref[h % 2] = dot(qd_ref[1, :, cols], gather(kv, 1, cols, pad), NT)

    products(0)
    for h in range(heads):
        if h + 1 < heads:
            products(h + 1)
        ratios = []
        for r in range(0, rows, step):
            band = slice(r, r + step)
            allowed = (code_ref[band, :] & closed_ref[0:1, h : h + 1]) == 0
            scores = jnp.where(allowed, s_ref[h % 2, band, :], NEG)
            peak = jnp.max(scores, axis=1, keepdims=True)
            raised = jnp.exp2((scores - peak) * (scale * LOG2E))
            total = jnp.sum(raised, axis=1, keepdims=True)
            grads = g_ref[h % 2, band, :]
            drift = jnp.sum(raised * grads, axis=1, keepdims=True) / total
            d_ref[h % 2, band, :] = (raised * (grads - drift)).astype(jnp.bfloat16)
            stat_ref[band, h : h + 1] = peak * (scale * LOG2E) + jnp.log2(total)
            stat_ref[band, heads + h : heads + h + 1] = drift
            ratios.append(scale / total)
        cols = columns(h)
        product = dot(d_ref[h % 2], gather(kv, 0, cols, pad), NN)
        put_tiles(dq_ref, product * jnp.concatenate(ratios, axis=0), cols)


def key_kernel(cfg, closed_ref, code_ref, kv_ref, *rest):
    heads, depth, pad, count = cfg
    qd = rest[:count]
    st = rest[count : 2 * count]
    dk_ref, dv_ref, row_ref = rest[2 * count :]
    scale = 1.0 / math.sqrt(depth)
    parts = [r[0] for r in st]
    if pad:
        parts.append(jnp.zeros((pad, parts[0].shape[1]), jnp.float32))
    row_ref[...] = jnp.concatenate(parts, axis=0).T
    for h in range(heads):
        cols = slice(h * depth, (h + 1) * depth)
        queries = gather(qd, 0, cols, pad)
        cotangent = gather(qd, 1, cols, pad)
        allowed = (code_ref[...] & closed_ref[0:1, h : h + 1]) == 0
        scores = dot(kv_ref[0, :, cols], queries, NT) * (scale * LOG2E)
        scores = jnp.where(allowed, scores, NEG)
        attention = jnp.exp2(scores - row_ref[h : h + 1, :])
        grads = dot(kv_ref[1, :, cols], cotangent, NT)
        score_grads = (attention * (grads - row_ref[heads + h : heads + h + 1, :])).astype(
            jnp.bfloat16
        )
        put_tiles(dk_ref, dot(score_grads, queries, NN) * scale, cols)
        put_tiles(dv_ref, dot(attention.astype(jnp.bfloat16), cotangent, NN), cols)


def per_device(queries, key_states, value_states, output_cotangent, tile_valid, window_radius):
    T, H, W, C, width = queries.shape
    block = (T, H, W, C)
    heads = window_radius.shape[0]
    depth = width // heads
    sizes = tuple(lax.axis_size(a) for a in AXES)
    grids = tuple(n * b for n, b in zip(sizes, block))
    counts = tuple(len(matchings(n)) for n in sizes)
    rows = T * H * W * C

    kind = jax.ShapeDtypeStruct
    args = [
        pltpu.with_memory_space_constraint(x, pltpu.HBM)
        for x in (key_states, value_states, queries, output_cotangent)
    ]
    made = local(
        functools.partial(prepare_kernel, block, counts[1]),
        [pltpu.VMEM((2, W * T * C, width), jnp.bfloat16)] * (2 * counts[1])
        + [pltpu.VMEM((2, rows, width), jnp.bfloat16)] * 2,
        args,
        space=pltpu.HBM,
        scratch_shapes=[
            pltpu.VMEM((4, T, H, W, C, width), jnp.bfloat16),
            pltpu.SemaphoreType.DMA((4, T)),
        ],
        name="prepare",
    )
    kv, qd = made[-2:]
    kv_ha = swap("ha", made[: counts[1]])
    qd_ha = swap("ha", made[counts[1] : 2 * counts[1]])
    kv_pieces = [kv] + spread(kv, kv_ha, block, counts, "kv")
    qd_pieces = [qd] + spread(qd, qd_ha, block, counts, "qd")

    coords = piece_coords(block, counts)
    total = coords.shape[0]
    padded = -(-total // 128) * 128
    pad = padded - total
    outer = np.full((8, padded), -(1 << 20), np.int32)
    outer[:3, :total] = coords.T
    inner = np.zeros((rows, 8), np.int32)
    inner[:, :3] = coords[:rows]
    cfg = (heads, depth, pad, len(kv_pieces))
    native = kind(queries.shape, jnp.bfloat16)
    lanes = -(-2 * heads // 128) * 128
    tables = [inner, outer, tile_valid.transpose(0, 2, 1), window_radius.T]
    query_code, key_code, closed = local(
        functools.partial(codes_kernel, block, grids),
        [pltpu.VMEM((rows, padded), jnp.int32)] * 2 + [pltpu.VMEM((8, heads), jnp.int32)],
        [pltpu.with_memory_space_constraint(jnp.asarray(x), pltpu.HBM) for x in tables],
        space=pltpu.HBM,
        scratch_shapes=[pltpu.VMEM(x.shape, jnp.int32) for x in tables]
        + [pltpu.SemaphoreType.DMA((4,))],
        name="codes",
    )

    query_gradient, stats = local(
        functools.partial(query_kernel, cfg),
        [native, pltpu.VMEM((rows, lanes), jnp.float32)],
        [closed, query_code, qd] + kv_pieces,
        scratch_shapes=[pltpu.VMEM((2, rows, padded), jnp.float32)] * 2
        + [pltpu.VMEM((2, rows, padded), jnp.bfloat16)],
        name="query_side",
    )
    stat_pieces = [stats[None]] + stat_halo(stats[None], block)
    key_gradient, value_gradient = local(
        functools.partial(key_kernel, cfg),
        [native, native],
        [closed, key_code, kv] + qd_pieces + stat_pieces,
        scratch_shapes=[pltpu.VMEM((lanes, padded), jnp.float32)],
        name="key_side",
    )
    return (query_gradient, key_gradient, value_gradient)


def solution(mesh):
    split = P("ta", "ha", "wa", None, None)

    return jax.shard_map(
        per_device,
        mesh=mesh,
        in_specs=(split, split, split, split, P(), P()),
        out_specs=(split, split, split),
        check_vma=False,
    )
```

time: 89.7 us -> 73.2 us (0.82)
  local copies, waits for them, and re-layouts: 33.1 us -> 0.03 us
  waiting for transfers between devices: 6.68 us -> 34.5 us
  other arithmetic: 6.94 us -> 0.03 us
  between operations: 6.85 us -> 0.78 us
  Pallas kernels: 11.3 us -> 14.1 us
    ppermute x15, waiting for transfers between devices: 6.68 us -> 34.5 us  [swap(): got.append(lax.ppermute(sends[k], axis, pairs))]
    unnamed x73 -> x4, local copies, waits for them, and re-layouts: 13 us -> 0.02 us
    select_n x11 -> x3, other arithmetic: 6.28 us -> 0.03 us  [the longest x2 0.02 us: exchange(): jnp.where(odd, last, first)]
    another operation x13 -> x0, local copies, waits for them, and re-layouts: 4.76 us -> none  [the longest x5 2.65 us: per_device(): kv = jnp.stack([rowwise(key_states), rowwise(value_states)])]
    reshape x10 -> x0, local copies, waits for them, and re-layouts: 4.16 us -> none  [the longest x6 3.95 us: tilewise(): return x.reshape(W, T, H, C, width).transpose(1, 2, 0, 3, 4)]
    transpose x8 -> x0, local copies, waits for them, and re-layouts: 4.05 us -> none  [rowwise(): return x.transpose(2, 0, 1, 3, 4).reshape(rows, width)]
    select_n x8 -> x0, local copies, waits for them, and re-layouts: 3.2 us -> none  [exchange(): pieces.append(lax.ppermute(jnp.where(flip, first, last), axis, pairs))]
    pallas_call x2 -> x8, Pallas kernels: 11.3 us -> 14.1 us  [local(): pl.pallas_call(kernel, out_shape=out_shape, in_specs=[place] * len(operan...]
  transfers between devices with their start and end apart: 15 -> 15, of which waited for: 5 -> 13; matrix products, arithmetic and copies ran while one was open for 32% -> 0% of each run, Pallas kernels for 8% -> 10%
where the time goes in v2:
time: 73.2 us; the launch traced here: 72.8 us
  waiting for transfers between devices  34.5 us (47%)
  starting transfers between devices  23.4 us (32%)
  Pallas kernels  14.1 us (19%)
  between operations  0.78 us (1%)
    ppermute x15, waiting for transfers between devices, swap(): got.append(lax.ppermute(sends[k], axis, pairs))  34.5 us
    ppermute x15, starting transfers between devices, swap(): got.append(lax.ppermute(sends[k], axis, pairs))  23.4 us
    pallas_call x8, Pallas kernels, local(): pl.pallas_call(kernel, out_shape=out_shape, in_specs=[place] * len(operan...  14.1 us
  transfers between devices with their start and end apart: 15, of which 13 were waited for; matrix products, arithmetic and copies ran while one was open for 0% of the time, Pallas kernels for 10%

profile of v2, /device:TPU:21, one launch (start us, length us, event | category | flops | bytes accessed | tf_op | source)
XLA Modules:
  0.0 72.8 jit_solution(15096910816001680484)
XLA Ops:
  0.6 1.7 %prepare.1 = (bf16[2,32,1536]{2,1,0:T(8,128)(2,1)S(1)}, bf16[2,32,1536]{2,1,0:T(8,128)(2,1)S(1)}, bf16[2,32,1536]{2,1,0:T(8,128)(2,1)S(1)}, bf16[2,32,1536]{2,1,...) custom-call(bf16[4,4,2,4,1536]{4,3,2,1,0:T(4,128)(2,1)} %refs_0_.2, ...), custom_call_target="tpu_custom_call" | custom-call | tf_op jit(solution)/shard_map/prepare/pallas_call | solution.py:113
  2.3 1.3 %collective-permute-start = (bf16[2,32,1536]{2,1,0:T(8,128)(2,1)S(1)}, bf16[2,32,1536]{2,1,0:T(8,128)(2,1)S(1)}, u32[]{:S(2)}, u32[]{:S(2)}) collective-permute-start(bf16[2,32,1536]{2,1,0:T(8,128)(2,1)S(1)} %get-tuple-element.24), channel_id=1, source_target_pairs={{0,2},{2,0},{4,6},{6,4},{1,3},{3,1},{5,7},{7,5},{8,10},{10,8},{12,... | collective-permute-start | bytes 589832 | tf_op jit(solution)/shard_map/ppermute | solution.py:28
  3.6 2.1 %collective-permute-start.1 = (bf16[2,32,1536]{2,1,0:T(8,128)(2,1)S(1)}, bf16[2,32,1536]{2,1,0:T(8,128)(2,1)S(1)}, u32[]{:S(2)}, u32[]{:S(2)}) collective-permute-start(bf16[2,32,1536]{2,1,0:T(8,128)(2,1)S(1)} %get-tuple-element.25), channel_id=1, source_target_pairs={{2,4},{4,2},{3,5},{5,3},{10,12},{12,10},{11,13},{13,11},{18,20},{2... | collective-permute-start | bytes 589832 | tf_op jit(solution)/shard_map/ppermute | solution.py:28
  5.7 2.5 %collective-permute-done.refs_0_.refs_1_.rest_1_ = bf16[2,32,1536]{2,1,0:T(8,128)(2,1)S(1)} collective-permute-done((bf16[2,32,1536]{2,1,0:T(8,128)(2,1)S(1)}, bf16[2,32,1536]{2,1,0:T(8,128)(2,1)S(1)}, u32[]{:S(2)}, u32[]{:S(2)}) %collective-permute-start) | collective-permute-done | bytes 196640 | tf_op jit(solution)/shard_map/ppermute | solution.py:28
  8.1 4.0 %collective-permute-done.1.refs_1_.refs_2_.rest_2_ = bf16[2,32,1536]{2,1,0:T(8,128)(2,1)S(1)} collective-permute-done((bf16[2,32,1536]{2,1,0:T(8,128)(2,1)S(1)}, bf16[2,32,1536]{2,1,0:T(8,128)(2,1)S(1)}, u32[]{:S(2)}, u32[]{:S(2)}) %collective-permute-start.1) | collective-permute-done | bytes 196640 | tf_op jit(solution)/shard_map/ppermute | solution.py:28
  12.2 0.1 kv_time.1
  12.3 1.4 %collective-permute-start.2 = (bf16[2,48,1536]{2,1,0:T(8,128)(2,1)S(1)}, bf16[2,48,1536]{2,1,0:T(8,128)(2,1)S(1)}, u32[]{:S(2)}, u32[]{:S(2)}) collective-permute-start(bf16[2,48,1536]{2,1,0:T(8,128)(2,1)S(1)} %get-tuple-element.26), channel_id=1, source_target_pairs={{0,8},{8,0},{16,24},{24,16},{1,9},{9,1},{17,25},{25,17},{2,10},{10... | collective-permute-start | bytes 884744 | tf_op jit(solution)/shard_map/ppermute | solution.py:28
  13.6 1.9 %collective-permute-start.3 = (bf16[2,48,1536]{2,1,0:T(8,128)(2,1)S(1)}, bf16[2,48,1536]{2,1,0:T(8,128)(2,1)S(1)}, u32[]{:S(2)}, u32[]{:S(2)}) collective-permute-start(bf16[2,48,1536]{2,1,0:T(8,128)(2,1)S(1)} %get-tuple-element.27), channel_id=1, source_target_pairs={{8,16},{16,8},{9,17},{17,9},{10,18},{18,10},{11,19},{19,11},{12,20... | collective-permute-start | bytes 884744 | tf_op jit(solution)/shard_map/ppermute | solution.py:28
  15.5 3.7 %collective-permute-done.2.refs_3_.rest_3_ = bf16[2,48,1536]{2,1,0:T(8,128)(2,1)S(1)} collective-permute-done((bf16[2,48,1536]{2,1,0:T(8,128)(2,1)S(1)}, bf16[2,48,1536]{2,1,0:T(8,128)(2,1)S(1)}, u32[]{:S(2)}, u32[]{:S(2)}) %collective-permute-start.2) | collective-permute-done | bytes 294944 | tf_op jit(solution)/shard_map/ppermute | solution.py:28
  19.2 2.9 %collective-permute-done.3.refs_4_.rest_4_ = bf16[2,48,1536]{2,1,0:T(8,128)(2,1)S(1)} collective-permute-done((bf16[2,48,1536]{2,1,0:T(8,128)(2,1)S(1)}, bf16[2,48,1536]{2,1,0:T(8,128)(2,1)S(1)}, u32[]{:S(2)}, u32[]{:S(2)}) %collective-permute-start.3) | collective-permute-done | bytes 294944 | tf_op jit(solution)/shard_map/ppermute | solution.py:28
  22.1 1.0 %kv_column.1 = bf16[2,144,1536]{2,1,0:T(8,128)(2,1)} custom-call(bf16[2,128,1536]{2,1,0:T(8,128)(2,1)S(1)} %get-tuple-element.23.own_ref.refs_0_.rest_0_.kv_ref, bf16[2,32,1536]{2,1,0:T(8,128)(2,1)S(1)} %collective-permute-done.refs_0_.refs_1_.rest_1_, bf16[2,32,1536]{2,1,0:T(8,128)(2,1)S(1)} %collective-permute-done.1.refs_1_.refs_2_.rest_2_, ...), custom_call_target="tpu_custom_call" | custom-call | tf_op jit(solution)/shard_map/kv_column/pallas_call | solution.py:113
  23.1 2.8 %collective-permute-start.4 = (bf16[2,144,1536]{2,1,0:T(8,128)(2,1)}, bf16[2,144,1536]{2,1,0:T(8,128)(2,1)}, u32[]{:S(2)}, u32[]{:S(2)}) collective-permute-start(bf16[2,144,1536]{2,1,0:T(8,128)(2,1)} %kv_column.1), channel_id=1, source_target_pairs={{0,1},{1,0},{2,3},{3,2},{4,5},{5,4},{6,7},{7,6},{8,9},{9,8},{10,11... | collective-permute-start | bytes 2654216 | tf_op jit(solution)/shard_map/ppermute | solution.py:28
  25.9 0.0 collective-permute-start.5
  25.9 4.2 %collective-permute-start.6 = (bf16[2,32,1536]{2,1,0:T(8,128)(2,1)S(1)}, bf16[2,32,1536]{2,1,0:T(8,128)(2,1)S(1)}, u32[]{:S(2)}, u32[]{:S(2)}) collective-permute-start(bf16[2,32,1536]{2,1,0:T(8,128)(2,1)S(1)} %get-tuple-element.31), channel_id=1, source_target_pairs={{2,4},{4,2},{3,5},{5,3},{10,12},{12,10},{11,13},{13,11},{18,20},{2... | collective-permute-start | bytes 589832 | tf_op jit(solution)/shard_map/ppermute | solution.py:28
  30.1 2.3 %collective-permute-done.5.refs_0_.refs_1_.rest_1_ = bf16[2,32,1536]{2,1,0:T(8,128)(2,1)S(1)} collective-permute-done((bf16[2,32,1536]{2,1,0:T(8,128)(2,1)S(1)}, bf16[2,32,1536]{2,1,0:T(8,128)(2,1)S(1)}, u32[]{:S(2)}, u32[]{:S(2)}) %collective-permute-start.5) | collective-permute-done | bytes 196640 | tf_op jit(solution)/shard_map/ppermute | solution.py:28
  32.4 5.3 %collective-permute-done.6.refs_1_.refs_2_.rest_2_ = bf16[2,32,1536]{2,1,0:T(8,128)(2,1)S(1)} collective-permute-done((bf16[2,32,1536]{2,1,0:T(8,128)(2,1)S(1)}, bf16[2,32,1536]{2,1,0:T(8,128)(2,1)S(1)}, u32[]{:S(2)}, u32[]{:S(2)}) %collective-permute-start.6) | collective-permute-done | bytes 196640 | tf_op jit(solution)/shard_map/ppermute | solution.py:28
  37.7 0.9 %qd_time.1 = (bf16[2,48,1536]{2,1,0:T(8,128)(2,1)}, bf16[2,48,1536]{2,1,0:T(8,128)(2,1)}) custom-call(bf16[2,128,1536]{2,1,0:T(8,128)(2,1)S(1)} %get-tuple-element.22.qd_ref.own_ref.refs_0_.rest_0_, bf16[2,32,1536]{2,1,0:T(8,128)(2,1)S(1)} %collective-permute-done.5.refs_0_.refs_1_.rest_1_, ...), custom_call_target="tpu_custom_call" | custom-call | tf_op jit(solution)/shard_map/qd_time/pallas_call | solution.py:113
  38.6 0.0 collective-permute-start.7
  38.6 1.9 %collective-permute-start.8 = (bf16[2,48,1536]{2,1,0:T(8,128)(2,1)}, bf16[2,48,1536]{2,1,0:T(8,128)(2,1)S(1)}, u32[]{:S(2)}, u32[]{:S(2)}) collective-permute-start(bf16[2,48,1536]{2,1,0:T(8,128)(2,1)} %get-tuple-element.33), channel_id=1, source_target_pairs={{8,16},{16,8},{9,17},{17,9},{10,18},{18,10},{11,19},{19,11},{12,20... | collective-permute-start | bytes 884744 | tf_op jit(solution)/shard_map/ppermute | solution.py:28
  40.5 1.3 %codes.1 = (s32[128,512]{1,0:T(8,128)S(1)}, s32[128,512]{1,0:T(8,128)S(1)}, s32[8,12]{1,0:T(8,128)S(1)}) custom-call(s32[128,8]{1,0:T(8,128)} %constant.25.clone.refs_0_, s32[8,512]{1,0:T(8,128)} %constant.26.clone.refs_1_, s32[16,4,16]{2,1,0:T(4,128)} %bitcast.102, s32[3,12]{1,0:T(4,128)} %bitcast.107), custom_call_target="tpu_custom_call" | custom-call | tf_op jit(solution)/shard_map/codes/pallas_call | solution.py:113
  41.8 5.0 %collective-permute-done.7.refs_3_.rest_3_ = bf16[2,48,1536]{2,1,0:T(8,128)(2,1)S(1)} collective-permute-done((bf16[2,48,1536]{2,1,0:T(8,128)(2,1)}, bf16[2,48,1536]{2,1,0:T(8,128)(2,1)S(1)}, u32[]{:S(2)}, u32[]{:S(2)}) %collective-permute-start.7) | collective-permute-done | bytes 294944 | tf_op jit(solution)/shard_map/ppermute | solution.py:28
  46.8 1.9 %collective-permute-done.8.refs_4_.rest_4_ = bf16[2,48,1536]{2,1,0:T(8,128)(2,1)S(1)} collective-permute-done((bf16[2,48,1536]{2,1,0:T(8,128)(2,1)}, bf16[2,48,1536]{2,1,0:T(8,128)(2,1)S(1)}, u32[]{:S(2)}, u32[]{:S(2)}) %collective-permute-start.8) | collective-permute-done | bytes 294944 | tf_op jit(solution)/shard_map/ppermute | solution.py:28
  48.6 0.1 qd_column.1
  48.7 1.5 %collective-permute-start.9 = (bf16[2,144,1536]{2,1,0:T(8,128)(2,1)S(1)}, bf16[2,144,1536]{2,1,0:T(8,128)(2,1)S(1)}, u32[]{:S(2)}, u32[]{:S(2)}) collective-permute-start(bf16[2,144,1536]{2,1,0:T(8,128)(2,1)S(1)} %qd_column.1), channel_id=1, source_target_pairs={{0,1},{1,0},{2,3},{3,2},{4,5},{5,4},{6,7},{7,6},{8,9},{9,8},{10,11... | collective-permute-start | bytes 2654216 | tf_op jit(solution)/shard_map/ppermute | solution.py:28
  50.2 0.0 collective-permute-done.4.rest_5_
  50.2 5.3 %query_side.1 = (bf16[4,4,2,4,1536]{4,3,2,1,0:T(4,128)(2,1)}, f32[128,128]{1,0:T(8,128)S(1)}) custom-call(s32[8,12]{1,0:T(8,128)S(1)} %get-tuple-element.20.closed_ref, s32[128,512]{1,0:T(8,128)S(1)} %get-tuple-element.21.code_ref, bf16[2,128,1536]{2,1,0:T(8,128)(2,1)S(1)} %get-tuple-element.22.qd_ref.own_ref.refs_0_.rest_0_, ...), custom_call_target="tpu_custom_call" | custom-call | tf_op jit(solution)/shard_map/query_side/pallas_call | solution.py:113
  55.5 0.1 collective-permute-start.10
  55.6 1.9 %collective-permute-start.11 = (f32[1,32,128]{2,1,0:T(8,128)S(1)}, f32[1,32,128]{2,1,0:T(8,128)S(1)}, u32[]{:S(2)}, u32[]{:S(2)}) collective-permute-start(f32[1,32,128]{2,1,0:T(8,128)S(1)} %bitcast.105), channel_id=1, source_target_pairs={{2,4},{4,2},{3,5},{5,3},{10,12},{12,10},{11,13},{13,11},{18,20},{2... | collective-permute-start | bytes 49160 | tf_op jit(solution)/shard_map/ppermute | solution.py:28
  57.5 0.6 collective-permute-done.10.rest_7_
  58.2 2.8 %collective-permute-done.11.rest_8_ = f32[1,32,128]{2,1,0:T(8,128)S(1)} collective-permute-done((f32[1,32,128]{2,1,0:T(8,128)S(1)}, f32[1,32,128]{2,1,0:T(8,128)S(1)}, u32[]{:S(2)}, u32[]{:S(2)}) %collective-permute-start.11) | collective-permute-done | bytes 16416 | tf_op jit(solution)/shard_map/ppermute | solution.py:28
  61.0 0.1 collective-permute-start.12
  61.1 1.9 %collective-permute-start.13 = (f32[1,48,128]{2,1,0:T(8,128)S(1)}, f32[1,48,128]{2,1,0:T(8,128)S(1)}, u32[]{:S(2)}, u32[]{:S(2)}) collective-permute-start(f32[1,48,128]{2,1,0:T(8,128)S(1)} %bitcast.103), channel_id=1, source_target_pairs={{8,16},{16,8},{9,17},{17,9},{10,18},{18,10},{11,19},{19,11},{12,20... | collective-permute-start | bytes 73736 | tf_op jit(solution)/shard_map/ppermute | solution.py:28
  63.0 0.7 collective-permute-done.12.rest_9_
  63.7 1.9 %collective-permute-done.13.rest_10_ = f32[1,48,128]{2,1,0:T(8,128)S(1)} collective-permute-done((f32[1,48,128]{2,1,0:T(8,128)S(1)}, f32[1,48,128]{2,1,0:T(8,128)S(1)}, u32[]{:S(2)}, u32[]{:S(2)}) %collective-permute-start.13) | collective-permute-done | bytes 24608 | tf_op jit(solution)/shard_map/ppermute | solution.py:28
  65.7 2.4 %collective-permute-start.14 = (f32[1,144,128]{2,1,0:T(8,128)S(1)}, f32[1,144,128]{2,1,0:T(8,128)S(1)}, u32[]{:S(2)}, u32[]{:S(2)}) collective-permute-start(f32[1,144,128]{2,1,0:T(8,128)S(1)} %broadcast_select_fusion), channel_id=1, source_target_pairs={{0,1},{1,0},{2,3},{3,2},{4,5},{5,4},{6,7},{7,6},{8,9},{9,8},{10,11... | collective-permute-start | bytes 221192 | tf_op jit(solution)/shard_map/ppermute | solution.py:28
  68.0 0.0 collective-permute-done.9.rest_5_
  68.0 0.9 %collective-permute-done.14.rest_11_ = f32[1,144,128]{2,1,0:T(8,128)S(1)} collective-permute-done((f32[1,144,128]{2,1,0:T(8,128)S(1)}, f32[1,144,128]{2,1,0:T(8,128)S(1)}, u32[]{:S(2)}, u32[]{:S(2)}) %collective-permute-start.14) | collective-permute-done | bytes 73760 | tf_op jit(solution)/shard_map/ppermute | solution.py:28
  68.9 3.9 %key_side.1 = (bf16[4,4,2,4,1536]{4,3,2,1,0:T(4,128)(2,1)}, bf16[4,4,2,4,1536]{4,3,2,1,0:T(4,128)(2,1)}) custom-call(s32[8,12]{1,0:T(8,128)S(1)} %get-tuple-element.20.closed_ref, s32[128,512]{1,0:T(8,128)S(1)} %get-tuple-element.29.code_ref, bf16[2,128,1536]{2,1,0:T(8,128)(2,1)S(1)} %get-tuple-element.23.own_ref.refs_0_.rest_0_.kv_ref, ...), custom_call_target="tpu_custom_call" | custom-call | tf_op jit(solution)/shard_map/key_side/pallas_call | solution.py:113
  (11 shorter events, 0.1 us)
Async XLA Ops:
  2.3 5.9 %collective-permute-start = (bf16[2,32,1536]{2,1,0:T(8,128)(2,1)S(1)}, bf16[2,32,1536]{2,1,0:T(8,128)(2,1)S(1)}, u32[]{:S(2)}, u32[]{:S(2)}) collective-permute-start(bf16[2,32,1536]{2,1,0:T(8,128)(2,1)S(1)} %get-tuple-element.24), channel_id=1, source_target_pairs={{0,2},{2,0},{4,6},{6,4},{1,3},{3,1},{5,7},{7,5},{8,10},{10,8},{12,... | collective-permute-start | bytes 589832 | tf_op jit(solution)/shard_map/ppermute | solution.py:28
  3.6 8.6 %collective-permute-start.1 = (bf16[2,32,1536]{2,1,0:T(8,128)(2,1)S(1)}, bf16[2,32,1536]{2,1,0:T(8,128)(2,1)S(1)}, u32[]{:S(2)}, u32[]{:S(2)}) collective-permute-start(bf16[2,32,1536]{2,1,0:T(8,128)(2,1)S(1)} %get-tuple-element.25), channel_id=1, source_target_pairs={{2,4},{4,2},{3,5},{5,3},{10,12},{12,10},{11,13},{13,11},{18,20},{2... | collective-permute-start | bytes 589832 | tf_op jit(solution)/shard_map/ppermute | solution.py:28
  12.3 7.0 %collective-permute-start.2 = (bf16[2,48,1536]{2,1,0:T(8,128)(2,1)S(1)}, bf16[2,48,1536]{2,1,0:T(8,128)(2,1)S(1)}, u32[]{:S(2)}, u32[]{:S(2)}) collective-permute-start(bf16[2,48,1536]{2,1,0:T(8,128)(2,1)S(1)} %get-tuple-element.26), channel_id=1, source_target_pairs={{0,8},{8,0},{16,24},{24,16},{1,9},{9,1},{17,25},{25,17},{2,10},{10... | collective-permute-start | bytes 884744 | tf_op jit(solution)/shard_map/ppermute | solution.py:28
  13.6 8.5 %collective-permute-start.3 = (bf16[2,48,1536]{2,1,0:T(8,128)(2,1)S(1)}, bf16[2,48,1536]{2,1,0:T(8,128)(2,1)S(1)}, u32[]{:S(2)}, u32[]{:S(2)}) collective-permute-start(bf16[2,48,1536]{2,1,0:T(8,128)(2,1)S(1)} %get-tuple-element.27), channel_id=1, source_target_pairs={{8,16},{16,8},{9,17},{17,9},{10,18},{18,10},{11,19},{19,11},{12,20... | collective-permute-start | bytes 884744 | tf_op jit(solution)/shard_map/ppermute | solution.py:28
  23.1 27.1 %collective-permute-start.4 = (bf16[2,144,1536]{2,1,0:T(8,128)(2,1)}, bf16[2,144,1536]{2,1,0:T(8,128)(2,1)}, u32[]{:S(2)}, u32[]{:S(2)}) collective-permute-start(bf16[2,144,1536]{2,1,0:T(8,128)(2,1)} %kv_column.1), channel_id=1, source_target_pairs={{0,1},{1,0},{2,3},{3,2},{4,5},{5,4},{6,7},{7,6},{8,9},{9,8},{10,11... | collective-permute-start | bytes 2654216 | tf_op jit(solution)/shard_map/ppermute | solution.py:28
  25.9 6.5 %collective-permute-start.5 = (bf16[2,32,1536]{2,1,0:T(8,128)(2,1)S(1)}, bf16[2,32,1536]{2,1,0:T(8,128)(2,1)S(1)}, u32[]{:S(2)}, u32[]{:S(2)}) collective-permute-start(bf16[2,32,1536]{2,1,0:T(8,128)(2,1)S(1)} %get-tuple-element.30), channel_id=1, source_target_pairs={{0,2},{2,0},{4,6},{6,4},{1,3},{3,1},{5,7},{7,5},{8,10},{10,8},{12,... | collective-permute-start | bytes 589832 | tf_op jit(solution)/shard_map/ppermute | solution.py:28
  25.9 11.8 %collective-permute-start.6 = (bf16[2,32,1536]{2,1,0:T(8,128)(2,1)S(1)}, bf16[2,32,1536]{2,1,0:T(8,128)(2,1)S(1)}, u32[]{:S(2)}, u32[]{:S(2)}) collective-permute-start(bf16[2,32,1536]{2,1,0:T(8,128)(2,1)S(1)} %get-tuple-element.31), channel_id=1, source_target_pairs={{2,4},{4,2},{3,5},{5,3},{10,12},{12,10},{11,13},{13,11},{18,20},{2... | collective-permute-start | bytes 589832 | tf_op jit(solution)/shard_map/ppermute | solution.py:28
  38.6 8.2 %collective-permute-start.7 = (bf16[2,48,1536]{2,1,0:T(8,128)(2,1)}, bf16[2,48,1536]{2,1,0:T(8,128)(2,1)S(1)}, u32[]{:S(2)}, u32[]{:S(2)}) collective-permute-start(bf16[2,48,1536]{2,1,0:T(8,128)(2,1)} %get-tuple-element.32), channel_id=1, source_target_pairs={{0,8},{8,0},{16,24},{24,16},{1,9},{9,1},{17,25},{25,17},{2,10},{10... | collective-permute-start | bytes 884744 | tf_op jit(solution)/shard_map/ppermute | solution.py:28
  38.6 10.1 %collective-permute-start.8 = (bf16[2,48,1536]{2,1,0:T(8,128)(2,1)}, bf16[2,48,1536]{2,1,0:T(8,128)(2,1)S(1)}, u32[]{:S(2)}, u32[]{:S(2)}) collective-permute-start(bf16[2,48,1536]{2,1,0:T(8,128)(2,1)} %get-tuple-element.33), channel_id=1, source_target_pairs={{8,16},{16,8},{9,17},{17,9},{10,18},{18,10},{11,19},{19,11},{12,20... | collective-permute-start | bytes 884744 | tf_op jit(solution)/shard_map/ppermute | solution.py:28
  48.7 19.3 %collective-permute-start.9 = (bf16[2,144,1536]{2,1,0:T(8,128)(2,1)S(1)}, bf16[2,144,1536]{2,1,0:T(8,128)(2,1)S(1)}, u32[]{:S(2)}, u32[]{:S(2)}) collective-permute-start(bf16[2,144,1536]{2,1,0:T(8,128)(2,1)S(1)} %qd_column.1), channel_id=1, source_target_pairs={{0,1},{1,0},{2,3},{3,2},{4,5},{5,4},{6,7},{7,6},{8,9},{9,8},{10,11... | collective-permute-start | bytes 2654216 | tf_op jit(solution)/shard_map/ppermute | solution.py:28
  55.5 2.7 %collective-permute-start.10 = (f32[1,32,128]{2,1,0:T(8,128)S(1)}, f32[1,32,128]{2,1,0:T(8,128)S(1)}, u32[]{:S(2)}, u32[]{:S(2)}) collective-permute-start(f32[1,32,128]{2,1,0:T(8,128)S(1)} %bitcast.106), channel_id=1, source_target_pairs={{0,2},{2,0},{4,6},{6,4},{1,3},{3,1},{5,7},{7,5},{8,10},{10,8},{12,... | collective-permute-start | bytes 49160 | tf_op jit(solution)/shard_map/ppermute | solution.py:28
  55.6 5.4 %collective-permute-start.11 = (f32[1,32,128]{2,1,0:T(8,128)S(1)}, f32[1,32,128]{2,1,0:T(8,128)S(1)}, u32[]{:S(2)}, u32[]{:S(2)}) collective-permute-start(f32[1,32,128]{2,1,0:T(8,128)S(1)} %bitcast.105), channel_id=1, source_target_pairs={{2,4},{4,2},{3,5},{5,3},{10,12},{12,10},{11,13},{13,11},{18,20},{2... | collective-permute-start | bytes 49160 | tf_op jit(solution)/shard_map/ppermute | solution.py:28
  61.0 2.7 %collective-permute-start.12 = (f32[1,48,128]{2,1,0:T(8,128)S(1)}, f32[1,48,128]{2,1,0:T(8,128)S(1)}, u32[]{:S(2)}, u32[]{:S(2)}) collective-permute-start(f32[1,48,128]{2,1,0:T(8,128)S(1)} %bitcast.104), channel_id=1, source_target_pairs={{0,8},{8,0},{16,24},{24,16},{1,9},{9,1},{17,25},{25,17},{2,10},{10... | collective-permute-start | bytes 73736 | tf_op jit(solution)/shard_map/ppermute | solution.py:28
  61.1 4.6 %collective-permute-start.13 = (f32[1,48,128]{2,1,0:T(8,128)S(1)}, f32[1,48,128]{2,1,0:T(8,128)S(1)}, u32[]{:S(2)}, u32[]{:S(2)}) collective-permute-start(f32[1,48,128]{2,1,0:T(8,128)S(1)} %bitcast.103), channel_id=1, source_target_pairs={{8,16},{16,8},{9,17},{17,9},{10,18},{18,10},{11,19},{19,11},{12,20... | collective-permute-start | bytes 73736 | tf_op jit(solution)/shard_map/ppermute | solution.py:28
  65.7 3.3 %collective-permute-start.14 = (f32[1,144,128]{2,1,0:T(8,128)S(1)}, f32[1,144,128]{2,1,0:T(8,128)S(1)}, u32[]{:S(2)}, u32[]{:S(2)}) collective-permute-start(f32[1,144,128]{2,1,0:T(8,128)S(1)} %broadcast_select_fusion), channel_id=1, source_target_pairs={{0,1},{1,0},{2,3},{3,2},{4,5},{5,4},{6,7},{7,6},{8,9},{9,8},{10,11... | collective-permute-start | bytes 221192 | tf_op jit(solution)/shard_map/ppermute | solution.py:28

commit v3 on v2

v3 whole, which is shorter than its diff:
```python
import functools
import math

import jax
import jax.numpy as jnp
import numpy as np
from jax import lax
from jax.experimental import pallas as pl
from jax.experimental.pallas import tpu as pltpu
from jax.sharding import PartitionSpec as P


NEG = -1e30
LOG2E = 1.4426950408889634
EVEN, ODD = 1000, 1001
AXES = ("ta", "ha", "wa")


def matchings(n):
    even = [(i, i ^ 1) for i in range(n) if (i ^ 1) < n]
    odd = [(i, ((i + 1) ^ 1) - 1) for i in range(n) if 0 <= ((i + 1) ^ 1) - 1 < n]
    return [m for m in (even, odd) if m]


def swap(axis, sends):
    got = []
    for k, pairs in enumerate(matchings(lax.axis_size(axis))):
        got.append(lax.ppermute(sends[k], axis, pairs))
    return got


def sent_layer(axis, k, length):
    odd = lax.rem(lax.axis_index(axis), 2)
    return (1 - odd if k == 0 else odd) * (length - 1)


def by_parity(axis, count, length, put):
    odd = lax.rem(lax.axis_index(axis), 2)

    @pl.when(odd == 0)
    def _():
        for k in range(count):
            put(k, length - 1 if k == 0 else 0)

    @pl.when(odd == 1)
    def _():
        for k in range(count):
            put(k, 0 if k == 0 else length - 1)


def prepare_kernel(block, axis, count, *refs):
    T, H, W, C = block
    args, faces, (whole, buf, sems) = refs[:2], refs[2 : 2 + count], refs[2 + count :]
    copies = [
        [pltpu.make_async_copy(args[a].at[t], buf.at[a, t], sems.at[a, t]) for t in range(T)]
        for a in range(2)
    ]
    for a in range(2):
        for copy in copies[a]:
            copy.start()
    width = buf.shape[-1]
    for a in range(2):
        for copy in copies[a]:
            copy.wait()
        for w in range(W):
            for t in range(T):
                r = (w * T + t) * H * C
                whole[a, r : r + H * C, :] = buf[a, t, :, w].reshape(H * C, width)
            for k in range(count):
                n = faces[k].shape[1] // W
                if axis == "ha":
                    layer = buf[a, :, sent_layer(axis, k, H), w]
                else:
                    layer = buf[a, sent_layer(axis, k, T), :, w]
                faces[k][a, w * n : (w + 1) * n, :] = layer.reshape(n, width)


def second_kernel(block, axis, near, count, own_ref, *refs):
    T, H, W, C = block
    got, outs = refs[:near], refs[near:]

    def put(k, layer):
        for a in range(own_ref.shape[0]):
            for w in range(W):
                if axis == "ta":
                    r = (w * T + layer) * H * C
                    parts = [own_ref[a, r : r + H * C, :]]
                    at = (w * T + layer) * C
                else:
                    parts = []
                    for t in range(T):
                        r = ((w * T + t) * H + layer) * C
                        parts.append(own_ref[a, r : r + C, :])
                    at = (w * H + layer) * C
                parts += [r[a, at : at + C, :] for r in got]
                n = outs[k].shape[1] // W
                outs[k][a, w * n : (w + 1) * n, :] = jnp.concatenate(parts, axis=0)

    by_parity(axis, count, T if axis == "ta" else H, put)


def column_kernel(block, count, *refs):
    _, _, W, _ = block
    pieces, outs = refs[: len(refs) - count], refs[len(refs) - count :]

    def put(k, w):
        for a in range(outs[k].shape[0]):
            at = 0
            for r in pieces:
                n = r.shape[1] // W
                outs[k][a, at : at + n, :] = r[a, w * n : (w + 1) * n, :]
                at += n

    by_parity("wa", count, W, put)


def local(kernel, out_shape, operands, space=pltpu.VMEM, **kw):
    place = pl.BlockSpec(memory_space=space)
    return pl.pallas_call(
        kernel,
        out_shape=out_shape,
        in_specs=[place] * len(operands),
        out_specs=[pl.BlockSpec(memory_space=pltpu.VMEM)] * len(out_shape),
        compiler_params=pltpu.CompilerParams(vmem_limit_bytes=16 << 20),
        **kw,
    )(*operands)


def spread(own, got, axis, block, counts, name):
    T, H, W, C = block
    k, _, width = own.shape
    near, count, length = (counts[1], counts[0], H) if axis == "ta" else (counts[0], counts[1], T)
    more = swap(
        axis,
        local(
            functools.partial(second_kernel, block, axis, near, count),
            [pltpu.VMEM((k, W * (length + near) * C, width), own.dtype)] * count,
            [own] + got,
            name=name + "_second",
        ),
    )
    columns = []
    for part, pieces in (("near", [own] + got), ("far", more)):
        n = sum(p.shape[1] for p in pieces) // W
        sends = local(
            functools.partial(column_kernel, block, counts[2]),
            [pltpu.VMEM((k, n, width), own.dtype)] * counts[2],
            pieces,
            name=f"{name}_{part}",
        )
        columns += swap("wa", sends)
    return got + more + columns


def piece_coords(block, counts, second):
    T, H, W, C = block
    marks = [(EVEN, ODD)[:n] for n in counts]
    ts, hs = list(range(T)), list(range(H))
    own = [[[(t, h, w) for h in hs] for t in ts] for w in range(W)]
    pieces = [np.array(own, np.int32).reshape(W, -1, 3)]
    if second == "ta":
        for m in marks[1]:
            pieces.append(np.array([[(t, m, w) for t in ts] for w in range(W)], np.int32))
        for m in marks[0]:
            line = hs + list(marks[1])
            pieces.append(np.array([[(m, h, w) for h in line] for w in range(W)], np.int32))
    else:
        for m in marks[0]:
            pieces.append(np.array([[(m, h, w) for h in hs] for w in range(W)], np.int32))
        for m in marks[1]:
            line = ts + list(marks[0])
            pieces.append(np.array([[(t, m, w) for t in line] for w in range(W)], np.int32))
    out = [p.reshape(-1, 3) for p in pieces]
    near = 1 + len(marks[1] if second == "ta" else marks[0])
    for part in (pieces[:near], pieces[near:]):
        for m in marks[2]:
            c = np.concatenate([p[0] for p in part], axis=0)
            c[:, 2] = m
            out.append(c)
    return np.repeat(np.concatenate(out, axis=0), C, axis=0)


def codes_kernel(block, grids, *refs):
    sources, outs, bufs, sems = refs[:5], refs[5:8], refs[8:13], refs[13]
    copies = [pltpu.make_async_copy(s, b, sems.at[i]) for i, (s, b) in enumerate(zip(sources, bufs))]
    for copy in copies:
        copy.start()
    for copy in copies:
        copy.wait()
    oc_ref, kc_ref, qc_ref, valid_ref, radius_ref = bufs
    query_ref, key_ref, closed_ref = outs
    r = radius_ref[...]
    closed = 8 + (1 - r[0:1]) + 2 * (1 - r[1:2]) + 4 * (1 - r[2:3])
    closed_ref[...] = jnp.broadcast_to(closed, closed_ref.shape)
    for outer_ref, code_ref, own_is_key in ((kc_ref, query_ref, False), (qc_ref, key_ref, True)):
        code = same = bad = 0
        for a, axis in enumerate(AXES):
            length, grid = block[a], grids[a]

            def line(i):
                i = i % grid
                if a == 0:
                    return valid_ref[i, 1:2, 1:2]
                if a == 1:
                    return valid_ref[1, 1:2, i : i + 1]
                return valid_ref[1, i : i + 1, 1:2]

            low = 1 - line(0)
            high = grid - 3 + line(-1) + line(-2)
            index = lax.axis_index(axis)
            odd = lax.rem(index, 2)
            at_even = jnp.where(odd == 1, -1, length)
            at_odd = jnp.where(odd == 1, length, -1)
            own = oc_ref[:, a : a + 1]
            outer = outer_ref[a : a + 1, :]
            outer = jnp.where(outer == EVEN, at_even, jnp.where(outer == ODD, at_odd, outer))
            place = outer + index * length
            outside = jnp.where((place >= 0) & (place < grid), 0, 8)
            apart = jnp.abs(own - outer)
            same = same | apart
            code = code | jnp.where(apart > 1, 8, apart << a) | outside
            key = own + index * length if own_is_key else place
            bad = bad | jnp.where((key >= low) & (key <= high), 0, 8)
        code_ref[...] = code | jnp.where(same == 0, 0, bad)


NT = (((1,), (1,)), ((), ()))
NN = (((1,), (0,)), ((), ()))


def dot(a, b, dims):
    return lax.dot_general(a, b, dims, preferred_element_type=jnp.float32)


def gather(refs, which, cols, pad):
    parts = [r[which, :, cols] for r in refs]
    if pad:
        parts.append(jnp.zeros((pad, parts[0].shape[1]), parts[0].dtype))
    return jnp.concatenate(parts, axis=0)


def put_tiles(ref, value, cols):
    T, H, W, C, _ = ref.shape
    value = value.astype(ref.dtype)
    for w in range(W):
        for t in range(T):
            r = (w * T + t) * H * C
            ref[t, :, w, :, cols] = value[r : r + H * C].reshape(H, C, value.shape[1])


def query_kernel(cfg, block, faces, closed_ref, code_ref, qd_ref, *rest):
    heads, depth, pad, count = cfg
    kv = rest[:count]
    dq_ref, stat_ref = rest[count : count + 2]
    first_refs = rest[count + 2 : count + 2 + faces]
    s_ref, g_ref, d_ref = rest[count + 2 + faces :]
    scale = 1.0 / math.sqrt(depth)
    rows = qd_ref.shape[1]
    step = math.gcd(rows, 32)
    stat_ref[...] = jnp.zeros(stat_ref.shape, jnp.float32)

    def columns(h):
        return slice(h * depth, (h + 1) * depth)

    def products(h):
        cols = columns(h)
        s_ref[h % 2] = dot(qd_ref[0, :, cols], gather(kv, 0, cols, pad), NT)
        g_ref[h % 2] = dot(qd_ref[1, :, cols], gather(kv, 1, cols, pad), NT)

    products(0)
    for h in range(heads):
        if h + 1 < heads:
            products(h + 1)
        ratios = []
        for r in range(0, rows, step):
            band = slice(r, r + step)
            allowed = (code_ref[band, :] & closed_ref[0:1, h : h + 1]) == 0
            scores = jnp.where(allowed, s_ref[h % 2, band, :], NEG)
            peak = jnp.max(scores, axis=1, keepdims=True)
            raised = jnp.exp2((scores - peak) * (scale * LOG2E))
            total = jnp.sum(raised, axis=1, keepdims=True)
            grads = g_ref[h % 2, band, :]
            drift = jnp.sum(raised * grads, axis=1, keepdims=True) / total
            d_ref[h % 2, band, :] = (raised * (grads - drift)).astype(jnp.bfloat16)
            stat_ref[0, band, h : h + 1] = peak * (scale * LOG2E) + jnp.log2(total)
            stat_ref[0, band, heads + h : heads + h + 1] = drift
            ratios.append(scale / total)
        cols = columns(h)
        product = dot(d_ref[h % 2], gather(kv, 0, cols, pad), NN)
        put_tiles(dq_ref, product * jnp.concatenate(ratios, axis=0), cols)
    T, H, W, C = block

    def put(k, t):
        for w in range(W):
            r = (w * T + t) * H * C
            first_refs[k][0, w * H * C : (w + 1) * H * C, :] = stat_ref[0, r : r + H * C, :]

    by_parity("ta", faces, T, put)


def key_products_kernel(cfg, begin, closed_ref, code_ref, kv_ref, *rest):
    _, depth, pad, count = cfg
    qd, (s_ref, g_ref) = rest[:count], rest[count:]
    scale = 1.0 / math.sqrt(depth)
    for i in range(s_ref.shape[0]):
        h = begin + i
        cols = slice(h * depth, (h + 1) * depth)
        allowed = (code_ref[...] & closed_ref[0:1, h : h + 1]) == 0
        scores = dot(kv_ref[0, :, cols], gather(qd, 0, cols, pad), NT) * (scale * LOG2E)
        s_ref[i] = jnp.where(allowed, scores, NEG)
        g_ref[i] = dot(kv_ref[1, :, cols], gather(qd, 1, cols, pad), NT)


def key_kernel(cfg, parts, *refs):
    heads, depth, pad, count = cfg
    products, refs = refs[: 2 * parts], refs[2 * parts :]
    qd, st = refs[:count], refs[count : 2 * count]
    dk_ref, dv_ref, row_ref = refs[2 * count :]
    scale = 1.0 / math.sqrt(depth)
    lines = [r[0] for r in st]
    if pad:
        lines.append(jnp.zeros((pad, lines[0].shape[1]), jnp.float32))
    row_ref[...] = jnp.concatenate(lines, axis=0).T
    each = heads // parts
    for h in range(heads):
        cols = slice(h * depth, (h + 1) * depth)
        s_ref, g_ref = products[2 * (h // each) : 2 * (h // each) + 2]
        attention = jnp.exp2(s_ref[h % each] - row_ref[h : h + 1, :])
        drift = row_ref[heads + h : heads + h + 1, :]
        score_grads = (attention * (g_ref[h % each] - drift)).astype(jnp.bfloat16)
        put_tiles(dk_ref, dot(score_grads, gather(qd, 0, cols, pad), NN) * scale, cols)
        put_tiles(dv_ref, dot(attention.astype(jnp.bfloat16), gather(qd, 1, cols, pad), NN), cols)


def per_device(queries, key_states, value_states, output_cotangent, tile_valid, window_radius):
    T, H, W, C, width = queries.shape
    block = (T, H, W, C)
    heads = window_radius.shape[0]
    depth = width // heads
    sizes = tuple(lax.axis_size(a) for a in AXES)
    grids = tuple(n * b for n, b in zip(sizes, block))
    counts = tuple(len(matchings(n)) for n in sizes)
    rows = T * H * W * C

    kind = jax.ShapeDtypeStruct
    args = [
        pltpu.with_memory_space_constraint(x, pltpu.HBM)
        for x in (key_states, value_states, queries, output_cotangent)
    ]

    def prepared(pair, axis, name):
        a = AXES.index(axis)
        n = W * C * (T if axis == "ha" else H)
        made = local(
            functools.partial(prepare_kernel, block, axis, counts[a]),
            [pltpu.VMEM((2, n, width), jnp.bfloat16)] * counts[a]
            + [pltpu.VMEM((2, rows, width), jnp.bfloat16)],
            pair,
            space=pltpu.HBM,
            scratch_shapes=[
                pltpu.VMEM((2, T, H, W, C, width), jnp.bfloat16),
                pltpu.SemaphoreType.DMA((2, T)),
            ],
            name=name + "_prepare",
        )
        return made[-1], swap(axis, made[:-1])

    kv, kv_ha = prepared(args[:2], "ha", "kv")
    qd, qd_ta = prepared(args[2:], "ta", "qd")
    kv_pieces = [kv] + spread(kv, kv_ha, "ta", block, counts, "kv")
    qd_pieces = [qd] + spread(qd, qd_ta, "ha", block, counts, "qd")

    def table(second):
        coords = piece_coords(block, counts, second)
        total = coords.shape[0]
        padded = -(-total // 128) * 128
        out = np.full((8, padded), -(1 << 20), np.int32)
        out[:3, :total] = coords.T
        inner = np.zeros((rows, 8), np.int32)
        inner[:, :3] = coords[:rows]
        return inner, out, padded - total

    inner, outer_k, pad_k = table("ta")
    _, outer_q, pad_q = table("ha")
    kcfg = (heads, depth, pad_k, len(kv_pieces))
    qcfg = (heads, depth, pad_q, len(qd_pieces))
    wide_k, wide_q = outer_k.shape[1], outer_q.shape[1]
    native = kind(queries.shape, jnp.bfloat16)
    lanes = -(-2 * heads // 128) * 128
    tables = [inner, outer_k, outer_q, tile_valid.transpose(0, 2, 1), window_radius.T]
    query_code, key_code, closed = local(
        functools.partial(codes_kernel, block, grids),
        [
            pltpu.VMEM((rows, wide_k), jnp.int32),
            pltpu.VMEM((rows, wide_q), jnp.int32),
            pltpu.VMEM((8, heads), jnp.int32),
        ],
        [pltpu.with_memory_space_constraint(jnp.asarray(x), pltpu.HBM) for x in tables],
        space=pltpu.HBM,
        scratch_shapes=[pltpu.VMEM(x.shape, jnp.int32) for x in tables]
        + [pltpu.SemaphoreType.DMA((len(tables),))],
        name="codes",
    )

    made = local(
        functools.partial(query_kernel, kcfg, block, counts[0]),
        [native, pltpu.VMEM((1, rows, lanes), jnp.float32)]
        + [pltpu.VMEM((1, W * H * C, lanes), jnp.float32)] * counts[0],
        [closed, query_code, qd] + kv_pieces,
        scratch_shapes=[pltpu.VMEM((2, rows, wide_k), jnp.float32)] * 2
        + [pltpu.VMEM((2, rows, wide_k), jnp.bfloat16)],
        name="query_side",
    )
    query_gradient, stats = made[:2]
    st_ta = swap("ta", made[2:])
    stat_pieces = [stats] + spread(stats, st_ta, "ha", block, counts, "st")
    parts = math.gcd(heads, 2)
    products = []
    for i in range(parts):
        products += local(
            functools.partial(key_products_kernel, qcfg, i * heads // parts),
            [pltpu.VMEM((heads // parts, rows, wide_q), jnp.float32)] * 2,
            [closed, key_code, kv] + qd_pieces,
            name=f"key_products_{i}",
        )
    key_gradient, value_gradient = local(
        functools.partial(key_kernel, qcfg, parts),
        [native, native],
        products + qd_pieces + stat_pieces,
        scratch_shapes=[pltpu.VMEM((lanes, wide_q), jnp.float32)],
        name="key_side",
    )
    return (query_gradient, key_gradient, value_gradient)


def solution(mesh):
    split = P("ta", "ha", "wa", None, None)

    return jax.shard_map(
        per_device,
        mesh=mesh,
        in_specs=(split, split, split, split, P(), P()),
        out_specs=(split, split, split),
        check_vma=False,
    )
```

time: 73.2 us -> 63.9 us (0.87)
  waiting for transfers between devices: 34.5 us -> 15.1 us
  starting transfers between devices: 23.4 us -> 35.1 us
  Pallas kernels: 14.1 us -> 12.5 us
    ppermute x15 -> x18, waiting for transfers between devices: 34.5 us -> 15.1 us  [swap(): got.append(lax.ppermute(sends[k], axis, pairs))]
    ppermute x15 -> x18, starting transfers between devices: 23.4 us -> 35.1 us  [swap(): got.append(lax.ppermute(sends[k], axis, pairs))]
    pallas_call x8 -> x16, Pallas kernels: 14.1 us -> 12.5 us  [local(): pl.pallas_call(kernel, out_shape=out_shape, in_specs=[place] * len(operan...]
  transfers between devices with their start and end apart: 15 -> 18, of which waited for: 13 -> 6; matrix products, arithmetic and copies ran while one was open for 0% -> 0% of each run, Pallas kernels for 10% -> 14%
where the time goes in v3:
time: 63.9 us; the launch traced here: 63.5 us
  starting transfers between devices  35.1 us (55%)
  waiting for transfers between devices  15.1 us (24%)
  Pallas kernels  12.5 us (20%)
  between operations  0.85 us (1%)
    ppermute x18, starting transfers between devices, swap(): got.append(lax.ppermute(sends[k], axis, pairs))  35.1 us
    ppermute x18, waiting for transfers between devices, swap(): got.append(lax.ppermute(sends[k], axis, pairs))  15.1 us
    pallas_call x16, Pallas kernels, local(): pl.pallas_call(kernel, out_shape=out_shape, in_specs=[place] * len(operan...  12.5 us
  transfers between devices with their start and end apart: 18, of which 6 were waited for; matrix products, arithmetic and copies ran while one was open for 0% of the time, Pallas kernels for 14%

profile of v3, /device:TPU:21, one launch (start us, length us, event | category | flops | bytes accessed | tf_op | source)
XLA Modules:
  0.0 63.5 jit_solution(14203557013701799999)
XLA Ops:
  0.6 1.3 %kv_prepare.1 = (bf16[2,32,1536]{2,1,0:T(8,128)(2,1)S(1)}, bf16[2,32,1536]{2,1,0:T(8,128)(2,1)S(1)}, bf16[2,128,1536]{2,1,0:T(8,128)(2,1)S(1)}) custom-call(bf16[4,4,2,4,1536]{4,3,2,1,0:T(4,128)(2,1)} %refs_0_.4, bf16[4,4,2,4,1536]{4,3,2,1,0:T(4,128)(2,1)} %refs_1_.4), custom_call_target="tpu_custom_call" | custom-call | tf_op jit(solution)/shard_map/kv_prepare/pallas_call | solution.py:119
  2.0 1.3 %collective-permute-start = (bf16[2,32,1536]{2,1,0:T(8,128)(2,1)S(1)}, bf16[2,32,1536]{2,1,0:T(8,128)(2,1)S(1)}, u32[]{:S(2)}, u32[]{:S(2)}) collective-permute-start(bf16[2,32,1536]{2,1,0:T(8,128)(2,1)S(1)} %get-tuple-element.32), channel_id=1, source_target_pairs={{0,2},{2,0},{4,6},{6,4},{1,3},{3,1},{5,7},{7,5},{8,10},{10,8},{12,... | collective-permute-start | bytes 589832 | tf_op jit(solution)/shard_map/ppermute | solution.py:28
  3.3 2.1 %collective-permute-start.1 = (bf16[2,32,1536]{2,1,0:T(8,128)(2,1)S(1)}, bf16[2,32,1536]{2,1,0:T(8,128)(2,1)S(1)}, u32[]{:S(2)}, u32[]{:S(2)}) collective-permute-start(bf16[2,32,1536]{2,1,0:T(8,128)(2,1)S(1)} %get-tuple-element.33), channel_id=1, source_target_pairs={{2,4},{4,2},{3,5},{5,3},{10,12},{12,10},{11,13},{13,11},{18,20},{2... | collective-permute-start | bytes 589832 | tf_op jit(solution)/shard_map/ppermute | solution.py:28
  5.4 2.5 %collective-permute-done.refs_0_.refs_1_.rest_1_ = bf16[2,32,1536]{2,1,0:T(8,128)(2,1)S(1)} collective-permute-done((bf16[2,32,1536]{2,1,0:T(8,128)(2,1)S(1)}, bf16[2,32,1536]{2,1,0:T(8,128)(2,1)S(1)}, u32[]{:S(2)}, u32[]{:S(2)}) %collective-permute-start) | collective-permute-done | bytes 196640 | tf_op jit(solution)/shard_map/ppermute | solution.py:28
  7.8 4.0 %collective-permute-done.1.refs_1_.refs_2_.rest_2_ = bf16[2,32,1536]{2,1,0:T(8,128)(2,1)S(1)} collective-permute-done((bf16[2,32,1536]{2,1,0:T(8,128)(2,1)S(1)}, bf16[2,32,1536]{2,1,0:T(8,128)(2,1)S(1)}, u32[]{:S(2)}, u32[]{:S(2)}) %collective-permute-start.1) | collective-permute-done | bytes 196640 | tf_op jit(solution)/shard_map/ppermute | solution.py:28
  11.9 0.1 kv_second.1
  11.9 1.4 %collective-permute-start.2 = (bf16[2,48,1536]{2,1,0:T(8,128)(2,1)S(1)}, bf16[2,48,1536]{2,1,0:T(8,128)(2,1)S(1)}, u32[]{:S(2)}, u32[]{:S(2)}) collective-permute-start(bf16[2,48,1536]{2,1,0:T(8,128)(2,1)S(1)} %get-tuple-element.34), channel_id=1, source_target_pairs={{0,8},{8,0},{16,24},{24,16},{1,9},{9,1},{17,25},{25,17},{2,10},{10... | collective-permute-start | bytes 884744 | tf_op jit(solution)/shard_map/ppermute | solution.py:28
  13.3 1.3 %qd_prepare.1 = (bf16[2,32,1536]{2,1,0:T(8,128)(2,1)S(1)}, bf16[2,32,1536]{2,1,0:T(8,128)(2,1)S(1)}, bf16[2,128,1536]{2,1,0:T(8,128)(2,1)S(1)}) custom-call(bf16[4,4,2,4,1536]{4,3,2,1,0:T(4,128)(2,1)} %refs_0_.3, bf16[4,4,2,4,1536]{4,3,2,1,0:T(4,128)(2,1)} %refs_1_.3), custom_call_target="tpu_custom_call" | custom-call | tf_op jit(solution)/shard_map/qd_prepare/pallas_call | solution.py:119
  14.7 0.2 collective-permute-start.6
  14.9 2.1 %collective-permute-start.7 = (bf16[2,32,1536]{2,1,0:T(8,128)(2,1)S(1)}, bf16[2,32,1536]{2,1,0:T(8,128)(2,1)S(1)}, u32[]{:S(2)}, u32[]{:S(2)}) collective-permute-start(bf16[2,32,1536]{2,1,0:T(8,128)(2,1)S(1)} %get-tuple-element.39), channel_id=1, source_target_pairs={{8,16},{16,8},{9,17},{17,9},{10,18},{18,10},{11,19},{19,11},{12,20... | collective-permute-start | bytes 589832 | tf_op jit(solution)/shard_map/ppermute | solution.py:28
  17.0 3.2 %collective-permute-start.3 = (bf16[2,48,1536]{2,1,0:T(8,128)(2,1)S(1)}, bf16[2,48,1536]{2,1,0:T(8,128)(2,1)S(1)}, u32[]{:S(2)}, u32[]{:S(2)}) collective-permute-start(bf16[2,48,1536]{2,1,0:T(8,128)(2,1)S(1)} %get-tuple-element.35), channel_id=1, source_target_pairs={{8,16},{16,8},{9,17},{17,9},{10,18},{18,10},{11,19},{19,11},{12,20... | collective-permute-start | bytes 884744 | tf_op jit(solution)/shard_map/ppermute | solution.py:28
  20.2 0.1 kv_near.1
  20.2 2.8 %collective-permute-start.4 = (bf16[2,96,1536]{2,1,0:T(8,128)(2,1)S(1)}, bf16[2,96,1536]{2,1,0:T(8,128)(2,1)S(1)}, u32[]{:S(2)}, u32[]{:S(2)}) collective-permute-start(bf16[2,96,1536]{2,1,0:T(8,128)(2,1)S(1)} %kv_near.1), channel_id=1, source_target_pairs={{0,1},{1,0},{2,3},{3,2},{4,5},{5,4},{6,7},{7,6},{8,9},{9,8},{10,11... | collective-permute-start | bytes 1769480 | tf_op jit(solution)/shard_map/ppermute | solution.py:28
  23.1 0.1 collective-permute-done.6.refs_0_.refs_1_.rest_1_.refs_5_
  23.1 0.0 collective-permute-done.7.refs_1_.refs_2_.rest_2_.refs_6_
  23.1 0.2 qd_second.1
  23.3 0.1 collective-permute-start.8
  23.4 4.3 %collective-permute-start.9 = (bf16[2,48,1536]{2,1,0:T(8,128)(2,1)S(1)}, bf16[2,48,1536]{2,1,0:T(8,128)(2,1)S(1)}, u32[]{:S(2)}, u32[]{:S(2)}) collective-permute-start(bf16[2,48,1536]{2,1,0:T(8,128)(2,1)S(1)} %get-tuple-element.41), channel_id=1, source_target_pairs={{2,4},{4,2},{3,5},{5,3},{10,12},{12,10},{11,13},{13,11},{18,20},{2... | collective-permute-start | bytes 884744 | tf_op jit(solution)/shard_map/ppermute | solution.py:28
  27.7 0.1 qd_near.1
  27.8 0.0 collective-permute-done.2.refs_0_.rest_3_
  27.8 3.7 %collective-permute-start.10 = (bf16[2,96,1536]{2,1,0:T(8,128)(2,1)S(1)}, bf16[2,96,1536]{2,1,0:T(8,128)(2,1)S(1)}, u32[]{:S(2)}, u32[]{:S(2)}) collective-permute-start(bf16[2,96,1536]{2,1,0:T(8,128)(2,1)S(1)} %qd_near.1), channel_id=1, source_target_pairs={{0,1},{1,0},{2,3},{3,2},{4,5},{5,4},{6,7},{7,6},{8,9},{9,8},{10,11... | collective-permute-start | bytes 1769480 | tf_op jit(solution)/shard_map/ppermute | solution.py:28
  31.5 0.0 collective-permute-done.3.refs_1_.rest_4_
  31.6 0.1 collective-permute-start.5
  31.7 0.0 collective-permute-done.8.refs_0_.rest_3_.refs_7_
  31.7 4.2 %collective-permute-done.9.refs_1_.rest_4_.refs_8_ = bf16[2,48,1536]{2,1,0:T(8,128)(2,1)S(1)} collective-permute-done((bf16[2,48,1536]{2,1,0:T(8,128)(2,1)S(1)}, bf16[2,48,1536]{2,1,0:T(8,128)(2,1)S(1)}, u32[]{:S(2)}, u32[]{:S(2)}) %collective-permute-start.9) | collective-permute-done | bytes 294944 | tf_op jit(solution)/shard_map/ppermute | solution.py:28
  35.9 4.3 %collective-permute-start.11 = (bf16[2,48,1536]{2,1,0:T(8,128)(2,1)S(1)}, bf16[2,48,1536]{2,1,0:T(8,128)(2,1)S(1)}, u32[]{:S(2)}, u32[]{:S(2)}) collective-permute-start(bf16[2,48,1536]{2,1,0:T(8,128)(2,1)S(1)} %qd_far.1), channel_id=1, source_target_pairs={{0,1},{1,0},{2,3},{3,2},{4,5},{5,4},{6,7},{7,6},{8,9},{9,8},{10,11... | collective-permute-start | bytes 884744 | tf_op jit(solution)/shard_map/ppermute | solution.py:28
  40.2 1.5 %codes.1 = (s32[128,512]{1,0:T(8,128)S(1)}, s32[128,512]{1,0:T(8,128)S(1)}, s32[8,12]{1,0:T(8,128)S(1)}) custom-call(s32[128,8]{1,0:T(8,128)} %constant.6.clone.refs_0_, s32[8,512]{1,0:T(8,128)} %constant.7.clone.refs_1_, s32[8,512]{1,0:T(8,128)} %constant.8.clone.refs_2_, s32[16,4,16]{2,1,0:T(4,128)} %bitcast.2, s32[3,12]{1,0:T(4,128)} %bitcast.3), custom_call_target="tpu_custom_call" | custom-call | tf_op jit(solution)/shard_map/codes/pallas_call | solution.py:119
  41.7 0.0 collective-permute-done.4.rest_5_
  41.7 0.0 collective-permute-done.5.rest_6_
  41.7 4.2 %query_side.1 = (bf16[4,4,2,4,1536]{4,3,2,1,0:T(4,128)(2,1)}, f32[1,128,128]{2,1,0:T(8,128)S(1)}, f32[1,32,128]{2,1,0:T(8,128)S(1)}, f32[1,32,128]{2,1,0:T(8,128)S(1)}) custom-call(s32[8,12]{1,0:T(8,128)S(1)} %get-tuple-element.28.closed_ref, s32[128,512]{1,0:T(8,128)S(1)} %get-tuple-element.29.code_ref, ...), custom_call_target="tpu_custom_call" | custom-call | tf_op jit(solution)/shard_map/query_side/pallas_call | solution.py:119
  45.9 1.3 %collective-permute-start.12 = (f32[1,32,128]{2,1,0:T(8,128)S(1)}, f32[1,32,128]{2,1,0:T(8,128)S(1)}, u32[]{:S(2)}, u32[]{:S(2)}) collective-permute-start(f32[1,32,128]{2,1,0:T(8,128)S(1)} %get-tuple-element.47), channel_id=1, source_target_pairs={{0,8},{8,0},{16,24},{24,16},{1,9},{9,1},{17,25},{25,17},{2,10},{10... | collective-permute-start | bytes 49160 | tf_op jit(solution)/shard_map/ppermute | solution.py:28
  47.2 1.9 %collective-permute-start.13 = (f32[1,32,128]{2,1,0:T(8,128)S(1)}, f32[1,32,128]{2,1,0:T(8,128)S(1)}, u32[]{:S(2)}, u32[]{:S(2)}) collective-permute-start(f32[1,32,128]{2,1,0:T(8,128)S(1)} %get-tuple-element.48), channel_id=1, source_target_pairs={{8,16},{16,8},{9,17},{17,9},{10,18},{18,10},{11,19},{19,11},{12,20... | collective-permute-start | bytes 49160 | tf_op jit(solution)/shard_map/ppermute | solution.py:28
  49.1 0.0 collective-permute-done.12.refs_0_.refs_1_.refs_12_
  49.1 2.5 %collective-permute-done.13.refs_1_.refs_2_.refs_13_ = f32[1,32,128]{2,1,0:T(8,128)S(1)} collective-permute-done((f32[1,32,128]{2,1,0:T(8,128)S(1)}, f32[1,32,128]{2,1,0:T(8,128)S(1)}, u32[]{:S(2)}, u32[]{:S(2)}) %collective-permute-start.13) | collective-permute-done | bytes 16416 | tf_op jit(solution)/shard_map/ppermute | solution.py:28
  51.7 0.1 collective-permute-start.14
  51.8 1.9 %collective-permute-start.15 = (f32[1,48,128]{2,1,0:T(8,128)S(1)}, f32[1,48,128]{2,1,0:T(8,128)S(1)}, u32[]{:S(2)}, u32[]{:S(2)}) collective-permute-start(f32[1,48,128]{2,1,0:T(8,128)S(1)} %get-tuple-element.50), channel_id=1, source_target_pairs={{2,4},{4,2},{3,5},{5,3},{10,12},{12,10},{11,13},{13,11},{18,20},{2... | collective-permute-start | bytes 73736 | tf_op jit(solution)/shard_map/ppermute | solution.py:28
  53.7 1.7 %collective-permute-start.16 = (f32[1,96,128]{2,1,0:T(8,128)S(1)}, f32[1,96,128]{2,1,0:T(8,128)S(1)}, u32[]{:S(2)}, u32[]{:S(2)}) collective-permute-start(f32[1,96,128]{2,1,0:T(8,128)S(1)} %st_near.1), channel_id=1, source_target_pairs={{0,1},{1,0},{2,3},{3,2},{4,5},{5,4},{6,7},{7,6},{8,9},{9,8},{10,11... | collective-permute-start | bytes 147464 | tf_op jit(solution)/shard_map/ppermute | solution.py:28
  55.5 0.0 collective-permute-done.14.refs_0_.refs_14_
  55.5 1.8 %collective-permute-done.15.refs_1_.refs_15_ = f32[1,48,128]{2,1,0:T(8,128)S(1)} collective-permute-done((f32[1,48,128]{2,1,0:T(8,128)S(1)}, f32[1,48,128]{2,1,0:T(8,128)S(1)}, u32[]{:S(2)}, u32[]{:S(2)}) %collective-permute-start.15) | collective-permute-done | bytes 24608 | tf_op jit(solution)/shard_map/ppermute | solution.py:28
  57.2 2.6 %collective-permute-start.17 = (f32[1,48,128]{2,1,0:T(8,128)S(1)}, f32[1,48,128]{2,1,0:T(8,128)S(1)}, u32[]{:S(2)}, u32[]{:S(2)}) collective-permute-start(f32[1,48,128]{2,1,0:T(8,128)S(1)} %st_far.1), channel_id=1, source_target_pairs={{0,1},{1,0},{2,3},{3,2},{4,5},{5,4},{6,7},{7,6},{8,9},{9,8},{10,11... | collective-permute-start | bytes 73736 | tf_op jit(solution)/shard_map/ppermute | solution.py:28
  59.8 0.0 collective-permute-done.10.rest_5_.refs_9_
  59.8 0.0 collective-permute-done.11.rest_6_.refs_10_
  59.9 0.7 %key_products_0.1 = (f32[6,128,512]{2,1,0:T(8,128)S(1)}, f32[6,128,512]{2,1,0:T(8,128)S(1)}) custom-call(s32[8,12]{1,0:T(8,128)S(1)} %get-tuple-element.28.closed_ref, s32[128,512]{1,0:T(8,128)S(1)} %get-tuple-element.37.code_ref, bf16[2,128,1536]{2,1,0:T(8,128)(2,1)S(1)} %get-tuple-element.31.own_ref.refs_0_.rest_0_.kv_ref, ...), custom_call_target="tpu_custom_call" | custom-call | tf_op jit(solution)/shard_map/key_products_0/pallas_call | solution.py:119
  60.6 0.7 %key_products_1.1 = (f32[6,128,512]{2,1,0:T(8,128)S(1)}, f32[6,128,512]{2,1,0:T(8,128)S(1)}) custom-call(s32[8,12]{1,0:T(8,128)S(1)} %get-tuple-element.28.closed_ref, s32[128,512]{1,0:T(8,128)S(1)} %get-tuple-element.37.code_ref, bf16[2,128,1536]{2,1,0:T(8,128)(2,1)S(1)} %get-tuple-element.31.own_ref.refs_0_.rest_0_.kv_ref, ...), custom_call_target="tpu_custom_call" | custom-call | tf_op jit(solution)/shard_map/key_products_1/pallas_call | solution.py:119
  61.3 0.0 collective-permute-done.16.refs_16_
  61.3 0.0 collective-permute-done.17.refs_17_
  61.3 2.2 %key_side.1 = (bf16[4,4,2,4,1536]{4,3,2,1,0:T(4,128)(2,1)}, bf16[4,4,2,4,1536]{4,3,2,1,0:T(4,128)(2,1)}) custom-call(f32[6,128,512]{2,1,0:T(8,128)S(1)} %get-tuple-element.42.refs_0_, f32[6,128,512]{2,1,0:T(8,128)S(1)} %get-tuple-element.43.refs_1_, f32[6,128,512]{2,1,0:T(8,128)S(1)} %get-tuple-element.44.refs_2_, ...), custom_call_target="tpu_custom_call" | custom-call | tf_op jit(solution)/shard_map/key_side/pallas_call | solution.py:119
  (5 shorter events, 0.1 us)
Async XLA Ops:
  2.0 5.9 %collective-permute-start = (bf16[2,32,1536]{2,1,0:T(8,128)(2,1)S(1)}, bf16[2,32,1536]{2,1,0:T(8,128)(2,1)S(1)}, u32[]{:S(2)}, u32[]{:S(2)}) collective-permute-start(bf16[2,32,1536]{2,1,0:T(8,128)(2,1)S(1)} %get-tuple-element.32), channel_id=1, source_target_pairs={{0,2},{2,0},{4,6},{6,4},{1,3},{3,1},{5,7},{7,5},{8,10},{10,8},{12,... | collective-permute-start | bytes 589832 | tf_op jit(solution)/shard_map/ppermute | solution.py:28
  3.3 8.6 %collective-permute-start.1 = (bf16[2,32,1536]{2,1,0:T(8,128)(2,1)S(1)}, bf16[2,32,1536]{2,1,0:T(8,128)(2,1)S(1)}, u32[]{:S(2)}, u32[]{:S(2)}) collective-permute-start(bf16[2,32,1536]{2,1,0:T(8,128)(2,1)S(1)} %get-tuple-element.33), channel_id=1, source_target_pairs={{2,4},{4,2},{3,5},{5,3},{10,12},{12,10},{11,13},{13,11},{18,20},{2... | collective-permute-start | bytes 589832 | tf_op jit(solution)/shard_map/ppermute | solution.py:28
  11.9 15.9 %collective-permute-start.2 = (bf16[2,48,1536]{2,1,0:T(8,128)(2,1)S(1)}, bf16[2,48,1536]{2,1,0:T(8,128)(2,1)S(1)}, u32[]{:S(2)}, u32[]{:S(2)}) collective-permute-start(bf16[2,48,1536]{2,1,0:T(8,128)(2,1)S(1)} %get-tuple-element.34), channel_id=1, source_target_pairs={{0,8},{8,0},{16,24},{24,16},{1,9},{9,1},{17,25},{25,17},{2,10},{10... | collective-permute-start | bytes 884744 | tf_op jit(solution)/shard_map/ppermute | solution.py:28
  14.7 8.5 %collective-permute-start.6 = (bf16[2,32,1536]{2,1,0:T(8,128)(2,1)S(1)}, bf16[2,32,1536]{2,1,0:T(8,128)(2,1)S(1)}, u32[]{:S(2)}, u32[]{:S(2)}) collective-permute-start(bf16[2,32,1536]{2,1,0:T(8,128)(2,1)S(1)} %get-tuple-element.38), channel_id=1, source_target_pairs={{0,8},{8,0},{16,24},{24,16},{1,9},{9,1},{17,25},{25,17},{2,10},{10... | collective-permute-start | bytes 589832 | tf_op jit(solution)/shard_map/ppermute | solution.py:28
  14.9 8.2 %collective-permute-start.7 = (bf16[2,32,1536]{2,1,0:T(8,128)(2,1)S(1)}, bf16[2,32,1536]{2,1,0:T(8,128)(2,1)S(1)}, u32[]{:S(2)}, u32[]{:S(2)}) collective-permute-start(bf16[2,32,1536]{2,1,0:T(8,128)(2,1)S(1)} %get-tuple-element.39), channel_id=1, source_target_pairs={{8,16},{16,8},{9,17},{17,9},{10,18},{18,10},{11,19},{19,11},{12,20... | collective-permute-start | bytes 589832 | tf_op jit(solution)/shard_map/ppermute | solution.py:28
  17.0 14.6 %collective-permute-start.3 = (bf16[2,48,1536]{2,1,0:T(8,128)(2,1)S(1)}, bf16[2,48,1536]{2,1,0:T(8,128)(2,1)S(1)}, u32[]{:S(2)}, u32[]{:S(2)}) collective-permute-start(bf16[2,48,1536]{2,1,0:T(8,128)(2,1)S(1)} %get-tuple-element.35), channel_id=1, source_target_pairs={{8,16},{16,8},{9,17},{17,9},{10,18},{18,10},{11,19},{19,11},{12,20... | collective-permute-start | bytes 884744 | tf_op jit(solution)/shard_map/ppermute | solution.py:28
  20.2 21.5 %collective-permute-start.4 = (bf16[2,96,1536]{2,1,0:T(8,128)(2,1)S(1)}, bf16[2,96,1536]{2,1,0:T(8,128)(2,1)S(1)}, u32[]{:S(2)}, u32[]{:S(2)}) collective-permute-start(bf16[2,96,1536]{2,1,0:T(8,128)(2,1)S(1)} %kv_near.1), channel_id=1, source_target_pairs={{0,1},{1,0},{2,3},{3,2},{4,5},{5,4},{6,7},{7,6},{8,9},{9,8},{10,11... | collective-permute-start | bytes 1769480 | tf_op jit(solution)/shard_map/ppermute | solution.py:28
  23.3 8.3 %collective-permute-start.8 = (bf16[2,48,1536]{2,1,0:T(8,128)(2,1)S(1)}, bf16[2,48,1536]{2,1,0:T(8,128)(2,1)S(1)}, u32[]{:S(2)}, u32[]{:S(2)}) collective-permute-start(bf16[2,48,1536]{2,1,0:T(8,128)(2,1)S(1)} %get-tuple-element.40), channel_id=1, source_target_pairs={{0,2},{2,0},{4,6},{6,4},{1,3},{3,1},{5,7},{7,5},{8,10},{10,8},{12,... | collective-permute-start | bytes 884744 | tf_op jit(solution)/shard_map/ppermute | solution.py:28
  23.4 12.4 %collective-permute-start.9 = (bf16[2,48,1536]{2,1,0:T(8,128)(2,1)S(1)}, bf16[2,48,1536]{2,1,0:T(8,128)(2,1)S(1)}, u32[]{:S(2)}, u32[]{:S(2)}) collective-permute-start(bf16[2,48,1536]{2,1,0:T(8,128)(2,1)S(1)} %get-tuple-element.41), channel_id=1, source_target_pairs={{2,4},{4,2},{3,5},{5,3},{10,12},{12,10},{11,13},{13,11},{18,20},{2... | collective-permute-start | bytes 884744 | tf_op jit(solution)/shard_map/ppermute | solution.py:28
  27.8 32.0 %collective-permute-start.10 = (bf16[2,96,1536]{2,1,0:T(8,128)(2,1)S(1)}, bf16[2,96,1536]{2,1,0:T(8,128)(2,1)S(1)}, u32[]{:S(2)}, u32[]{:S(2)}) collective-permute-start(bf16[2,96,1536]{2,1,0:T(8,128)(2,1)S(1)} %qd_near.1), channel_id=1, source_target_pairs={{0,1},{1,0},{2,3},{3,2},{4,5},{5,4},{6,7},{7,6},{8,9},{9,8},{10,11... | collective-permute-start | bytes 1769480 | tf_op jit(solution)/shard_map/ppermute | solution.py:28
  31.6 10.2 %collective-permute-start.5 = (bf16[2,48,1536]{2,1,0:T(8,128)(2,1)S(1)}, bf16[2,48,1536]{2,1,0:T(8,128)(2,1)S(1)}, u32[]{:S(2)}, u32[]{:S(2)}) collective-permute-start(bf16[2,48,1536]{2,1,0:T(8,128)(2,1)S(1)} %kv_far.1), channel_id=1, source_target_pairs={{0,1},{1,0},{2,3},{3,2},{4,5},{5,4},{6,7},{7,6},{8,9},{9,8},{10,11... | collective-permute-start | bytes 884744 | tf_op jit(solution)/shard_map/ppermute | solution.py:28
  35.9 24.0 %collective-permute-start.11 = (bf16[2,48,1536]{2,1,0:T(8,128)(2,1)S(1)}, bf16[2,48,1536]{2,1,0:T(8,128)(2,1)S(1)}, u32[]{:S(2)}, u32[]{:S(2)}) collective-permute-start(bf16[2,48,1536]{2,1,0:T(8,128)(2,1)S(1)} %qd_far.1), channel_id=1, source_target_pairs={{0,1},{1,0},{2,3},{3,2},{4,5},{5,4},{6,7},{7,6},{8,9},{9,8},{10,11... | collective-permute-start | bytes 884744 | tf_op jit(solution)/shard_map/ppermute | solution.py:28
  45.9 3.2 %collective-permute-start.12 = (f32[1,32,128]{2,1,0:T(8,128)S(1)}, f32[1,32,128]{2,1,0:T(8,128)S(1)}, u32[]{:S(2)}, u32[]{:S(2)}) collective-permute-start(f32[1,32,128]{2,1,0:T(8,128)S(1)} %get-tuple-element.47), channel_id=1, source_target_pairs={{0,8},{8,0},{16,24},{24,16},{1,9},{9,1},{17,25},{25,17},{2,10},{10... | collective-permute-start | bytes 49160 | tf_op jit(solution)/shard_map/ppermute | solution.py:28
  47.2 4.5 %collective-permute-start.13 = (f32[1,32,128]{2,1,0:T(8,128)S(1)}, f32[1,32,128]{2,1,0:T(8,128)S(1)}, u32[]{:S(2)}, u32[]{:S(2)}) collective-permute-start(f32[1,32,128]{2,1,0:T(8,128)S(1)} %get-tuple-element.48), channel_id=1, source_target_pairs={{8,16},{16,8},{9,17},{17,9},{10,18},{18,10},{11,19},{19,11},{12,20... | collective-permute-start | bytes 49160 | tf_op jit(solution)/shard_map/ppermute | solution.py:28
  51.7 3.8 %collective-permute-start.14 = (f32[1,48,128]{2,1,0:T(8,128)S(1)}, f32[1,48,128]{2,1,0:T(8,128)S(1)}, u32[]{:S(2)}, u32[]{:S(2)}) collective-permute-start(f32[1,48,128]{2,1,0:T(8,128)S(1)} %get-tuple-element.49), channel_id=1, source_target_pairs={{0,2},{2,0},{4,6},{6,4},{1,3},{3,1},{5,7},{7,5},{8,10},{10,8},{12,... | collective-permute-start | bytes 73736 | tf_op jit(solution)/shard_map/ppermute | solution.py:28
  51.8 5.5 %collective-permute-start.15 = (f32[1,48,128]{2,1,0:T(8,128)S(1)}, f32[1,48,128]{2,1,0:T(8,128)S(1)}, u32[]{:S(2)}, u32[]{:S(2)}) collective-permute-start(f32[1,48,128]{2,1,0:T(8,128)S(1)} %get-tuple-element.50), channel_id=1, source_target_pairs={{2,4},{4,2},{3,5},{5,3},{10,12},{12,10},{11,13},{13,11},{18,20},{2... | collective-permute-start | bytes 73736 | tf_op jit(solution)/shard_map/ppermute | solution.py:28
  53.7 7.6 %collective-permute-start.16 = (f32[1,96,128]{2,1,0:T(8,128)S(1)}, f32[1,96,128]{2,1,0:T(8,128)S(1)}, u32[]{:S(2)}, u32[]{:S(2)}) collective-permute-start(f32[1,96,128]{2,1,0:T(8,128)S(1)} %st_near.1), channel_id=1, source_target_pairs={{0,1},{1,0},{2,3},{3,2},{4,5},{5,4},{6,7},{7,6},{8,9},{9,8},{10,11... | collective-permute-start | bytes 147464 | tf_op jit(solution)/shard_map/ppermute | solution.py:28
  57.2 4.1 %collective-permute-start.17 = (f32[1,48,128]{2,1,0:T(8,128)S(1)}, f32[1,48,128]{2,1,0:T(8,128)S(1)}, u32[]{:S(2)}, u32[]{:S(2)}) collective-permute-start(f32[1,48,128]{2,1,0:T(8,128)S(1)} %st_far.1), channel_id=1, source_target_pairs={{0,1},{1,0},{2,3},{3,2},{4,5},{5,4},{6,7},{7,6},{8,9},{9,8},{10,11... | collective-permute-start | bytes 73736 | tf_op jit(solution)/shard_map/ppermute | solution.py:28

commit v4 on v3

--- a/solution.py
+++ b/solution.py
@@ -16,16 +16,26 @@
 AXES = ("ta", "ha", "wa")
 
 
-def matchings(n):
-    even = [(i, i ^ 1) for i in range(n) if (i ^ 1) < n]
-    odd = [(i, ((i + 1) ^ 1) - 1) for i in range(n) if 0 <= ((i + 1) ^ 1) - 1 < n]
-    return [m for m in (even, odd) if m]
+def matchings(axis):
+    n, m = lax.axis_size(axis), lax.axis_size("wa")
+    if axis == "wa":
+        sets = [[(i, i + 1) for i in range(k, n - 1, 2)] for k in range(2)]
+        return [s + [(j, i) for i, j in s] for s in sets if s]
+    sets = []
+    for k in range(min(2, n - 1)):
+        paired = [(i, i + 1) for i in range(k, n - 1, 2)]
+        alone = sorted(set(range(n)) - {i for p in paired for i in p})
+        pairs = [(i * m + w, j * m + w) for w in range(m) for i, j in paired]
+        pairs += [(i * m + w, i * m + w + 1) for i in alone for w in range(0, m - 1, 2)]
+        sets.append(pairs + [(j, i) for i, j in pairs])
+    return sets
 
 
 def swap(axis, sends):
+    axes = axis if axis == "wa" else (axis, "wa")
     got = []
-    for k, pairs in enumerate(matchings(lax.axis_size(axis))):
-        got.append(lax.ppermute(sends[k], axis, pairs))
+    for k, pairs in enumerate(matchings(axis)):
+        got.append(lax.ppermute(sends[k], axes, pairs))
     return got
 
 
@@ -48,8 +58,9 @@
             put(k, 0 if k == 0 else length - 1)
 
 
-def prepare_kernel(block, axis, count, *refs):
+def prepare_kernel(block, plan, *refs):
     T, H, W, C = block
+    count = len(plan)
     args, faces, (whole, buf, sems) = refs[:2], refs[2 : 2 + count], refs[2 + count :]
     copies = [
         [pltpu.make_async_copy(args[a].at[t], buf.at[a, t], sems.at[a, t]) for t in range(T)]
@@ -66,13 +77,28 @@
             for t in range(T):
                 r = (w * T + t) * H * C
                 whole[a, r : r + H * C, :] = buf[a, t, :, w].reshape(H * C, width)
-            for k in range(count):
-                n = faces[k].shape[1] // W
+            for face, (axis, k) in zip(faces, plan):
+                n = face.shape[1] // W
                 if axis == "ha":
                     layer = buf[a, :, sent_layer(axis, k, H), w]
                 else:
                     layer = buf[a, sent_layer(axis, k, T), :, w]
-                faces[k][a, w * n : (w + 1) * n, :] = layer.reshape(n, width)
+                face[a, w * n : (w + 1) * n, :] = layer.reshape(n, width)
+
+
+def corner_kernel(block, near, count, *refs):
+    T, _, W, C = block
+    got, outs = refs[:near], refs[near:]
+
+    def put(k, t):
+        for a in range(got[0].shape[0]):
+            for w in range(W):
+                at = (w * T + t) * C
+                outs[k][a, w * near * C : (w + 1) * near * C, :] = jnp.concatenate(
+                    [r[a, at : at + C, :] for r in got], axis=0
+                )
+
+    by_parity("ta", count, T, put)
 
 
 def second_kernel(block, axis, near, count, own_ref, *refs):
@@ -116,7 +142,7 @@
 
 def local(kernel, out_shape, operands, space=pltpu.VMEM, **kw):
     place = pl.BlockSpec(memory_space=space)
-    return pl.pallas_call(
+    made = pl.pallas_call(
         kernel,
         out_shape=out_shape,
         in_specs=[place] * len(operands),
@@ -124,60 +150,82 @@
         compiler_params=pltpu.CompilerParams(vmem_limit_bytes=16 << 20),
         **kw,
     )(*operands)
-
-
-def spread(own, got, axis, block, counts, name):
-    T, H, W, C = block
+    return list(made)
+
+
+def column_swap(pieces, block, counts, name):
+    k, _, width = pieces[0].shape
+    n = sum(p.shape[1] for p in pieces) // block[2]
+    sends = local(
+        functools.partial(column_kernel, block, counts[2]),
+        [pltpu.VMEM((k, n, width), pieces[0].dtype)] * counts[2],
+        pieces,
+        name=name,
+    )
+    return swap("wa", sends)
+
+
+def spread(own, got, block, counts, name):
+    T, _, W, C = block
     k, _, width = own.shape
-    near, count, length = (counts[1], counts[0], H) if axis == "ta" else (counts[0], counts[1], T)
     more = swap(
-        axis,
+        "ha",
         local(
-            functools.partial(second_kernel, block, axis, near, count),
-            [pltpu.VMEM((k, W * (length + near) * C, width), own.dtype)] * count,
+            functools.partial(second_kernel, block, "ha", counts[0], counts[1]),
+            [pltpu.VMEM((k, W * (T + counts[0]) * C, width), own.dtype)] * counts[1],
             [own] + got,
             name=name + "_second",
         ),
     )
-    columns = []
-    for part, pieces in (("near", [own] + got), ("far", more)):
-        n = sum(p.shape[1] for p in pieces) // W
-        sends = local(
-            functools.partial(column_kernel, block, counts[2]),
-            [pltpu.VMEM((k, n, width), own.dtype)] * counts[2],
-            pieces,
-            name=f"{name}_{part}",
-        )
-        columns += swap("wa", sends)
-    return got + more + columns
-
-
-def piece_coords(block, counts, second):
+    near = column_swap([own] + got, block, counts, name + "_near")
+    far = column_swap(more, block, counts, name + "_far")
+    return got + more + near + far
+
+
+def spread_early(own, ha, ta, block, counts, name):
+    _, _, W, C = block
+    k, _, width = own.shape
+    corners = swap(
+        "ta",
+        local(
+            functools.partial(corner_kernel, block, counts[1], counts[0]),
+            [pltpu.VMEM((k, W * counts[1] * C, width), own.dtype)] * counts[0],
+            ha,
+            name=name + "_corner",
+        ),
+    )
+    near = [own] + ha + ta
+    near += column_swap(near, block, counts, name + "_near")
+    far = corners + column_swap(corners, block, counts, name + "_far")
+    return near, far
+
+
+def piece_coords(block, counts, early):
     T, H, W, C = block
     marks = [(EVEN, ODD)[:n] for n in counts]
-    ts, hs = list(range(T)), list(range(H))
-    own = [[[(t, h, w) for h in hs] for t in ts] for w in range(W)]
-    pieces = [np.array(own, np.int32).reshape(W, -1, 3)]
-    if second == "ta":
-        for m in marks[1]:
-            pieces.append(np.array([[(t, m, w) for t in ts] for w in range(W)], np.int32))
-        for m in marks[0]:
-            line = hs + list(marks[1])
-            pieces.append(np.array([[(m, h, w) for h in line] for w in range(W)], np.int32))
+    ts, hs, ws = list(range(T)), list(range(H)), list(range(W))
+
+    def piece(cells):
+        return np.array([[cell + (w,) for cell in cells] for w in ws], np.int32)
+
+    own = piece([(t, h) for t in ts for h in hs])
+    if early:
+        near = [own] + [piece([(t, m) for t in ts]) for m in marks[1]]
+        near += [piece([(m, h) for h in hs]) for m in marks[0]]
+        far = [piece([(m, h) for h in marks[1]]) for m in marks[0]]
     else:
-        for m in marks[0]:
-            pieces.append(np.array([[(m, h, w) for h in hs] for w in range(W)], np.int32))
-        for m in marks[1]:
-            line = ts + list(marks[0])
-            pieces.append(np.array([[(t, m, w) for t in line] for w in range(W)], np.int32))
-    out = [p.reshape(-1, 3) for p in pieces]
-    near = 1 + len(marks[1] if second == "ta" else marks[0])
-    for part in (pieces[:near], pieces[near:]):
+        near = [own] + [piece([(m, h) for h in hs]) for m in marks[0]]
+        far = [piece([(t, m) for t in ts + list(marks[0])]) for m in marks[1]]
+    columns = []
+    for part in (near, far):
+        column = np.concatenate([p[0] for p in part], axis=0)
+        columns.append([])
         for m in marks[2]:
-            c = np.concatenate([p[0] for p in part], axis=0)
-            c[:, 2] = m
-            out.append(c)
-    return np.repeat(np.concatenate(out, axis=0), C, axis=0)
+            columns[-1].append(column.copy())
+            columns[-1][-1][:, 2] = m
+    near, far = ([p.reshape(-1, 3) for p in part] for part in (near, far))
+    groups = [near + columns[0], far + columns[1]] if early else [near + far + sum(columns, [])]
+    return [np.repeat(np.concatenate(g, axis=0), C, axis=0) for g in groups]
 
 
 def codes_kernel(block, grids, *refs):
@@ -232,10 +280,12 @@
     return lax.dot_general(a, b, dims, preferred_element_type=jnp.float32)
 
 
-def gather(refs, which, cols, pad):
-    parts = [r[which, :, cols] for r in refs]
-    if pad:
-        parts.append(jnp.zeros((pad, parts[0].shape[1]), parts[0].dtype))
+def gather(groups, which, cols):
+    parts = []
+    for refs, pad in groups:
+        parts += [r[which, :, cols] for r in refs]
+        if pad:
+            parts.append(jnp.zeros((pad, parts[0].shape[1]), parts[0].dtype))
     return jnp.concatenate(parts, axis=0)
 
 
@@ -248,14 +298,29 @@
             ref[t, :, w, :, cols] = value[r : r + H * C].reshape(H, C, value.shape[1])
 
 
-def query_kernel(cfg, block, faces, closed_ref, code_ref, qd_ref, *rest):
-    heads, depth, pad, count = cfg
-    kv = rest[:count]
-    dq_ref, stat_ref = rest[count : count + 2]
-    first_refs = rest[count + 2 : count + 2 + faces]
-    s_ref, g_ref, d_ref = rest[count + 2 + faces :]
+def products_kernel(cfg, begin, closed_ref, code_ref, own_ref, *rest):
+    depth, pad, count, factor = cfg
+    groups, (s_ref, g_ref) = [(rest[:count], pad)], rest[count:]
+    wide = s_ref.shape[2]
+    for i in range(s_ref.shape[0]):
+        h = begin + i
+        cols = slice(h * depth, (h + 1) * depth)
+        allowed = (code_ref[:, :wide] & closed_ref[0:1, h : h + 1]) == 0
+        scores = dot(own_ref[0, :, cols], gather(groups, 0, cols), NT) * factor
+        s_ref[i] = jnp.where(allowed, scores, NEG)
+        g_ref[i] = dot(own_ref[1, :, cols], gather(groups, 1, cols), NT)
+
+
+def query_kernel(cfg, block, faces, closed_ref, code_ref, near_s_ref, near_g_ref, qd_ref, *rest):
+    heads, depth, pads, counts = cfg
+    kv, rest = rest[: sum(counts)], rest[sum(counts) :]
+    near, far = (kv[: counts[0]], pads[0]), (kv[counts[0] :], pads[1])
+    dq_ref, stat_ref = rest[:2]
+    first_refs = rest[2 : 2 + faces]
+    s_ref, g_ref, d_ref = rest[2 + faces :]
     scale = 1.0 / math.sqrt(depth)
     rows = qd_ref.shape[1]
+    wide = near_s_ref.shape[2]
     step = math.gcd(rows, 32)
     stat_ref[...] = jnp.zeros(stat_ref.shape, jnp.float32)
 
@@ -264,8 +329,8 @@
 
     def products(h):
         cols = columns(h)
-        s_ref[h % 2] = dot(qd_ref[0, :, cols], gather(kv, 0, cols, pad), NT)
-        g_ref[h % 2] = dot(qd_ref[1, :, cols], gather(kv, 1, cols, pad), NT)
+        s_ref[h % 2] = dot(qd_ref[0, :, cols], gather([far], 0, cols), NT)
+        g_ref[h % 2] = dot(qd_ref[1, :, cols], gather([far], 1, cols), NT)
 
     products(0)
     for h in range(heads):
@@ -274,19 +339,21 @@
         ratios = []
         for r in range(0, rows, step):
             band = slice(r, r + step)
-            allowed = (code_ref[band, :] & closed_ref[0:1, h : h + 1]) == 0
-            scores = jnp.where(allowed, s_ref[h % 2, band, :], NEG)
+            allowed = (code_ref[band, wide:] & closed_ref[0:1, h : h + 1]) == 0
+            scores = jnp.concatenate(
+                [near_s_ref[h, band, :], jnp.where(allowed, s_ref[h % 2, band, :], NEG)], axis=1
+            )
             peak = jnp.max(scores, axis=1, keepdims=True)
             raised = jnp.exp2((scores - peak) * (scale * LOG2E))
             total = jnp.sum(raised, axis=1, keepdims=True)
-            grads = g_ref[h % 2, band, :]
+            grads = jnp.concatenate([near_g_ref[h, band, :], g_ref[h % 2, band, :]], axis=1)
             drift = jnp.sum(raised * grads, axis=1, keepdims=True) / total
             d_ref[h % 2, band, :] = (raised * (grads - drift)).astype(jnp.bfloat16)
             stat_ref[0, band, h : h + 1] = peak * (scale * LOG2E) + jnp.log2(total)
             stat_ref[0, band, heads + h : heads + h + 1] = drift
             ratios.append(scale / total)
         cols = columns(h)
-        product = dot(d_ref[h % 2], gather(kv, 0, cols, pad), NN)
+        product = dot(d_ref[h % 2], gather([near, far], 0, cols), NN)
         put_tiles(dq_ref, product * jnp.concatenate(ratios, axis=0), cols)
     T, H, W, C = block
 
@@ -298,23 +365,10 @@
     by_parity("ta", faces, T, put)
 
 
-def key_products_kernel(cfg, begin, closed_ref, code_ref, kv_ref, *rest):
-    _, depth, pad, count = cfg
-    qd, (s_ref, g_ref) = rest[:count], rest[count:]
-    scale = 1.0 / math.sqrt(depth)
-    for i in range(s_ref.shape[0]):
-        h = begin + i
-        cols = slice(h * depth, (h + 1) * depth)
-        allowed = (code_ref[...] & closed_ref[0:1, h : h + 1]) == 0
-        scores = dot(kv_ref[0, :, cols], gather(qd, 0, cols, pad), NT) * (scale * LOG2E)
-        s_ref[i] = jnp.where(allowed, scores, NEG)
-        g_ref[i] = dot(kv_ref[1, :, cols], gather(qd, 1, cols, pad), NT)
-
-
 def key_kernel(cfg, parts, *refs):
     heads, depth, pad, count = cfg
     products, refs = refs[: 2 * parts], refs[2 * parts :]
-    qd, st = refs[:count], refs[count : 2 * count]
+    qd, st = [(refs[:count], pad)], refs[count : 2 * count]
     dk_ref, dv_ref, row_ref = refs[2 * count :]
     scale = 1.0 / math.sqrt(depth)
     lines = [r[0] for r in st]
@@ -328,8 +382,8 @@
         attention = jnp.exp2(s_ref[h % each] - row_ref[h : h + 1, :])
         drift = row_ref[heads + h : heads + h + 1, :]
         score_grads = (attention * (g_ref[h % each] - drift)).astype(jnp.bfloat16)
-        put_tiles(dk_ref, dot(score_grads, gather(qd, 0, cols, pad), NN) * scale, cols)
-        put_tiles(dv_ref, dot(attention.astype(jnp.bfloat16), gather(qd, 1, cols, pad), NN), cols)
+        put_tiles(dk_ref, dot(score_grads, gather(qd, 0, cols), NN) * scale, cols)
+        put_tiles(dv_ref, dot(attention.astype(jnp.bfloat16), gather(qd, 1, cols), NN), cols)
 
 
 def per_device(queries, key_states, value_states, output_cotangent, tile_valid, window_radius):
@@ -339,7 +393,7 @@
     depth = width // heads
     sizes = tuple(lax.axis_size(a) for a in AXES)
     grids = tuple(n * b for n, b in zip(sizes, block))
-    counts = tuple(len(matchings(n)) for n in sizes)
+    counts = tuple(len(matchings(a)) for a in AXES)
     rows = T * H * W * C
 
     kind = jax.ShapeDtypeStruct
@@ -348,12 +402,11 @@
         for x in (key_states, value_states, queries, output_cotangent)
     ]
 
-    def prepared(pair, axis, name):
-        a = AXES.index(axis)
-        n = W * C * (T if axis == "ha" else H)
+    def prepared(pair, axes, name):
+        plan = [(x, k) for x in axes for k in range(counts[AXES.index(x)])]
         made = local(
-            functools.partial(prepare_kernel, block, axis, counts[a]),
-            [pltpu.VMEM((2, n, width), jnp.bfloat16)] * counts[a]
+            functools.partial(prepare_kernel, block, plan),
+            [pltpu.VMEM((2, W * C * (T if x == "ha" else H), width), jnp.bfloat16) for x, _ in plan]
             + [pltpu.VMEM((2, rows, width), jnp.bfloat16)],
             pair,
             space=pltpu.HBM,
@@ -363,28 +416,35 @@
             ],
             name=name + "_prepare",
         )
-        return made[-1], swap(axis, made[:-1])
-
-    kv, kv_ha = prepared(args[:2], "ha", "kv")
-    qd, qd_ta = prepared(args[2:], "ta", "qd")
-    kv_pieces = [kv] + spread(kv, kv_ha, "ta", block, counts, "kv")
-    qd_pieces = [qd] + spread(qd, qd_ta, "ha", block, counts, "qd")
-
-    def table(second):
-        coords = piece_coords(block, counts, second)
-        total = coords.shape[0]
-        padded = -(-total // 128) * 128
-        out = np.full((8, padded), -(1 << 20), np.int32)
-        out[:3, :total] = coords.T
-        inner = np.zeros((rows, 8), np.int32)
-        inner[:, :3] = coords[:rows]
-        return inner, out, padded - total
-
-    inner, outer_k, pad_k = table("ta")
-    _, outer_q, pad_q = table("ha")
-    kcfg = (heads, depth, pad_k, len(kv_pieces))
+        got, at = [], 0
+        for x in axes:
+            n = counts[AXES.index(x)]
+            got.append(swap(x, made[at : at + n]))
+            at += n
+        return made[-1], got
+
+    kv, (kv_ha, kv_ta) = prepared(args[:2], ("ha", "ta"), "kv")
+    qd, (qd_ta,) = prepared(args[2:], ("ta",), "qd")
+    near, far = spread_early(kv, kv_ha, kv_ta, block, counts, "kv")
+    qd_pieces = [qd] + spread(qd, qd_ta, block, counts, "qd")
+
+    def table(early):
+        groups = piece_coords(block, counts, early)
+        pads = [-len(g) % 128 for g in groups]
+        out = np.full((8, sum(len(g) + p for g, p in zip(groups, pads))), -(1 << 20), np.int32)
+        at = 0
+        for g, p in zip(groups, pads):
+            out[:3, at : at + len(g)] = g.T
+            at += len(g) + p
+        return groups, pads, out
+
+    groups, pads_k, outer_k = table(True)
+    _, (pad_q,), outer_q = table(False)
+    inner = np.zeros((rows, 8), np.int32)
+    inner[:, :3] = groups[0][:rows]
+    wide = len(groups[0]) + pads_k[0]
+    wide_k, wide_q = outer_k.shape[1], outer_q.shape[1]
     qcfg = (heads, depth, pad_q, len(qd_pieces))
-    wide_k, wide_q = outer_k.shape[1], outer_q.shape[1]
     native = kind(queries.shape, jnp.bfloat16)
     lanes = -(-2 * heads // 128) * 128
     tables = [inner, outer_k, outer_q, tile_valid.transpose(0, 2, 1), window_radius.T]
@@ -402,23 +462,34 @@
         name="codes",
     )
 
+    near_products = local(
+        functools.partial(products_kernel, (depth, pads_k[0], len(near), 1.0), 0),
+        [pltpu.VMEM((heads, rows, wide), jnp.float32)] * 2,
+        [closed, query_code, qd] + near,
+        name="query_products",
+    )
+    kcfg = (heads, depth, pads_k, (len(near), len(far)))
     made = local(
         functools.partial(query_kernel, kcfg, block, counts[0]),
         [native, pltpu.VMEM((1, rows, lanes), jnp.float32)]
         + [pltpu.VMEM((1, W * H * C, lanes), jnp.float32)] * counts[0],
-        [closed, query_code, qd] + kv_pieces,
-        scratch_shapes=[pltpu.VMEM((2, rows, wide_k), jnp.float32)] * 2
+        [closed, query_code] + near_products + [qd] + near + far,
+        scratch_shapes=[pltpu.VMEM((2, rows, wide_k - wide), jnp.float32)] * 2
         + [pltpu.VMEM((2, rows, wide_k), jnp.bfloat16)],
         name="query_side",
     )
     query_gradient, stats = made[:2]
     st_ta = swap("ta", made[2:])
-    stat_pieces = [stats] + spread(stats, st_ta, "ha", block, counts, "st")
+    stat_pieces = [stats] + spread(stats, st_ta, block, counts, "st")
     parts = math.gcd(heads, 2)
     products = []
     for i in range(parts):
         products += local(
-            functools.partial(key_products_kernel, qcfg, i * heads // parts),
+            functools.partial(
+                products_kernel,
+                (depth, pad_q, len(qd_pieces), LOG2E / math.sqrt(depth)),
+                i * heads // parts,
+            ),
             [pltpu.VMEM((heads // parts, rows, wide_q), jnp.float32)] * 2,
             [closed, key_code, kv] + qd_pieces,
             name=f"key_products_{i}",

time: 63.9 us -> 64.6 us (1.011)
  starting transfers between devices: 35.1 us -> 17.8 us
  waiting for transfers between devices: 15.1 us -> 32.4 us
  Pallas kernels: 12.5 us -> 13.4 us
    ppermute x18 -> x20, starting transfers between devices: 35.1 us -> 17.8 us  [swap(): got.append(lax.ppermute(sends[k], axes, pairs))]
    ppermute x18 -> x20, waiting for transfers between devices: 15.1 us -> 32.4 us  [swap(): got.append(lax.ppermute(sends[k], axes, pairs))]
    pallas_call x16 -> x17, Pallas kernels: 12.5 us -> 13.4 us  [local(): pl.pallas_call(kernel, out_shape=out_shape, in_specs=[place] * len(operan...]
  transfers between devices with their start and end apart: 18 -> 20, of which waited for: 6 -> 10; matrix products, arithmetic and copies ran while one was open for 0% -> 0% of each run, Pallas kernels for 14% -> 15%
where the time goes in v4:
time: 64.6 us; the launch traced here: 64.3 us
  waiting for transfers between devices  32.4 us (50%)
  starting transfers between devices  17.8 us (28%)
  Pallas kernels  13.4 us (21%)
  between operations  0.77 us (1%)
    ppermute x20, waiting for transfers between devices, swap(): got.append(lax.ppermute(sends[k], axes, pairs))  32.4 us
    ppermute x20, starting transfers between devices, swap(): got.append(lax.ppermute(sends[k], axes, pairs))  17.8 us
    pallas_call x17, Pallas kernels, local(): pl.pallas_call(kernel, out_shape=out_shape, in_specs=[place] * len(operan...  13.4 us
  transfers between devices with their start and end apart: 20, of which 10 were waited for; matrix products, arithmetic and copies ran while one was open for 0% of the time, Pallas kernels for 15%

profile of v4, /device:TPU:21, one launch (start us, length us, event | category | flops | bytes accessed | tf_op | source)
XLA Modules:
  0.0 64.3 jit_solution(8379707510846489077)
XLA Ops:
  0.6 1.4 %kv_prepare.1 = (bf16[2,32,1536]{2,1,0:T(8,128)(2,1)S(1)}, bf16[2,32,1536]{2,1,0:T(8,128)(2,1)S(1)}, bf16[2,32,1536]{2,1,0:T(8,128)(2,1)S(1)}, bf16[2,32,1536]{2,1,0:T(8,128)(2,1)S(1)}, bf16[2,128,1536]{2,1,0:T(8,128)(2,1)S(1)}) custom-call(bf16[4,4,2,4,1536]{4,3,2,1,0:T(4,128)(2,1)} %refs_0_.4, bf16[4,4,2,4,1536]{4,3,2,1,0:T(4,128)(2,1)} %refs_1_.4), custom_call_target="tpu_custom_call" | custom-call | tf_op jit(solution)/shard_map/kv_prepare/pallas_call | solution.py:145
  2.0 1.3 %collective-permute-start = (bf16[2,32,1536]{2,1,0:T(8,128)(2,1)S(1)}, bf16[2,32,1536]{2,1,0:T(8,128)(2,1)S(1)}, u32[]{:S(2)}, u32[]{:S(2)}) collective-permute-start(bf16[2,32,1536]{2,1,0:T(8,128)(2,1)S(1)} %get-tuple-element.36), channel_id=1, source_target_pairs={{0,2},{4,6},{1,3},{5,7},{2,0},{6,4},{3,1},{7,5},{8,10},{12,14},{9,... | collective-permute-start | bytes 589832 | tf_op jit(solution)/shard_map/ppermute | solution.py:38
  3.3 0.2 collective-permute-start.1
  3.5 1.3 %collective-permute-start.2 = (bf16[2,32,1536]{2,1,0:T(8,128)(2,1)S(1)}, bf16[2,32,1536]{2,1,0:T(8,128)(2,1)S(1)}, u32[]{:S(2)}, u32[]{:S(2)}) collective-permute-start(bf16[2,32,1536]{2,1,0:T(8,128)(2,1)S(1)} %get-tuple-element.38), channel_id=1, source_target_pairs={{0,8},{16,24},{1,9},{17,25},{8,0},{24,16},{9,1},{25,17},{2,10},{18... | collective-permute-start | bytes 589832 | tf_op jit(solution)/shard_map/ppermute | solution.py:38
  4.8 0.0 collective-permute-start.3
  4.8 3.1 %collective-permute-done.refs_1_.rest_1_.refs_0_ = bf16[2,32,1536]{2,1,0:T(8,128)(2,1)S(1)} collective-permute-done((bf16[2,32,1536]{2,1,0:T(8,128)(2,1)S(1)}, bf16[2,32,1536]{2,1,0:T(8,128)(2,1)S(1)}, u32[]{:S(2)}, u32[]{:S(2)}) %collective-permute-start) | collective-permute-done | bytes 196640 | tf_op jit(solution)/shard_map/ppermute | solution.py:38
  7.9 4.2 %collective-permute-done.1.refs_2_.rest_2_.refs_1_ = bf16[2,32,1536]{2,1,0:T(8,128)(2,1)S(1)} collective-permute-done((bf16[2,32,1536]{2,1,0:T(8,128)(2,1)S(1)}, bf16[2,32,1536]{2,1,0:T(8,128)(2,1)S(1)}, u32[]{:S(2)}, u32[]{:S(2)}) %collective-permute-start.1) | collective-permute-done | bytes 196640 | tf_op jit(solution)/shard_map/ppermute | solution.py:38
  12.0 0.0 collective-permute-done.2.refs_3_.rest_3_
  12.0 0.0 collective-permute-done.3.refs_4_.rest_4_
  12.0 0.1 kv_near.1
  12.1 1.6 %collective-permute-start.4 = (bf16[2,128,1536]{2,1,0:T(8,128)(2,1)S(1)}, bf16[2,128,1536]{2,1,0:T(8,128)(2,1)S(1)}, u32[]{:S(2)}, u32[]{:S(2)}) collective-permute-start(bf16[2,128,1536]{2,1,0:T(8,128)(2,1)S(1)} %kv_near.1), channel_id=1, source_target_pairs={{0,1},{1,0},{2,3},{3,2},{4,5},{5,4},{6,7},{7,6},{8,9},{9,8},{10,11... | collective-permute-start | bytes 2359304 | tf_op jit(solution)/shard_map/ppermute | solution.py:38
  13.7 1.3 %qd_prepare.1 = (bf16[2,32,1536]{2,1,0:T(8,128)(2,1)S(1)}, bf16[2,32,1536]{2,1,0:T(8,128)(2,1)S(1)}, bf16[2,128,1536]{2,1,0:T(8,128)(2,1)S(1)}) custom-call(bf16[4,4,2,4,1536]{4,3,2,1,0:T(4,128)(2,1)} %refs_0_.3, bf16[4,4,2,4,1536]{4,3,2,1,0:T(4,128)(2,1)} %refs_1_.3), custom_call_target="tpu_custom_call" | custom-call | tf_op jit(solution)/shard_map/qd_prepare/pallas_call | solution.py:145
  15.0 1.4 %collective-permute-start.8 = (bf16[2,32,1536]{2,1,0:T(8,128)(2,1)S(1)}, bf16[2,32,1536]{2,1,0:T(8,128)(2,1)S(1)}, u32[]{:S(2)}, u32[]{:S(2)}) collective-permute-start(bf16[2,32,1536]{2,1,0:T(8,128)(2,1)S(1)} %get-tuple-element.46), channel_id=1, source_target_pairs={{0,8},{16,24},{1,9},{17,25},{8,0},{24,16},{9,1},{25,17},{2,10},{18... | collective-permute-start | bytes 589832 | tf_op jit(solution)/shard_map/ppermute | solution.py:38
  16.4 0.0 collective-permute-start.9
  16.4 5.1 %collective-permute-done.8.refs_0_.refs_1_.rest_1_.refs_5_ = bf16[2,32,1536]{2,1,0:T(8,128)(2,1)S(1)} collective-permute-done((bf16[2,32,1536]{2,1,0:T(8,128)(2,1)S(1)}, bf16[2,32,1536]{2,1,0:T(8,128)(2,1)S(1)}, u32[]{:S(2)}, u32[]{:S(2)}) %collective-permute-start.8) | collective-permute-done | bytes 196640 | tf_op jit(solution)/shard_map/ppermute | solution.py:38
  21.5 1.0 %collective-permute-done.9.refs_1_.refs_2_.rest_2_.refs_6_ = bf16[2,32,1536]{2,1,0:T(8,128)(2,1)S(1)} collective-permute-done((bf16[2,32,1536]{2,1,0:T(8,128)(2,1)S(1)}, bf16[2,32,1536]{2,1,0:T(8,128)(2,1)S(1)}, u32[]{:S(2)}, u32[]{:S(2)}) %collective-permute-start.9) | collective-permute-done | bytes 196640 | tf_op jit(solution)/shard_map/ppermute | solution.py:38
  22.6 0.2 qd_second.1
  22.7 0.1 collective-permute-start.10
  22.8 2.2 %collective-permute-start.11 = (bf16[2,48,1536]{2,1,0:T(8,128)(2,1)S(1)}, bf16[2,48,1536]{2,1,0:T(8,128)(2,1)S(1)}, u32[]{:S(2)}, u32[]{:S(2)}) collective-permute-start(bf16[2,48,1536]{2,1,0:T(8,128)(2,1)S(1)} %get-tuple-element.49), channel_id=1, source_target_pairs={{2,4},{3,5},{0,1},{6,7},{4,2},{5,3},{1,0},{7,6},{10,12},{11,13},{8... | collective-permute-start | bytes 884744 | tf_op jit(solution)/shard_map/ppermute | solution.py:38
  25.1 1.5 %collective-permute-start.12 = (bf16[2,96,1536]{2,1,0:T(8,128)(2,1)S(1)}, bf16[2,96,1536]{2,1,0:T(8,128)(2,1)S(1)}, u32[]{:S(2)}, u32[]{:S(2)}) collective-permute-start(bf16[2,96,1536]{2,1,0:T(8,128)(2,1)S(1)} %qd_near.1), channel_id=1, source_target_pairs={{0,1},{1,0},{2,3},{3,2},{4,5},{5,4},{6,7},{7,6},{8,9},{9,8},{10,11... | collective-permute-start | bytes 1769480 | tf_op jit(solution)/shard_map/ppermute | solution.py:38
  26.6 3.6 %collective-permute-done.10.refs_0_.rest_3_.refs_7_ = bf16[2,48,1536]{2,1,0:T(8,128)(2,1)S(1)} collective-permute-done((bf16[2,48,1536]{2,1,0:T(8,128)(2,1)S(1)}, bf16[2,48,1536]{2,1,0:T(8,128)(2,1)S(1)}, u32[]{:S(2)}, u32[]{:S(2)}) %collective-permute-start.10) | collective-permute-done | bytes 294944 | tf_op jit(solution)/shard_map/ppermute | solution.py:38
  30.2 7.3 %collective-permute-done.11.refs_1_.rest_4_.refs_8_ = bf16[2,48,1536]{2,1,0:T(8,128)(2,1)S(1)} collective-permute-done((bf16[2,48,1536]{2,1,0:T(8,128)(2,1)S(1)}, bf16[2,48,1536]{2,1,0:T(8,128)(2,1)S(1)}, u32[]{:S(2)}, u32[]{:S(2)}) %collective-permute-start.11) | collective-permute-done | bytes 294944 | tf_op jit(solution)/shard_map/ppermute | solution.py:38
  37.6 1.8 %collective-permute-start.13 = (bf16[2,48,1536]{2,1,0:T(8,128)(2,1)S(1)}, bf16[2,48,1536]{2,1,0:T(8,128)(2,1)S(1)}, u32[]{:S(2)}, u32[]{:S(2)}) collective-permute-start(bf16[2,48,1536]{2,1,0:T(8,128)(2,1)S(1)} %qd_far.1), channel_id=1, source_target_pairs={{0,1},{1,0},{2,3},{3,2},{4,5},{5,4},{6,7},{7,6},{8,9},{9,8},{10,11... | collective-permute-start | bytes 884744 | tf_op jit(solution)/shard_map/ppermute | solution.py:38
  39.4 0.1 kv_corner.1
  39.4 0.3 collective-permute-start.5
  39.8 0.1 collective-permute-start.6
  39.8 4.0 %collective-permute-done.5.refs_0_.rest_6_ = bf16[2,16,1536]{2,1,0:T(8,128)(2,1)S(1)} collective-permute-done((bf16[2,16,1536]{2,1,0:T(8,128)(2,1)S(1)}, bf16[2,16,1536]{2,1,0:T(8,128)(2,1)S(1)}, u32[]{:S(2)}, u32[]{:S(2)}) %collective-permute-start.5) | collective-permute-done | bytes 98336 | tf_op jit(solution)/shard_map/ppermute | solution.py:38
  43.8 0.0 collective-permute-done.6.refs_1_.rest_7_
  43.8 1.2 %collective-permute-start.7 = (bf16[2,16,1536]{2,1,0:T(8,128)(2,1)S(1)}, bf16[2,16,1536]{2,1,0:T(8,128)(2,1)S(1)}, u32[]{:S(2)}, u32[]{:S(2)}) collective-permute-start(bf16[2,16,1536]{2,1,0:T(8,128)(2,1)S(1)} %kv_far.1), channel_id=1, source_target_pairs={{0,1},{1,0},{2,3},{3,2},{4,5},{5,4},{6,7},{7,6},{8,9},{9,8},{10,11... | collective-permute-start | bytes 294920 | tf_op jit(solution)/shard_map/ppermute | solution.py:38
  45.1 1.5 %codes.1 = (s32[128,512]{1,0:T(8,128)S(1)}, s32[128,512]{1,0:T(8,128)S(1)}, s32[8,12]{1,0:T(8,128)S(1)}) custom-call(s32[128,8]{1,0:T(8,128)} %constant.6.clone.refs_0_, s32[8,512]{1,0:T(8,128)} %constant.7.clone.refs_1_, s32[8,512]{1,0:T(8,128)} %constant.8.clone.refs_2_, s32[16,4,16]{2,1,0:T(4,128)} %bitcast.2, s32[3,12]{1,0:T(4,128)} %bitcast.3), custom_call_target="tpu_custom_call" | custom-call | tf_op jit(solution)/shard_map/codes/pallas_call | solution.py:145
  46.6 0.0 collective-permute-done.4.rest_5_
  46.6 1.1 %query_products.1 = (f32[12,128,384]{2,1,0:T(8,128)S(1)}, f32[12,128,384]{2,1,0:T(8,128)S(1)}) custom-call(s32[8,12]{1,0:T(8,128)S(1)} %get-tuple-element.32.closed_ref, s32[128,512]{1,0:T(8,128)S(1)} %get-tuple-element.33.code_ref, bf16[2,128,1536]{2,1,0:T(8,128)(2,1)S(1)} %get-tuple-element.34.own_ref.qd_ref.refs_0_.rest_0_.refs_4_, ...), custom_call_target="tpu_custom_call" | custom-call | tf_op jit(solution)/shard_map/query_products/pallas_call | solution.py:145
  47.7 0.0 collective-permute-done.7.rest_8_
  47.8 4.0 %query_side.1 = (bf16[4,4,2,4,1536]{4,3,2,1,0:T(4,128)(2,1)}, f32[1,128,128]{2,1,0:T(8,128)S(1)}, f32[1,32,128]{2,1,0:T(8,128)S(1)}, f32[1,32,128]{2,1,0:T(8,128)S(1)}) custom-call(s32[8,12]{1,0:T(8,128)S(1)} %get-tuple-element.32.closed_ref, s32[128,512]{1,0:T(8,128)S(1)} %get-tuple-element.33.code_ref, f32[12,128,384]{2,1,0:T(8,128)S(1)} %get-tuple-element.40.near_s_ref, ...), custom_call_target="tpu_custom_call" | custom-call | tf_op jit(solution)/shard_map/query_side/pallas_call | solution.py:145
  51.7 0.0 collective-permute-start.14
  51.7 0.1 collective-permute-start.15
  51.8 2.5 %collective-permute-done.14.refs_0_.refs_1_.refs_12_ = f32[1,32,128]{2,1,0:T(8,128)S(1)} collective-permute-done((f32[1,32,128]{2,1,0:T(8,128)S(1)}, f32[1,32,128]{2,1,0:T(8,128)S(1)}, u32[]{:S(2)}, u32[]{:S(2)}) %collective-permute-start.14) | collective-permute-done | bytes 16416 | tf_op jit(solution)/shard_map/ppermute | solution.py:38
  54.3 0.0 collective-permute-done.15.refs_1_.refs_2_.refs_13_
  54.3 0.1 collective-permute-start.16
  54.4 0.3 collective-permute-start.17
  54.7 1.7 %collective-permute-start.18 = (f32[1,96,128]{2,1,0:T(8,128)S(1)}, f32[1,96,128]{2,1,0:T(8,128)S(1)}, u32[]{:S(2)}, u32[]{:S(2)}) collective-permute-start(f32[1,96,128]{2,1,0:T(8,128)S(1)} %st_near.1), channel_id=1, source_target_pairs={{0,1},{1,0},{2,3},{3,2},{4,5},{5,4},{6,7},{7,6},{8,9},{9,8},{10,11... | collective-permute-start | bytes 147464 | tf_op jit(solution)/shard_map/ppermute | solution.py:38
  56.4 0.7 %collective-permute-done.16.refs_0_.refs_14_ = f32[1,48,128]{2,1,0:T(8,128)S(1)} collective-permute-done((f32[1,48,128]{2,1,0:T(8,128)S(1)}, f32[1,48,128]{2,1,0:T(8,128)S(1)}, u32[]{:S(2)}, u32[]{:S(2)}) %collective-permute-start.16) | collective-permute-done | bytes 24608 | tf_op jit(solution)/shard_map/ppermute | solution.py:38
  57.1 1.0 %collective-permute-done.17.refs_1_.refs_15_ = f32[1,48,128]{2,1,0:T(8,128)S(1)} collective-permute-done((f32[1,48,128]{2,1,0:T(8,128)S(1)}, f32[1,48,128]{2,1,0:T(8,128)S(1)}, u32[]{:S(2)}, u32[]{:S(2)}) %collective-permute-start.17) | collective-permute-done | bytes 24608 | tf_op jit(solution)/shard_map/ppermute | solution.py:38
  58.1 2.6 %collective-permute-start.19 = (f32[1,48,128]{2,1,0:T(8,128)S(1)}, f32[1,48,128]{2,1,0:T(8,128)S(1)}, u32[]{:S(2)}, u32[]{:S(2)}) collective-permute-start(f32[1,48,128]{2,1,0:T(8,128)S(1)} %st_far.1), channel_id=1, source_target_pairs={{0,1},{1,0},{2,3},{3,2},{4,5},{5,4},{6,7},{7,6},{8,9},{9,8},{10,11... | collective-permute-start | bytes 73736 | tf_op jit(solution)/shard_map/ppermute | solution.py:38
  60.7 0.0 collective-permute-done.12.rest_5_.refs_9_
  60.7 0.0 collective-permute-done.13.rest_6_.refs_10_
  60.7 0.7 %key_products_0.1 = (f32[6,128,512]{2,1,0:T(8,128)S(1)}, f32[6,128,512]{2,1,0:T(8,128)S(1)}) custom-call(s32[8,12]{1,0:T(8,128)S(1)} %get-tuple-element.32.closed_ref, s32[128,512]{1,0:T(8,128)S(1)} %get-tuple-element.45.code_ref, bf16[2,128,1536]{2,1,0:T(8,128)(2,1)S(1)} %get-tuple-element.35.refs_0_.rest_0_.own_ref, ...), custom_call_target="tpu_custom_call" | custom-call | tf_op jit(solution)/shard_map/key_products_0/pallas_call | solution.py:145
  61.4 0.7 %key_products_1.1 = (f32[6,128,512]{2,1,0:T(8,128)S(1)}, f32[6,128,512]{2,1,0:T(8,128)S(1)}) custom-call(s32[8,12]{1,0:T(8,128)S(1)} %get-tuple-element.32.closed_ref, s32[128,512]{1,0:T(8,128)S(1)} %get-tuple-element.45.code_ref, bf16[2,128,1536]{2,1,0:T(8,128)(2,1)S(1)} %get-tuple-element.35.refs_0_.rest_0_.own_ref, ...), custom_call_target="tpu_custom_call" | custom-call | tf_op jit(solution)/shard_map/key_products_1/pallas_call | solution.py:145
  62.1 0.0 collective-permute-done.18.refs_16_
  62.1 0.0 collective-permute-done.19.refs_17_
  62.1 2.2 %key_side.1 = (bf16[4,4,2,4,1536]{4,3,2,1,0:T(4,128)(2,1)}, bf16[4,4,2,4,1536]{4,3,2,1,0:T(4,128)(2,1)}) custom-call(f32[6,128,512]{2,1,0:T(8,128)S(1)} %get-tuple-element.50.refs_0_, f32[6,128,512]{2,1,0:T(8,128)S(1)} %get-tuple-element.51.refs_1_, f32[6,128,512]{2,1,0:T(8,128)S(1)} %get-tuple-element.52.refs_2_, ...), custom_call_target="tpu_custom_call" | custom-call | tf_op jit(solution)/shard_map/key_side/pallas_call | solution.py:145
  (6 shorter events, 0.1 us)
Async XLA Ops:
  2.0 5.9 %collective-permute-start = (bf16[2,32,1536]{2,1,0:T(8,128)(2,1)S(1)}, bf16[2,32,1536]{2,1,0:T(8,128)(2,1)S(1)}, u32[]{:S(2)}, u32[]{:S(2)}) collective-permute-start(bf16[2,32,1536]{2,1,0:T(8,128)(2,1)S(1)} %get-tuple-element.36), channel_id=1, source_target_pairs={{0,2},{4,6},{1,3},{5,7},{2,0},{6,4},{3,1},{7,5},{8,10},{12,14},{9,... | collective-permute-start | bytes 589832 | tf_op jit(solution)/shard_map/ppermute | solution.py:38
  3.3 8.7 %collective-permute-start.1 = (bf16[2,32,1536]{2,1,0:T(8,128)(2,1)S(1)}, bf16[2,32,1536]{2,1,0:T(8,128)(2,1)S(1)}, u32[]{:S(2)}, u32[]{:S(2)}) collective-permute-start(bf16[2,32,1536]{2,1,0:T(8,128)(2,1)S(1)} %get-tuple-element.37), channel_id=1, source_target_pairs={{2,4},{3,5},{0,1},{6,7},{4,2},{5,3},{1,0},{7,6},{10,12},{11,13},{8... | collective-permute-start | bytes 589832 | tf_op jit(solution)/shard_map/ppermute | solution.py:38
  3.5 8.5 %collective-permute-start.2 = (bf16[2,32,1536]{2,1,0:T(8,128)(2,1)S(1)}, bf16[2,32,1536]{2,1,0:T(8,128)(2,1)S(1)}, u32[]{:S(2)}, u32[]{:S(2)}) collective-permute-start(bf16[2,32,1536]{2,1,0:T(8,128)(2,1)S(1)} %get-tuple-element.38), channel_id=1, source_target_pairs={{0,8},{16,24},{1,9},{17,25},{8,0},{24,16},{9,1},{25,17},{2,10},{18... | collective-permute-start | bytes 589832 | tf_op jit(solution)/shard_map/ppermute | solution.py:38
  4.8 7.2 %collective-permute-start.3 = (bf16[2,32,1536]{2,1,0:T(8,128)(2,1)S(1)}, bf16[2,32,1536]{2,1,0:T(8,128)(2,1)S(1)}, u32[]{:S(2)}, u32[]{:S(2)}) collective-permute-start(bf16[2,32,1536]{2,1,0:T(8,128)(2,1)S(1)} %get-tuple-element.39), channel_id=1, source_target_pairs={{8,16},{9,17},{0,1},{24,25},{16,8},{17,9},{1,0},{25,24},{10,18},{1... | collective-permute-start | bytes 589832 | tf_op jit(solution)/shard_map/ppermute | solution.py:38
  12.1 34.5 %collective-permute-start.4 = (bf16[2,128,1536]{2,1,0:T(8,128)(2,1)S(1)}, bf16[2,128,1536]{2,1,0:T(8,128)(2,1)S(1)}, u32[]{:S(2)}, u32[]{:S(2)}) collective-permute-start(bf16[2,128,1536]{2,1,0:T(8,128)(2,1)S(1)} %kv_near.1), channel_id=1, source_target_pairs={{0,1},{1,0},{2,3},{3,2},{4,5},{5,4},{6,7},{7,6},{8,9},{9,8},{10,11... | collective-permute-start | bytes 2359304 | tf_op jit(solution)/shard_map/ppermute | solution.py:38
  15.0 6.5 %collective-permute-start.8 = (bf16[2,32,1536]{2,1,0:T(8,128)(2,1)S(1)}, bf16[2,32,1536]{2,1,0:T(8,128)(2,1)S(1)}, u32[]{:S(2)}, u32[]{:S(2)}) collective-permute-start(bf16[2,32,1536]{2,1,0:T(8,128)(2,1)S(1)} %get-tuple-element.46), channel_id=1, source_target_pairs={{0,8},{16,24},{1,9},{17,25},{8,0},{24,16},{9,1},{25,17},{2,10},{18... | collective-permute-start | bytes 589832 | tf_op jit(solution)/shard_map/ppermute | solution.py:38
  16.4 6.2 %collective-permute-start.9 = (bf16[2,32,1536]{2,1,0:T(8,128)(2,1)S(1)}, bf16[2,32,1536]{2,1,0:T(8,128)(2,1)S(1)}, u32[]{:S(2)}, u32[]{:S(2)}) collective-permute-start(bf16[2,32,1536]{2,1,0:T(8,128)(2,1)S(1)} %get-tuple-element.47), channel_id=1, source_target_pairs={{8,16},{9,17},{0,1},{24,25},{16,8},{17,9},{1,0},{25,24},{10,18},{1... | collective-permute-start | bytes 589832 | tf_op jit(solution)/shard_map/ppermute | solution.py:38
  22.7 7.5 %collective-permute-start.10 = (bf16[2,48,1536]{2,1,0:T(8,128)(2,1)S(1)}, bf16[2,48,1536]{2,1,0:T(8,128)(2,1)S(1)}, u32[]{:S(2)}, u32[]{:S(2)}) collective-permute-start(bf16[2,48,1536]{2,1,0:T(8,128)(2,1)S(1)} %get-tuple-element.48), channel_id=1, source_target_pairs={{0,2},{4,6},{1,3},{5,7},{2,0},{6,4},{3,1},{7,5},{8,10},{12,14},{9,... | collective-permute-start | bytes 884744 | tf_op jit(solution)/shard_map/ppermute | solution.py:38
  22.8 14.7 %collective-permute-start.11 = (bf16[2,48,1536]{2,1,0:T(8,128)(2,1)S(1)}, bf16[2,48,1536]{2,1,0:T(8,128)(2,1)S(1)}, u32[]{:S(2)}, u32[]{:S(2)}) collective-permute-start(bf16[2,48,1536]{2,1,0:T(8,128)(2,1)S(1)} %get-tuple-element.49), channel_id=1, source_target_pairs={{2,4},{3,5},{0,1},{6,7},{4,2},{5,3},{1,0},{7,6},{10,12},{11,13},{8... | collective-permute-start | bytes 884744 | tf_op jit(solution)/shard_map/ppermute | solution.py:38
  25.1 35.6 %collective-permute-start.12 = (bf16[2,96,1536]{2,1,0:T(8,128)(2,1)S(1)}, bf16[2,96,1536]{2,1,0:T(8,128)(2,1)S(1)}, u32[]{:S(2)}, u32[]{:S(2)}) collective-permute-start(bf16[2,96,1536]{2,1,0:T(8,128)(2,1)S(1)} %qd_near.1), channel_id=1, source_target_pairs={{0,1},{1,0},{2,3},{3,2},{4,5},{5,4},{6,7},{7,6},{8,9},{9,8},{10,11... | collective-permute-start | bytes 1769480 | tf_op jit(solution)/shard_map/ppermute | solution.py:38
  37.6 23.1 %collective-permute-start.13 = (bf16[2,48,1536]{2,1,0:T(8,128)(2,1)S(1)}, bf16[2,48,1536]{2,1,0:T(8,128)(2,1)S(1)}, u32[]{:S(2)}, u32[]{:S(2)}) collective-permute-start(bf16[2,48,1536]{2,1,0:T(8,128)(2,1)S(1)} %qd_far.1), channel_id=1, source_target_pairs={{0,1},{1,0},{2,3},{3,2},{4,5},{5,4},{6,7},{7,6},{8,9},{9,8},{10,11... | collective-permute-start | bytes 884744 | tf_op jit(solution)/shard_map/ppermute | solution.py:38
  39.4 4.4 %collective-permute-start.5 = (bf16[2,16,1536]{2,1,0:T(8,128)(2,1)S(1)}, bf16[2,16,1536]{2,1,0:T(8,128)(2,1)S(1)}, u32[]{:S(2)}, u32[]{:S(2)}) collective-permute-start(bf16[2,16,1536]{2,1,0:T(8,128)(2,1)S(1)} %get-tuple-element.42), channel_id=1, source_target_pairs={{0,8},{16,24},{1,9},{17,25},{8,0},{24,16},{9,1},{25,17},{2,10},{18... | collective-permute-start | bytes 294920 | tf_op jit(solution)/shard_map/ppermute | solution.py:38
  39.8 4.0 %collective-permute-start.6 = (bf16[2,16,1536]{2,1,0:T(8,128)(2,1)S(1)}, bf16[2,16,1536]{2,1,0:T(8,128)(2,1)S(1)}, u32[]{:S(2)}, u32[]{:S(2)}) collective-permute-start(bf16[2,16,1536]{2,1,0:T(8,128)(2,1)S(1)} %get-tuple-element.43), channel_id=1, source_target_pairs={{8,16},{9,17},{0,1},{24,25},{16,8},{17,9},{1,0},{25,24},{10,18},{1... | collective-permute-start | bytes 294920 | tf_op jit(solution)/shard_map/ppermute | solution.py:38
  43.8 3.9 %collective-permute-start.7 = (bf16[2,16,1536]{2,1,0:T(8,128)(2,1)S(1)}, bf16[2,16,1536]{2,1,0:T(8,128)(2,1)S(1)}, u32[]{:S(2)}, u32[]{:S(2)}) collective-permute-start(bf16[2,16,1536]{2,1,0:T(8,128)(2,1)S(1)} %kv_far.1), channel_id=1, source_target_pairs={{0,1},{1,0},{2,3},{3,2},{4,5},{5,4},{6,7},{7,6},{8,9},{9,8},{10,11... | collective-permute-start | bytes 294920 | tf_op jit(solution)/shard_map/ppermute | solution.py:38
  51.7 2.6 %collective-permute-start.14 = (f32[1,32,128]{2,1,0:T(8,128)S(1)}, f32[1,32,128]{2,1,0:T(8,128)S(1)}, u32[]{:S(2)}, u32[]{:S(2)}) collective-permute-start(f32[1,32,128]{2,1,0:T(8,128)S(1)} %get-tuple-element.55), channel_id=1, source_target_pairs={{0,8},{16,24},{1,9},{17,25},{8,0},{24,16},{9,1},{25,17},{2,10},{18... | collective-permute-start | bytes 49160 | tf_op jit(solution)/shard_map/ppermute | solution.py:38
  51.7 2.6 %collective-permute-start.15 = (f32[1,32,128]{2,1,0:T(8,128)S(1)}, f32[1,32,128]{2,1,0:T(8,128)S(1)}, u32[]{:S(2)}, u32[]{:S(2)}) collective-permute-start(f32[1,32,128]{2,1,0:T(8,128)S(1)} %get-tuple-element.56), channel_id=1, source_target_pairs={{8,16},{9,17},{0,1},{24,25},{16,8},{17,9},{1,0},{25,24},{10,18},{1... | collective-permute-start | bytes 49160 | tf_op jit(solution)/shard_map/ppermute | solution.py:38
  54.3 2.7 %collective-permute-start.16 = (f32[1,48,128]{2,1,0:T(8,128)S(1)}, f32[1,48,128]{2,1,0:T(8,128)S(1)}, u32[]{:S(2)}, u32[]{:S(2)}) collective-permute-start(f32[1,48,128]{2,1,0:T(8,128)S(1)} %get-tuple-element.57), channel_id=1, source_target_pairs={{0,2},{4,6},{1,3},{5,7},{2,0},{6,4},{3,1},{7,5},{8,10},{12,14},{9,... | collective-permute-start | bytes 73736 | tf_op jit(solution)/shard_map/ppermute | solution.py:38
  54.4 3.6 %collective-permute-start.17 = (f32[1,48,128]{2,1,0:T(8,128)S(1)}, f32[1,48,128]{2,1,0:T(8,128)S(1)}, u32[]{:S(2)}, u32[]{:S(2)}) collective-permute-start(f32[1,48,128]{2,1,0:T(8,128)S(1)} %get-tuple-element.58), channel_id=1, source_target_pairs={{2,4},{3,5},{0,1},{6,7},{4,2},{5,3},{1,0},{7,6},{10,12},{11,13},{8... | collective-permute-start | bytes 73736 | tf_op jit(solution)/shard_map/ppermute | solution.py:38
  54.7 7.4 %collective-permute-start.18 = (f32[1,96,128]{2,1,0:T(8,128)S(1)}, f32[1,96,128]{2,1,0:T(8,128)S(1)}, u32[]{:S(2)}, u32[]{:S(2)}) collective-permute-start(f32[1,96,128]{2,1,0:T(8,128)S(1)} %st_near.1), channel_id=1, source_target_pairs={{0,1},{1,0},{2,3},{3,2},{4,5},{5,4},{6,7},{7,6},{8,9},{9,8},{10,11... | collective-permute-start | bytes 147464 | tf_op jit(solution)/shard_map/ppermute | solution.py:38
  58.1 4.1 %collective-permute-start.19 = (f32[1,48,128]{2,1,0:T(8,128)S(1)}, f32[1,48,128]{2,1,0:T(8,128)S(1)}, u32[]{:S(2)}, u32[]{:S(2)}) collective-permute-start(f32[1,48,128]{2,1,0:T(8,128)S(1)} %st_far.1), channel_id=1, source_target_pairs={{0,1},{1,0},{2,3},{3,2},{4,5},{5,4},{6,7},{7,6},{8,9},{9,8},{10,11... | collective-permute-start | bytes 73736 | tf_op jit(solution)/shard_map/ppermute | solution.py:38

commit v5 on v4

v5 whole, which is shorter than its diff:
```python
import functools
import math

import jax
import jax.numpy as jnp
import numpy as np
from jax import lax
from jax.experimental import pallas as pl
from jax.experimental.pallas import tpu as pltpu
from jax.sharding import PartitionSpec as P


NEG = -1e30
LOG2E = 1.4426950408889634
EVEN, ODD = 1000, 1001
AXES = ("ta", "ha", "wa")


def matchings(axis):
    n, m = lax.axis_size(axis), lax.axis_size("wa")
    if axis == "wa":
        sets = [[(i, i + 1) for i in range(k, n - 1, 2)] for k in range(2)]
        return [s + [(j, i) for i, j in s] for s in sets if s]
    sets = []
    for k in range(min(2, n - 1)):
        paired = [(i, i + 1) for i in range(k, n - 1, 2)]
        alone = sorted(set(range(n)) - {i for p in paired for i in p})
        pairs = [(i * m + w, j * m + w) for w in range(m) for i, j in paired]
        pairs += [(i * m + w, i * m + w + 1) for i in alone for w in range(0, m - 1, 2)]
        sets.append(pairs + [(j, i) for i, j in pairs])
    return sets


def swap(axis, sends):
    axes = axis if axis == "wa" else (axis, "wa")
    got = []
    for k, pairs in enumerate(matchings(axis)):
        got.append(lax.ppermute(sends[k], axes, pairs))
    return got


def sent_layer(axis, k, length):
    odd = lax.rem(lax.axis_index(axis), 2)
    return (1 - odd if k == 0 else odd) * (length - 1)


def by_parity(axis, count, length, put):
    odd = lax.rem(lax.axis_index(axis), 2)

    @pl.when(odd == 0)
    def _():
        for k in range(count):
            put(k, length - 1 if k == 0 else 0)

    @pl.when(odd == 1)
    def _():
        for k in range(count):
            put(k, 0 if k == 0 else length - 1)


def prepare_kernel(block, plan, *refs):
    T, H, W, C = block
    count = len(plan)
    args, faces, (whole, buf, sems) = refs[:2], refs[2 : 2 + count], refs[2 + count :]
    copies = [
        [pltpu.make_async_copy(args[a].at[t], buf.at[a, t], sems.at[a, t]) for t in range(T)]
        for a in range(2)
    ]
    for a in range(2):
        for copy in copies[a]:
            copy.start()
    width = buf.shape[-1]
    for a in range(2):
        for copy in copies[a]:
            copy.wait()
        for w in range(W):
            for t in range(T):
                r = (w * T + t) * H * C
                whole[a, r : r + H * C, :] = buf[a, t, :, w].reshape(H * C, width)
            for face, (axis, k) in zip(faces, plan):
                n = face.shape[1] // W
                if axis == "ha":
                    layer = buf[a, :, sent_layer(axis, k, H), w]
                else:
                    layer = buf[a, sent_layer(axis, k, T), :, w]
                face[a, w * n : (w + 1) * n, :] = layer.reshape(n, width)


def corner_kernel(block, axis, near, count, *refs):
    T, H, W, C = block
    got, outs = refs[:near], refs[near:]
    other = T if axis == "ta" else H

    def put(k, layer):
        for a in range(got[0].shape[0]):
            for w in range(W):
                at = (w * other + layer) * C
                outs[k][a, w * near * C : (w + 1) * near * C, :] = jnp.concatenate(
                    [r[a, at : at + C, :] for r in got], axis=0
                )

    by_parity(axis, count, other, put)


def second_kernel(block, axis, near, count, own_ref, *refs):
    T, H, W, C = block
    got, outs = refs[:near], refs[near:]

    def put(k, layer):
        for a in range(own_ref.shape[0]):
            for w in range(W):
                if axis == "ta":
                    r = (w * T + layer) * H * C
                    parts = [own_ref[a, r : r + H * C, :]]
                    at = (w * T + layer) * C
                else:
                    parts = []
                    for t in range(T):
                        r = ((w * T + t) * H + layer) * C
                        parts.append(own_ref[a, r : r + C, :])
                    at = (w * H + layer) * C
                parts += [r[a, at : at + C, :] for r in got]
                n = outs[k].shape[1] // W
                outs[k][a, w * n : (w + 1) * n, :] = jnp.concatenate(parts, axis=0)

    by_parity(axis, count, T if axis == "ta" else H, put)


def column_kernel(block, count, *refs):
    _, _, W, _ = block
    pieces, outs = refs[: len(refs) - count], refs[len(refs) - count :]

    def put(k, w):
        for a in range(outs[k].shape[0]):
            at = 0
            for r in pieces:
                n = r.shape[1] // W
                outs[k][a, at : at + n, :] = r[a, w * n : (w + 1) * n, :]
                at += n

    by_parity("wa", count, W, put)


def local(kernel, out_shape, operands, space=pltpu.VMEM, out_space=pltpu.VMEM, **kw):
    place = pl.BlockSpec(memory_space=space)
    made = pl.pallas_call(
        kernel,
        out_shape=out_shape,
        in_specs=[place] * len(operands),
        out_specs=[pl.BlockSpec(memory_space=out_space)] * len(out_shape),
        compiler_params=pltpu.CompilerParams(vmem_limit_bytes=16 << 20),
        **kw,
    )(*operands)
    return list(made)


def column_swap(pieces, block, counts, name):
    k, _, width = pieces[0].shape
    n = sum(p.shape[1] for p in pieces) // block[2]
    sends = local(
        functools.partial(column_kernel, block, counts[2]),
        [pltpu.VMEM((k, n, width), pieces[0].dtype)] * counts[2],
        pieces,
        name=name,
    )
    return swap("wa", sends)


def spread(own, got, block, counts, name):
    T, _, W, C = block
    k, _, width = own.shape
    more = swap(
        "ha",
        local(
            functools.partial(second_kernel, block, "ha", counts[0], counts[1]),
            [pltpu.VMEM((k, W * (T + counts[0]) * C, width), own.dtype)] * counts[1],
            [own] + got,
            name=name + "_second",
        ),
    )
    near = column_swap([own] + got, block, counts, name + "_near")
    far = column_swap(more, block, counts, name + "_far")
    return [own], got, near, more, far


def spread_early(own, ha, ta, axis, block, counts, name):
    _, _, W, C = block
    k, _, width = own.shape
    got, near_count, count = (ha, counts[1], counts[0]) if axis == "ta" else (ta, counts[0], counts[1])
    corners = swap(
        axis,
        local(
            functools.partial(corner_kernel, block, axis, near_count, count),
            [pltpu.VMEM((k, W * near_count * C, width), own.dtype)] * count,
            got,
            name=name + "_corner",
        ),
    )
    near = [own] + ha + ta
    near += column_swap(near, block, counts, name + "_near")
    far = corners + column_swap(corners, block, counts, name + "_far")
    return near, far


def piece_coords(block, counts, axis):
    T, H, W, C = block
    marks = [(EVEN, ODD)[:n] for n in counts]
    ts, hs, ws = list(range(T)), list(range(H)), list(range(W))

    def piece(cells):
        return np.array([[cell + (w,) for cell in cells] for w in ws], np.int32)

    near = [piece([(t, h) for t in ts for h in hs])]
    near += [piece([(t, m) for t in ts]) for m in marks[1]]
    near += [piece([(m, h) for h in hs]) for m in marks[0]]
    if axis == "ta":
        far = [piece([(m, h) for h in marks[1]]) for m in marks[0]]
    else:
        far = [piece([(t, m) for t in marks[0]]) for m in marks[1]]
    groups = []
    for part in (near, far):
        column = np.concatenate([p[0] for p in part], axis=0)
        rows = [p.reshape(-1, 3) for p in part]
        for m in marks[2]:
            rows.append(column.copy())
            rows[-1][:, 2] = m
        groups.append(np.repeat(np.concatenate(rows, axis=0), C, axis=0))
    return groups


def codes_kernel(block, grids, own_is_key, *refs):
    sources, (code_ref, closed_ref), bufs, sems = refs[:4], refs[4:6], refs[6:10], refs[10]
    copies = [pltpu.make_async_copy(s, b, sems.at[i]) for i, (s, b) in enumerate(zip(sources, bufs))]
    for copy in copies:
        copy.start()
    for copy in copies:
        copy.wait()
    own_ref, outer_ref, valid_ref, radius_ref = bufs
    r = radius_ref[...]
    closed = 8 + (1 - r[0:1]) + 2 * (1 - r[1:2]) + 4 * (1 - r[2:3])
    closed_ref[...] = jnp.broadcast_to(closed, closed_ref.shape)
    own_all, outer_all = own_ref[...], outer_ref[...]
    if own_is_key:
        own_all = own_all.T
    else:
        outer_all = outer_all.T
    code = same = bad = 0
    for a, axis in enumerate(AXES):
        length, grid = block[a], grids[a]

        def line(i):
            i = i % grid
            if a == 0:
                return valid_ref[i, 1:2, 1:2]
            if a == 1:
                return valid_ref[1, 1:2, i : i + 1]
            return valid_ref[1, i : i + 1, 1:2]

        low = 1 - line(0)
        high = grid - 3 + line(-1) + line(-2)
        index = lax.axis_index(axis)
        odd = lax.rem(index, 2)
        at_even = jnp.where(odd == 1, -1, length)
        at_odd = jnp.where(odd == 1, length, -1)
        if own_is_key:
            own, outer = own_all[:, a : a + 1], outer_all[a : a + 1, :]
        else:
            own, outer = own_all[a : a + 1, :], outer_all[:, a : a + 1]
        outer = jnp.where(outer == EVEN, at_even, jnp.where(outer == ODD, at_odd, outer))
        place = outer + index * length
        outside = jnp.where((place >= 0) & (place < grid), 0, 8)
        apart = jnp.abs(own - outer)
        same = same | apart
        code = code | jnp.where(apart > 1, 8, apart << a) | outside
        key = own + index * length if own_is_key else place
        bad = bad | jnp.where((key >= low) & (key <= high), 0, 8)
    code_ref[...] = code | jnp.where(same == 0, 0, bad)


NT = (((1,), (1,)), ((), ()))
NN = (((1,), (0,)), ((), ()))
TN = (((0,), (0,)), ((), ()))
STEP = 64


def dot(a, b, dims):
    return lax.dot_general(a, b, dims, preferred_element_type=jnp.float32)


def gather(groups, which, cols):
    parts = []
    for refs, pad in groups:
        parts += [r[which, :, cols] for r in refs]
        if pad:
            parts.append(jnp.zeros((pad, parts[0].shape[1]), parts[0].dtype))
    return jnp.concatenate(parts, axis=0)


def put_tiles(ref, value, cols):
    T, H, W, C, _ = ref.shape
    value = value.astype(ref.dtype)
    for w in range(W):
        for t in range(T):
            r = (w * T + t) * H * C
            ref[t, :, w, :, cols] = value[r : r + H * C].reshape(H, C, value.shape[1])


def products_kernel(cfg, closed_ref, code_ref, own_ref, *rest):
    depth, pad, first, own_is_key = cfg
    groups, (s_ref, g_ref) = [(rest[:-2], pad)], rest[-2:]
    factor = LOG2E / math.sqrt(depth)
    for h in range(s_ref.shape[0]):
        cols = slice(h * depth, (h + 1) * depth)
        own, outer = ([own_ref[i, :, cols] for i in (0, 1)], [gather(groups, i, cols) for i in (0, 1)])
        if own_is_key:
            code = code_ref[:, first : first + s_ref.shape[2]]
            scores, grads = (dot(a, b, NT) for a, b in zip(own, outer))
        else:
            code = code_ref[first : first + s_ref.shape[1], :]
            scores, grads = (dot(b, a, NT) for a, b in zip(own, outer))
        s_ref[h] = jnp.where((code & closed_ref[0:1, h : h + 1]) == 0, scores * factor, NEG)
        g_ref[h] = grads


def near_kernel(cfg, closed_ref, code_ref, own_ref, *rest):
    s_ref, g_ref, m_ref = rest[-3:]
    heads, wide, _ = s_ref.shape
    products_kernel(cfg, closed_ref, code_ref, own_ref, *rest[:-1])
    for h in range(heads):
        bands = range(0, wide, STEP)
        peak = functools.reduce(jnp.maximum, [s_ref[h, r : r + STEP, :] for r in bands])
        peak = jnp.max(peak, axis=0, keepdims=True)
        total = part = 0.0
        for r in bands:
            raised = jnp.exp2(s_ref[h, r : r + STEP, :] - peak)
            total = total + raised
            part = part + raised * g_ref[h, r : r + STEP, :]
        m_ref[h, 0:1, :] = peak
        m_ref[h, 1:2, :] = jnp.sum(total, axis=0, keepdims=True)
        m_ref[h, 2:3, :] = jnp.sum(part, axis=0, keepdims=True)


def query_kernel(cfg, block, faces, closed_ref, code_ref, near_s_ref, near_g_ref, near_m_ref, *rest):
    heads, depth, pads, counts = cfg
    qd_ref, rest = rest[0], rest[1:]
    kv, rest = rest[: sum(counts)], rest[sum(counts) :]
    near, far = (kv[: counts[0]], pads[0]), (kv[counts[0] :], pads[1])
    dq_ref, stat_ref = rest[:2]
    first_refs = rest[2 : 2 + faces]
    s_ref, g_ref, d_ref, stat_rows = rest[2 + faces :]
    scale = 1.0 / math.sqrt(depth)
    wide = near_s_ref.shape[1]
    total_rows = code_ref.shape[0]
    stat_rows[...] = jnp.zeros(stat_rows.shape, jnp.float32)

    def columns(h):
        return slice(h * depth, (h + 1) * depth)

    def products(h):
        cols = columns(h)
        scores = dot(gather([far], 0, cols), qd_ref[0, :, cols], NT) * (scale * LOG2E)
        allowed = (code_ref[wide:, :] & closed_ref[0:1, h : h + 1]) == 0
        s_ref[h % 2] = jnp.where(allowed, scores, NEG)
        g_ref[h % 2] = dot(gather([far], 1, cols), qd_ref[1, :, cols], NT)

    products(0)
    for h in range(heads):
        if h + 1 < heads:
            products(h + 1)
        near_peak = near_m_ref[h, 0:1, :]
        scores, grads = s_ref[h % 2], g_ref[h % 2]
        peak = jnp.maximum(near_peak, jnp.max(scores, axis=0, keepdims=True))
        raised = jnp.exp2(scores - peak)
        lower = jnp.exp2(near_peak - peak)
        total = near_m_ref[h, 1:2, :] * lower + jnp.sum(raised, axis=0, keepdims=True)
        part = near_m_ref[h, 2:3, :] * lower + jnp.sum(raised * grads, axis=0, keepdims=True)
        drift = part / total
        logsum = peak + jnp.log2(total)
        stat_rows[h : h + 1, :] = logsum
        stat_rows[heads + h : heads + h + 1, :] = drift
        for r in range(0, total_rows, STEP):
            if r < wide:
                scores, grads = near_s_ref[h, r : r + STEP, :], near_g_ref[h, r : r + STEP, :]
            else:
                at = slice(r - wide, r - wide + STEP)
                scores, grads = s_ref[h % 2, at, :], g_ref[h % 2, at, :]
            attention = jnp.exp2(scores - logsum)
            d_ref[h % 2, r : r + STEP, :] = (attention * (grads - drift)).astype(jnp.bfloat16)
        cols = columns(h)
        put_tiles(dq_ref, dot(d_ref[h % 2], gather([near, far], 0, cols), TN) * scale, cols)
    stat_ref[0] = stat_rows[...].T
    T, H, W, C = block

    def put(k, t):
        for w in range(W):
            r = (w * T + t) * H * C
            first_refs[k][0, w * H * C : (w + 1) * H * C, :] = stat_ref[0, r : r + H * C, :]

    by_parity("ta", faces, T, put)


def statistics_rows(st, pads, block, counts):
    T, H, W, C = block
    na, nh, nw = counts
    own, ta, near = st[0], st[1 : 1 + na], st[1 + na : 1 + na + nw]
    ha, far = st[1 + na + nw : 1 + na + nw + nh], st[1 + na + nw + nh :]
    a, each = T * C, (T + na) * C
    lines = [own[0]]
    lines += [r[0, w * each : w * each + a, :] for r in ha for w in range(W)]
    lines += [r[0] for r in ta]
    cut = T * H * C
    for n, f in zip(near, far):
        lines.append(n[0, :cut, :])
        lines += [f[0, k * each : k * each + a, :] for k in range(nh)]
        lines.append(n[0, cut:, :])
    if pads[0]:
        lines.append(jnp.zeros((pads[0], own.shape[2]), jnp.float32))
    lines += [r[0, w * each + a : (w + 1) * each, :] for r in ha for w in range(W)]
    lines += [f[0, k * each + a : (k + 1) * each, :] for f in far for k in range(nh)]
    if pads[1]:
        lines.append(jnp.zeros((pads[1], own.shape[2]), jnp.float32))
    return jnp.concatenate(lines, axis=0)


def key_kernel(cfg, *refs):
    heads, depth, pads, counts, parts, split, block, axes = cfg
    products, dq_ref, refs = refs[: 2 * parts], refs[2 * parts], refs[2 * parts + 1 :]
    near, far, refs = refs[: counts[0]], refs[counts[0] : sum(counts)], refs[sum(counts) :]
    qd = [(near, pads[0]), (far, pads[1])]
    st, refs = refs[: 1 + 2 * axes[2] + axes[0] + axes[1]], refs[-8:]
    dq_out, dk_out, dv_out, row_ref, dk_ref, dv_ref, dq_sem, sems = refs
    scale = 1.0 / math.sqrt(depth)
    row_ref[...] = statistics_rows(st, pads, block, axes).T
    copies = [pltpu.make_async_copy(dq_ref, dq_out, dq_sem)]
    copies[0].start()
    for h in range(heads):
        cols = slice(h * depth, (h + 1) * depth)
        scores = jnp.concatenate([r[h] for r in products[0::2]], axis=1)
        grads = jnp.concatenate([r[h] for r in products[1::2]], axis=1)
        attention = jnp.exp2(scores - row_ref[h : h + 1, :])
        drift = row_ref[heads + h : heads + h + 1, :]
        score_grads = (attention * (grads - drift)).astype(jnp.bfloat16)
        put_tiles(dk_ref, dot(score_grads, gather(qd, 0, cols), NN) * scale, cols)
        put_tiles(dv_ref, dot(attention.astype(jnp.bfloat16), gather(qd, 1, cols), NN), cols)
        if (h + 1) % (heads // split) == 0:
            i = (h + 1) // (heads // split) - 1
            done = slice((h + 1 - heads // split) * depth, (h + 1) * depth)
            for j, (ref, out) in enumerate(((dk_ref, dk_out), (dv_ref, dv_out))):
                copies.append(
                    pltpu.make_async_copy(
                        ref.at[:, :, :, :, done], out.at[:, :, :, :, done], sems.at[j, i]
                    )
                )
                copies[-1].start()
    for copy in copies:
        copy.wait()


def per_device(queries, key_states, value_states, output_cotangent, tile_valid, window_radius):
    T, H, W, C, width = queries.shape
    block = (T, H, W, C)
    heads = window_radius.shape[0]
    depth = width // heads
    sizes = tuple(lax.axis_size(a) for a in AXES)
    grids = tuple(n * b for n, b in zip(sizes, block))
    counts = tuple(len(matchings(a)) for a in AXES)
    rows = T * H * W * C

    kind = jax.ShapeDtypeStruct
    args = [
        pltpu.with_memory_space_constraint(x, pltpu.HBM)
        for x in (key_states, value_states, queries, output_cotangent)
    ]

    def prepared(pair, axes, name):
        plan = [(x, k) for x in axes for k in range(counts[AXES.index(x)])]
        made = local(
            functools.partial(prepare_kernel, block, plan),
            [pltpu.VMEM((2, W * C * (T if x == "ha" else H), width), jnp.bfloat16) for x, _ in plan]
            + [pltpu.VMEM((2, rows, width), jnp.bfloat16)],
            pair,
            space=pltpu.HBM,
            scratch_shapes=[
                pltpu.VMEM((2, T, H, W, C, width), jnp.bfloat16),
                pltpu.SemaphoreType.DMA((2, T)),
            ],
            name=name + "_prepare",
        )
        got, at = [], 0
        for x in axes:
            n = counts[AXES.index(x)]
            got.append(swap(x, made[at : at + n]))
            at += n
        return made[-1], got

    kv, (kv_ha, kv_ta) = prepared(args[:2], ("ha", "ta"), "kv")
    qd, (qd_ta, qd_ha) = prepared(args[2:], ("ta", "ha"), "qd")
    near, far = spread_early(kv, kv_ha, kv_ta, "ta", block, counts, "kv")
    qd_near, qd_far = spread_early(qd, qd_ha, qd_ta, "ha", block, counts, "qd")

    def table(axis):
        groups = piece_coords(block, counts, axis)
        pads = [-len(g) % 128 for g in groups]
        out = np.full((8, sum(len(g) + p for g, p in zip(groups, pads))), -(1 << 20), np.int32)
        at = 0
        for g, p in zip(groups, pads):
            out[:3, at : at + len(g)] = g.T
            at += len(g) + p
        return groups, pads, out

    groups, pads, outer_k = table("ta")
    _, pads_q, outer_q = table("ha")
    inner = np.zeros((8, rows), np.int32)
    inner[:3] = groups[0][:rows].T
    wide, all_wide = len(groups[0]) + pads[0], outer_k.shape[1]
    native = kind(queries.shape, jnp.bfloat16)
    lanes = -(-2 * heads // 128) * 128

    def codes(outer, own_is_key, name):
        tables = [inner, outer, tile_valid.transpose(0, 2, 1), window_radius.T]
        shape = (rows, all_wide) if own_is_key else (all_wide, rows)
        return local(
            functools.partial(codes_kernel, block, grids, own_is_key),
            [pltpu.VMEM(shape, jnp.int32), pltpu.VMEM((8, heads), jnp.int32)],
            [pltpu.with_memory_space_constraint(jnp.asarray(x), pltpu.HBM) for x in tables],
            space=pltpu.HBM,
            scratch_shapes=[pltpu.VMEM(x.shape, jnp.int32) for x in tables]
            + [pltpu.SemaphoreType.DMA((len(tables),))],
            name=name,
        )

    query_code, closed = codes(outer_k, False, "query_codes")
    key_code, key_closed = codes(outer_q, True, "key_codes")
    near_products = local(
        functools.partial(near_kernel, (depth, pads[0], 0, False)),
        [pltpu.VMEM((heads, wide, rows), jnp.float32)] * 2
        + [pltpu.VMEM((heads, 8, rows), jnp.float32)],
        [closed, query_code, qd] + near,
        name="query_products",
    )
    kcfg = (heads, depth, pads, (len(near), len(far)))
    made = local(
        functools.partial(query_kernel, kcfg, block, counts[0]),
        [pltpu.VMEM(queries.shape, jnp.bfloat16), pltpu.VMEM((1, rows, lanes), jnp.float32)]
        + [pltpu.VMEM((1, W * H * C, lanes), jnp.float32)] * counts[0],
        [closed, query_code] + near_products + [qd] + near + far,
        scratch_shapes=[pltpu.VMEM((2, all_wide - wide, rows), jnp.float32)] * 2
        + [pltpu.VMEM((2, all_wide, rows), jnp.bfloat16), pltpu.VMEM((lanes, rows), jnp.float32)],
        name="query_side",
    )
    query_gradient, stats = made[:2]
    st_ta = swap("ta", made[2:])
    stat_pieces = sum(spread(stats, st_ta, block, counts, "st"), [])
    products = []
    for i, pieces in enumerate((qd_near, qd_far)):
        products += local(
            functools.partial(products_kernel, (depth, pads_q[i], i * wide, True)),
            [pltpu.VMEM((heads, rows, all_wide - wide if i else wide), jnp.float32)] * 2,
            [key_closed, key_code, kv] + pieces,
            name=f"key_products_{i}",
        )
    split = math.gcd(heads, 6)
    lengths = (len(qd_near), len(qd_far))
    query_gradient, key_gradient, value_gradient = local(
        functools.partial(
            key_kernel, (heads, depth, pads_q, lengths, 2, split, block, counts)
        ),
        [native] * 3,
        products + [query_gradient] + qd_near + qd_far + stat_pieces,
        out_space=pltpu.HBM,
        scratch_shapes=[pltpu.VMEM((lanes, all_wide), jnp.float32)]
        + [pltpu.VMEM(queries.shape, jnp.bfloat16)] * 2
        + [pltpu.SemaphoreType.DMA, pltpu.SemaphoreType.DMA((2, split))],
        name="key_side",
    )
    return (query_gradient, key_gradient, value_gradient)


def solution(mesh):
    split = P("ta", "ha", "wa", None, None)

    return jax.shard_map(
        per_device,
        mesh=mesh,
        in_specs=(split, split, split, split, P(), P()),
        out_specs=(split, split, split),
        check_vma=False,
    )
```

time: 64.6 us -> 56.9 us (0.88)
  waiting for transfers between devices: 32.4 us -> 20 us
  starting transfers between devices: 17.8 us -> 21.9 us
    ppermute x20 -> x22, waiting for transfers between devices: 32.4 us -> 20 us  [swap(): got.append(lax.ppermute(sends[k], axes, pairs))]
    ppermute x20 -> x22, starting transfers between devices: 17.8 us -> 21.9 us  [swap(): got.append(lax.ppermute(sends[k], axes, pairs))]
    pallas_call x17 -> x18, Pallas kernels: 13.4 us -> 13.8 us  [local(): pl.pallas_call(kernel, out_shape=out_shape, in_specs=[place] * len(operan...]
  transfers between devices with their start and end apart: 20 -> 22, of which waited for: 10 -> 10; matrix products, arithmetic and copies ran while one was open for 0% -> 0% of each run, Pallas kernels for 15% -> 18%
where the time goes in v5:
time: 56.9 us; the launch traced here: 56.5 us
  starting transfers between devices  21.9 us (38%)
  waiting for transfers between devices  20 us (35%)
  Pallas kernels  13.8 us (24%)
  between operations  0.8 us (1%)
    ppermute x22, starting transfers between devices, swap(): got.append(lax.ppermute(sends[k], axes, pairs))  21.9 us
    ppermute x22, waiting for transfers between devices, swap(): got.append(lax.ppermute(sends[k], axes, pairs))  20 us
    pallas_call x18, Pallas kernels, local(): pl.pallas_call(kernel, out_shape=out_shape, in_specs=[place] * len(operan...  13.8 us
  transfers between devices with their start and end apart: 22, of which 10 were waited for; matrix products, arithmetic and copies ran while one was open for 0% of the time, Pallas kernels for 18%

profile of v5, /device:TPU:21, one launch (start us, length us, event | category | flops | bytes accessed | tf_op | source)
XLA Modules:
  0.0 56.5 jit_solution(5719869864940114995)
XLA Ops:
  0.6 1.4 %kv_prepare.1 = (bf16[2,32,1536]{2,1,0:T(8,128)(2,1)S(1)}, bf16[2,32,1536]{2,1,0:T(8,128)(2,1)S(1)}, bf16[2,32,1536]{2,1,0:T(8,128)(2,1)S(1)}, bf16[2,32,1536]{2,1,0:T(8,128)(2,1)S(1)}, bf16[2,128,1536]{2,1,0:T(8,128)(2,1)S(1)}) custom-call(bf16[4,4,2,4,1536]{4,3,2,1,0:T(4,128)(2,1)} %refs_0_.4, bf16[4,4,2,4,1536]{4,3,2,1,0:T(4,128)(2,1)} %refs_1_.4), custom_call_target="tpu_custom_call" | custom-call | tf_op jit(solution)/shard_map/kv_prepare/pallas_call | solution.py:146
  2.0 1.3 %collective-permute-start.8 = (bf16[2,32,1536]{2,1,0:T(8,128)(2,1)S(1)}, bf16[2,32,1536]{2,1,0:T(8,128)(2,1)S(1)}, u32[]{:S(2)}, u32[]{:S(2)}) collective-permute-start(bf16[2,32,1536]{2,1,0:T(8,128)(2,1)S(1)} %get-tuple-element.50), channel_id=1, source_target_pairs={{0,2},{4,6},{1,3},{5,7},{2,0},{6,4},{3,1},{7,5},{8,10},{12,14},{9,... | collective-permute-start | bytes 589832 | tf_op jit(solution)/shard_map/ppermute | solution.py:38
  3.3 0.2 collective-permute-start.9
  3.5 1.3 %collective-permute-start.10 = (bf16[2,32,1536]{2,1,0:T(8,128)(2,1)S(1)}, bf16[2,32,1536]{2,1,0:T(8,128)(2,1)S(1)}, u32[]{:S(2)}, u32[]{:S(2)}) collective-permute-start(bf16[2,32,1536]{2,1,0:T(8,128)(2,1)S(1)} %get-tuple-element.52), channel_id=1, source_target_pairs={{0,8},{16,24},{1,9},{17,25},{8,0},{24,16},{9,1},{25,17},{2,10},{18... | collective-permute-start | bytes 589832 | tf_op jit(solution)/shard_map/ppermute | solution.py:38
  4.8 0.0 collective-permute-start.11
  4.8 1.4 %qd_prepare.1 = (bf16[2,32,1536]{2,1,0:T(8,128)(2,1)S(1)}, bf16[2,32,1536]{2,1,0:T(8,128)(2,1)S(1)}, bf16[2,32,1536]{2,1,0:T(8,128)(2,1)S(1)}, bf16[2,32,1536]{2,1,0:T(8,128)(2,1)S(1)}, bf16[2,128,1536]{2,1,0:T(8,128)(2,1)S(1)}) custom-call(bf16[4,4,2,4,1536]{4,3,2,1,0:T(4,128)(2,1)} %refs_0_.5, bf16[4,4,2,4,1536]{4,3,2,1,0:T(4,128)(2,1)} %refs_1_.5), custom_call_target="tpu_custom_call" | custom-call | tf_op jit(solution)/shard_map/qd_prepare/pallas_call | solution.py:146
  6.1 1.7 %collective-permute-start.2 = (bf16[2,32,1536]{2,1,0:T(8,128)(2,1)S(1)}, bf16[2,32,1536]{2,1,0:T(8,128)(2,1)S(1)}, u32[]{:S(2)}, u32[]{:S(2)}) collective-permute-start(bf16[2,32,1536]{2,1,0:T(8,128)(2,1)S(1)} %get-tuple-element.40), channel_id=1, source_target_pairs={{0,8},{16,24},{1,9},{17,25},{8,0},{24,16},{9,1},{25,17},{2,10},{18... | collective-permute-start | bytes 589832 | tf_op jit(solution)/shard_map/ppermute | solution.py:38
  7.9 0.0 collective-permute-done.8.refs_1_.rest_1_.refs_0_.rest_2_
  7.9 0.2 collective-permute-start.3
  8.1 3.9 %collective-permute-done.9.refs_2_.rest_2_.refs_1_.rest_3_ = bf16[2,32,1536]{2,1,0:T(8,128)(2,1)S(1)} collective-permute-done((bf16[2,32,1536]{2,1,0:T(8,128)(2,1)S(1)}, bf16[2,32,1536]{2,1,0:T(8,128)(2,1)S(1)}, u32[]{:S(2)}, u32[]{:S(2)}) %collective-permute-start.9) | collective-permute-done | bytes 196640 | tf_op jit(solution)/shard_map/ppermute | solution.py:38
  12.0 0.0 collective-permute-start
  12.0 0.0 collective-permute-done.10.refs_3_.rest_3_.rest_4_
  12.0 2.2 %collective-permute-start.1 = (bf16[2,32,1536]{2,1,0:T(8,128)(2,1)S(1)}, bf16[2,32,1536]{2,1,0:T(8,128)(2,1)S(1)}, u32[]{:S(2)}, u32[]{:S(2)}) collective-permute-start(bf16[2,32,1536]{2,1,0:T(8,128)(2,1)S(1)} %get-tuple-element.39), channel_id=1, source_target_pairs={{2,4},{3,5},{0,1},{6,7},{4,2},{5,3},{1,0},{7,6},{10,12},{11,13},{8... | collective-permute-start | bytes 589832 | tf_op jit(solution)/shard_map/ppermute | solution.py:38
  14.2 0.0 collective-permute-done.11.refs_4_.rest_4_.rest_5_
  14.2 0.1 kv_near.1
  14.2 1.9 %collective-permute-start.12 = (bf16[2,128,1536]{2,1,0:T(8,128)(2,1)S(1)}, bf16[2,128,1536]{2,1,0:T(8,128)(2,1)S(1)}, u32[]{:S(2)}, u32[]{:S(2)}) collective-permute-start(bf16[2,128,1536]{2,1,0:T(8,128)(2,1)S(1)} %kv_near.1), channel_id=1, source_target_pairs={{0,1},{1,0},{2,3},{3,2},{4,5},{5,4},{6,7},{7,6},{8,9},{9,8},{10,11... | collective-permute-start | bytes 2359304 | tf_op jit(solution)/shard_map/ppermute | solution.py:38
  16.1 0.0 collective-permute-done.2.refs_3_.rest_3_.refs_0_.refs_8_
  16.1 0.0 collective-permute-done.3.refs_4_.rest_4_.refs_1_.refs_9_
  16.1 0.8 %collective-permute-done.refs_1_.rest_1_.refs_6_ = bf16[2,32,1536]{2,1,0:T(8,128)(2,1)S(1)} collective-permute-done((bf16[2,32,1536]{2,1,0:T(8,128)(2,1)S(1)}, bf16[2,32,1536]{2,1,0:T(8,128)(2,1)S(1)}, u32[]{:S(2)}, u32[]{:S(2)}) %collective-permute-start) | collective-permute-done | bytes 196640 | tf_op jit(solution)/shard_map/ppermute | solution.py:38
  16.9 5.2 %collective-permute-done.1.refs_2_.rest_2_.refs_7_ = bf16[2,32,1536]{2,1,0:T(8,128)(2,1)S(1)} collective-permute-done((bf16[2,32,1536]{2,1,0:T(8,128)(2,1)S(1)}, bf16[2,32,1536]{2,1,0:T(8,128)(2,1)S(1)}, u32[]{:S(2)}, u32[]{:S(2)}) %collective-permute-start.1) | collective-permute-done | bytes 196640 | tf_op jit(solution)/shard_map/ppermute | solution.py:38
  22.1 0.1 qd_near.1
  22.2 2.2 %collective-permute-start.4 = (bf16[2,128,1536]{2,1,0:T(8,128)(2,1)S(1)}, bf16[2,128,1536]{2,1,0:T(8,128)(2,1)S(1)}, u32[]{:S(2)}, u32[]{:S(2)}) collective-permute-start(bf16[2,128,1536]{2,1,0:T(8,128)(2,1)S(1)} %qd_near.1), channel_id=1, source_target_pairs={{0,1},{1,0},{2,3},{3,2},{4,5},{5,4},{6,7},{7,6},{8,9},{9,8},{10,11... | collective-permute-start | bytes 2359304 | tf_op jit(solution)/shard_map/ppermute | solution.py:38
  24.4 0.1 kv_corner.1
  24.4 1.4 %collective-permute-start.13 = (bf16[2,16,1536]{2,1,0:T(8,128)(2,1)S(1)}, bf16[2,16,1536]{2,1,0:T(8,128)(2,1)S(1)}, u32[]{:S(2)}, u32[]{:S(2)}) collective-permute-start(bf16[2,16,1536]{2,1,0:T(8,128)(2,1)S(1)} %get-tuple-element.57), channel_id=1, source_target_pairs={{0,8},{16,24},{1,9},{17,25},{8,0},{24,16},{9,1},{25,17},{2,10},{18... | collective-permute-start | bytes 294920 | tf_op jit(solution)/shard_map/ppermute | solution.py:38
  25.8 0.0 collective-permute-start.14
  25.8 0.1 qd_corner.1
  25.9 0.1 collective-permute-start.5
  26.0 2.9 %collective-permute-done.13.refs_0_.rest_7_ = bf16[2,16,1536]{2,1,0:T(8,128)(2,1)S(1)} collective-permute-done((bf16[2,16,1536]{2,1,0:T(8,128)(2,1)S(1)}, bf16[2,16,1536]{2,1,0:T(8,128)(2,1)S(1)}, u32[]{:S(2)}, u32[]{:S(2)}) %collective-permute-start.13) | collective-permute-done | bytes 98336 | tf_op jit(solution)/shard_map/ppermute | solution.py:38
  28.8 0.2 collective-permute-start.6
  29.0 0.8 %collective-permute-done.14.refs_1_.rest_8_ = bf16[2,16,1536]{2,1,0:T(8,128)(2,1)S(1)} collective-permute-done((bf16[2,16,1536]{2,1,0:T(8,128)(2,1)S(1)}, bf16[2,16,1536]{2,1,0:T(8,128)(2,1)S(1)}, u32[]{:S(2)}, u32[]{:S(2)}) %collective-permute-start.14) | collective-permute-done | bytes 98336 | tf_op jit(solution)/shard_map/ppermute | solution.py:38
  29.8 1.2 %collective-permute-start.15 = (bf16[2,16,1536]{2,1,0:T(8,128)(2,1)S(1)}, bf16[2,16,1536]{2,1,0:T(8,128)(2,1)S(1)}, u32[]{:S(2)}, u32[]{:S(2)}) collective-permute-start(bf16[2,16,1536]{2,1,0:T(8,128)(2,1)S(1)} %kv_far.1), channel_id=1, source_target_pairs={{0,1},{1,0},{2,3},{3,2},{4,5},{5,4},{6,7},{7,6},{8,9},{9,8},{10,11... | collective-permute-start | bytes 294920 | tf_op jit(solution)/shard_map/ppermute | solution.py:38
  31.1 0.0 collective-permute-done.5.refs_0_.rest_0_.refs_11_
  31.1 2.1 %collective-permute-done.6.refs_1_.rest_1_.refs_12_ = bf16[2,16,1536]{2,1,0:T(8,128)(2,1)S(1)} collective-permute-done((bf16[2,16,1536]{2,1,0:T(8,128)(2,1)S(1)}, bf16[2,16,1536]{2,1,0:T(8,128)(2,1)S(1)}, u32[]{:S(2)}, u32[]{:S(2)}) %collective-permute-start.6) | collective-permute-done | bytes 98336 | tf_op jit(solution)/shard_map/ppermute | solution.py:38
  33.2 2.1 %collective-permute-start.7 = (bf16[2,16,1536]{2,1,0:T(8,128)(2,1)S(1)}, bf16[2,16,1536]{2,1,0:T(8,128)(2,1)S(1)}, u32[]{:S(2)}, u32[]{:S(2)}) collective-permute-start(bf16[2,16,1536]{2,1,0:T(8,128)(2,1)S(1)} %qd_far.1), channel_id=1, source_target_pairs={{0,1},{1,0},{2,3},{3,2},{4,5},{5,4},{6,7},{7,6},{8,9},{9,8},{10,11... | collective-permute-start | bytes 294920 | tf_op jit(solution)/shard_map/ppermute | solution.py:38
  35.3 1.9 %query_codes.1 = (s32[512,128]{1,0:T(8,128)S(1)}, s32[8,12]{1,0:T(8,128)S(1)}) custom-call(s32[8,128]{1,0:T(8,128)} %constant.6.clone.refs_0_, s32[8,512]{1,0:T(8,128)} %constant.7.clone.refs_1_, s32[16,4,16]{2,1,0:T(4,128)} %bitcast.2, s32[3,12]{1,0:T(4,128)} %bitcast.4), custom_call_target="tpu_custom_call" | custom-call | tf_op jit(solution)/shard_map/query_codes/pallas_call | solution.py:146
  37.3 0.0 collective-permute-done.12.rest_5_.rest_6_
  37.3 1.3 %query_products.1 = (f32[12,384,128]{2,1,0:T(8,128)S(1)}, f32[12,384,128]{2,1,0:T(8,128)S(1)}, f32[12,8,128]{2,1,0:T(8,128)S(1)}) custom-call(s32[8,12]{1,0:T(8,128)S(1)} %get-tuple-element.48.closed_ref, s32[512,128]{1,0:T(8,128)S(1)} %get-tuple-element.49.code_ref, bf16[2,128,1536]{2,1,0:T(8,128)(2,1)S(1)} %get-tuple-element.37.refs_0_.rest_0_.own_ref.refs_5_, ...), custom_call_target="tpu_custom_call" | custom-call | tf_op jit(solution)/shard_map/query_products/pallas_call | solution.py:146
  38.6 0.0 collective-permute-done.15.rest_9_
  38.6 2.5 %query_side.1 = (bf16[4,4,2,4,1536]{4,3,2,1,0:T(4,128)(2,1)S(1)}, f32[1,128,128]{2,1,0:T(8,128)S(1)}, f32[1,32,128]{2,1,0:T(8,128)S(1)}, f32[1,32,128]{2,1,0:T(8,128)S(1)}) custom-call(s32[8,12]{1,0:T(8,128)S(1)} %get-tuple-element.48.closed_ref, s32[512,128]{1,0:T(8,128)S(1)} %get-tuple-element.49.code_ref, ...), custom_call_target="tpu_custom_call" | custom-call | tf_op jit(solution)/shard_map/query_side/pallas_call | solution.py:146
  41.1 1.4 %collective-permute-start.16 = (f32[1,32,128]{2,1,0:T(8,128)S(1)}, f32[1,32,128]{2,1,0:T(8,128)S(1)}, u32[]{:S(2)}, u32[]{:S(2)}) collective-permute-start(f32[1,32,128]{2,1,0:T(8,128)S(1)} %get-tuple-element.61), channel_id=1, source_target_pairs={{0,8},{16,24},{1,9},{17,25},{8,0},{24,16},{9,1},{25,17},{2,10},{18... | collective-permute-start | bytes 49160 | tf_op jit(solution)/shard_map/ppermute | solution.py:38
  42.5 0.0 collective-permute-start.17
  42.5 1.3 %collective-permute-done.16.refs_1_.refs_0_.refs_15_ = f32[1,32,128]{2,1,0:T(8,128)S(1)} collective-permute-done((f32[1,32,128]{2,1,0:T(8,128)S(1)}, f32[1,32,128]{2,1,0:T(8,128)S(1)}, u32[]{:S(2)}, u32[]{:S(2)}) %collective-permute-start.16) | collective-permute-done | bytes 16416 | tf_op jit(solution)/shard_map/ppermute | solution.py:38
  43.8 1.3 %collective-permute-done.17.refs_2_.refs_1_.refs_16_ = f32[1,32,128]{2,1,0:T(8,128)S(1)} collective-permute-done((f32[1,32,128]{2,1,0:T(8,128)S(1)}, f32[1,32,128]{2,1,0:T(8,128)S(1)}, u32[]{:S(2)}, u32[]{:S(2)}) %collective-permute-start.17) | collective-permute-done | bytes 16416 | tf_op jit(solution)/shard_map/ppermute | solution.py:38
  45.1 0.1 collective-permute-start.19
  45.2 0.3 collective-permute-start.20
  45.4 1.7 %collective-permute-start.18 = (f32[1,96,128]{2,1,0:T(8,128)S(1)}, f32[1,96,128]{2,1,0:T(8,128)S(1)}, u32[]{:S(2)}, u32[]{:S(2)}) collective-permute-start(f32[1,96,128]{2,1,0:T(8,128)S(1)} %st_near.1), channel_id=1, source_target_pairs={{0,1},{1,0},{2,3},{3,2},{4,5},{5,4},{6,7},{7,6},{8,9},{9,8},{10,11... | collective-permute-start | bytes 147464 | tf_op jit(solution)/shard_map/ppermute | solution.py:38
  47.2 0.7 %collective-permute-done.19.refs_0_.refs_18_ = f32[1,48,128]{2,1,0:T(8,128)S(1)} collective-permute-done((f32[1,48,128]{2,1,0:T(8,128)S(1)}, f32[1,48,128]{2,1,0:T(8,128)S(1)}, u32[]{:S(2)}, u32[]{:S(2)}) %collective-permute-start.19) | collective-permute-done | bytes 24608 | tf_op jit(solution)/shard_map/ppermute | solution.py:38
  47.8 1.0 %collective-permute-done.20.refs_1_.refs_19_ = f32[1,48,128]{2,1,0:T(8,128)S(1)} collective-permute-done((f32[1,48,128]{2,1,0:T(8,128)S(1)}, f32[1,48,128]{2,1,0:T(8,128)S(1)}, u32[]{:S(2)}, u32[]{:S(2)}) %collective-permute-start.20) | collective-permute-done | bytes 24608 | tf_op jit(solution)/shard_map/ppermute | solution.py:38
  48.8 2.6 %collective-permute-start.21 = (f32[1,48,128]{2,1,0:T(8,128)S(1)}, f32[1,48,128]{2,1,0:T(8,128)S(1)}, u32[]{:S(2)}, u32[]{:S(2)}) collective-permute-start(f32[1,48,128]{2,1,0:T(8,128)S(1)} %st_far.1), channel_id=1, source_target_pairs={{0,1},{1,0},{2,3},{3,2},{4,5},{5,4},{6,7},{7,6},{8,9},{9,8},{10,11... | collective-permute-start | bytes 73736 | tf_op jit(solution)/shard_map/ppermute | solution.py:38
  51.4 1.3 %key_codes.1 = (s32[128,512]{1,0:T(8,128)S(1)}, s32[8,12]{1,0:T(8,128)S(1)}) custom-call(s32[8,128]{1,0:T(8,128)} %constant.6.clone.refs_0_, s32[8,512]{1,0:T(8,128)} %constant.8.clone.refs_1_, s32[16,4,16]{2,1,0:T(4,128)} %bitcast.3, s32[3,12]{1,0:T(4,128)} %bitcast.5), custom_call_target="tpu_custom_call" | custom-call | tf_op jit(solution)/shard_map/key_codes/pallas_call | solution.py:146
  52.7 0.0 collective-permute-done.7.rest_2_.refs_13_
  52.7 0.4 key_products_1.1
  53.1 0.0 collective-permute-done.4.rest_5_.refs_10_
  53.1 1.1 %key_products_0.1 = (f32[12,128,384]{2,1,0:T(8,128)S(1)}, f32[12,128,384]{2,1,0:T(8,128)S(1)}) custom-call(s32[8,12]{1,0:T(8,128)S(1)} %get-tuple-element.34.closed_ref, s32[128,512]{1,0:T(8,128)S(1)} %get-tuple-element.35.code_ref, bf16[2,128,1536]{2,1,0:T(8,128)(2,1)S(1)} %get-tuple-element.36.own_ref.refs_0_.rest_0_.rest_1_, ...), custom_call_target="tpu_custom_call" | custom-call | tf_op jit(solution)/shard_map/key_products_0/pallas_call | solution.py:146
  54.2 0.0 collective-permute-done.21.refs_20_
  54.2 0.0 collective-permute-done.18.refs_17_
  54.2 2.3 %key_side.1 = (bf16[4,4,2,4,1536]{4,3,2,1,0:T(4,128)(2,1)}, bf16[4,4,2,4,1536]{4,3,2,1,0:T(4,128)(2,1)}, bf16[4,4,2,4,1536]{4,3,2,1,0:T(4,128)(2,1)}) custom-call(f32[12,128,384]{2,1,0:T(8,128)S(1)} %get-tuple-element.42.refs_0_, f32[12,128,384]{2,1,0:T(8,128)S(1)} %get-tuple-element.43.refs_1_, f32[12,128,128]{2,1,0:T(8,128)S(1)} %get-tuple-element.46.refs_2_, ...), custom_call_target="tpu_custom_call" | custom-call | tf_op jit(solution)/shard_map/key_side/pallas_call | solution.py:146
  (5 shorter events, 0.0 us)
Async XLA Ops:
  2.0 5.9 %collective-permute-start.8 = (bf16[2,32,1536]{2,1,0:T(8,128)(2,1)S(1)}, bf16[2,32,1536]{2,1,0:T(8,128)(2,1)S(1)}, u32[]{:S(2)}, u32[]{:S(2)}) collective-permute-start(bf16[2,32,1536]{2,1,0:T(8,128)(2,1)S(1)} %get-tuple-element.50), channel_id=1, source_target_pairs={{0,2},{4,6},{1,3},{5,7},{2,0},{6,4},{3,1},{7,5},{8,10},{12,14},{9,... | collective-permute-start | bytes 589832 | tf_op jit(solution)/shard_map/ppermute | solution.py:38
  3.3 8.7 %collective-permute-start.9 = (bf16[2,32,1536]{2,1,0:T(8,128)(2,1)S(1)}, bf16[2,32,1536]{2,1,0:T(8,128)(2,1)S(1)}, u32[]{:S(2)}, u32[]{:S(2)}) collective-permute-start(bf16[2,32,1536]{2,1,0:T(8,128)(2,1)S(1)} %get-tuple-element.51), channel_id=1, source_target_pairs={{2,4},{3,5},{0,1},{6,7},{4,2},{5,3},{1,0},{7,6},{10,12},{11,13},{8... | collective-permute-start | bytes 589832 | tf_op jit(solution)/shard_map/ppermute | solution.py:38
  3.5 8.5 %collective-permute-start.10 = (bf16[2,32,1536]{2,1,0:T(8,128)(2,1)S(1)}, bf16[2,32,1536]{2,1,0:T(8,128)(2,1)S(1)}, u32[]{:S(2)}, u32[]{:S(2)}) collective-permute-start(bf16[2,32,1536]{2,1,0:T(8,128)(2,1)S(1)} %get-tuple-element.52), channel_id=1, source_target_pairs={{0,8},{16,24},{1,9},{17,25},{8,0},{24,16},{9,1},{25,17},{2,10},{18... | collective-permute-start | bytes 589832 | tf_op jit(solution)/shard_map/ppermute | solution.py:38
  4.8 9.4 %collective-permute-start.11 = (bf16[2,32,1536]{2,1,0:T(8,128)(2,1)S(1)}, bf16[2,32,1536]{2,1,0:T(8,128)(2,1)S(1)}, u32[]{:S(2)}, u32[]{:S(2)}) collective-permute-start(bf16[2,32,1536]{2,1,0:T(8,128)(2,1)S(1)} %get-tuple-element.53), channel_id=1, source_target_pairs={{8,16},{9,17},{0,1},{24,25},{16,8},{17,9},{1,0},{25,24},{10,18},{1... | collective-permute-start | bytes 589832 | tf_op jit(solution)/shard_map/ppermute | solution.py:38
  6.1 10.0 %collective-permute-start.2 = (bf16[2,32,1536]{2,1,0:T(8,128)(2,1)S(1)}, bf16[2,32,1536]{2,1,0:T(8,128)(2,1)S(1)}, u32[]{:S(2)}, u32[]{:S(2)}) collective-permute-start(bf16[2,32,1536]{2,1,0:T(8,128)(2,1)S(1)} %get-tuple-element.40), channel_id=1, source_target_pairs={{0,8},{16,24},{1,9},{17,25},{8,0},{24,16},{9,1},{25,17},{2,10},{18... | collective-permute-start | bytes 589832 | tf_op jit(solution)/shard_map/ppermute | solution.py:38
  7.9 8.2 %collective-permute-start.3 = (bf16[2,32,1536]{2,1,0:T(8,128)(2,1)S(1)}, bf16[2,32,1536]{2,1,0:T(8,128)(2,1)S(1)}, u32[]{:S(2)}, u32[]{:S(2)}) collective-permute-start(bf16[2,32,1536]{2,1,0:T(8,128)(2,1)S(1)} %get-tuple-element.41), channel_id=1, source_target_pairs={{8,16},{9,17},{0,1},{24,25},{16,8},{17,9},{1,0},{25,24},{10,18},{1... | collective-permute-start | bytes 589832 | tf_op jit(solution)/shard_map/ppermute | solution.py:38
  12.0 4.9 %collective-permute-start = (bf16[2,32,1536]{2,1,0:T(8,128)(2,1)S(1)}, bf16[2,32,1536]{2,1,0:T(8,128)(2,1)S(1)}, u32[]{:S(2)}, u32[]{:S(2)}) collective-permute-start(bf16[2,32,1536]{2,1,0:T(8,128)(2,1)S(1)} %get-tuple-element.38), channel_id=1, source_target_pairs={{0,2},{4,6},{1,3},{5,7},{2,0},{6,4},{3,1},{7,5},{8,10},{12,14},{9,... | collective-permute-start | bytes 589832 | tf_op jit(solution)/shard_map/ppermute | solution.py:38
  12.0 10.1 %collective-permute-start.1 = (bf16[2,32,1536]{2,1,0:T(8,128)(2,1)S(1)}, bf16[2,32,1536]{2,1,0:T(8,128)(2,1)S(1)}, u32[]{:S(2)}, u32[]{:S(2)}) collective-permute-start(bf16[2,32,1536]{2,1,0:T(8,128)(2,1)S(1)} %get-tuple-element.39), channel_id=1, source_target_pairs={{2,4},{3,5},{0,1},{6,7},{4,2},{5,3},{1,0},{7,6},{10,12},{11,13},{8... | collective-permute-start | bytes 589832 | tf_op jit(solution)/shard_map/ppermute | solution.py:38
  14.2 23.0 %collective-permute-start.12 = (bf16[2,128,1536]{2,1,0:T(8,128)(2,1)S(1)}, bf16[2,128,1536]{2,1,0:T(8,128)(2,1)S(1)}, u32[]{:S(2)}, u32[]{:S(2)}) collective-permute-start(bf16[2,128,1536]{2,1,0:T(8,128)(2,1)S(1)} %kv_near.1), channel_id=1, source_target_pairs={{0,1},{1,0},{2,3},{3,2},{4,5},{5,4},{6,7},{7,6},{8,9},{9,8},{10,11... | collective-permute-start | bytes 2359304 | tf_op jit(solution)/shard_map/ppermute | solution.py:38
  22.2 30.9 %collective-permute-start.4 = (bf16[2,128,1536]{2,1,0:T(8,128)(2,1)S(1)}, bf16[2,128,1536]{2,1,0:T(8,128)(2,1)S(1)}, u32[]{:S(2)}, u32[]{:S(2)}) collective-permute-start(bf16[2,128,1536]{2,1,0:T(8,128)(2,1)S(1)} %qd_near.1), channel_id=1, source_target_pairs={{0,1},{1,0},{2,3},{3,2},{4,5},{5,4},{6,7},{7,6},{8,9},{9,8},{10,11... | collective-permute-start | bytes 2359304 | tf_op jit(solution)/shard_map/ppermute | solution.py:38
  24.4 4.4 %collective-permute-start.13 = (bf16[2,16,1536]{2,1,0:T(8,128)(2,1)S(1)}, bf16[2,16,1536]{2,1,0:T(8,128)(2,1)S(1)}, u32[]{:S(2)}, u32[]{:S(2)}) collective-permute-start(bf16[2,16,1536]{2,1,0:T(8,128)(2,1)S(1)} %get-tuple-element.57), channel_id=1, source_target_pairs={{0,8},{16,24},{1,9},{17,25},{8,0},{24,16},{9,1},{25,17},{2,10},{18... | collective-permute-start | bytes 294920 | tf_op jit(solution)/shard_map/ppermute | solution.py:38
  25.8 4.0 %collective-permute-start.14 = (bf16[2,16,1536]{2,1,0:T(8,128)(2,1)S(1)}, bf16[2,16,1536]{2,1,0:T(8,128)(2,1)S(1)}, u32[]{:S(2)}, u32[]{:S(2)}) collective-permute-start(bf16[2,16,1536]{2,1,0:T(8,128)(2,1)S(1)} %get-tuple-element.58), channel_id=1, source_target_pairs={{8,16},{9,17},{0,1},{24,25},{16,8},{17,9},{1,0},{25,24},{10,18},{1... | collective-permute-start | bytes 294920 | tf_op jit(solution)/shard_map/ppermute | solution.py:38
  25.9 5.2 %collective-permute-start.5 = (bf16[2,16,1536]{2,1,0:T(8,128)(2,1)S(1)}, bf16[2,16,1536]{2,1,0:T(8,128)(2,1)S(1)}, u32[]{:S(2)}, u32[]{:S(2)}) collective-permute-start(bf16[2,16,1536]{2,1,0:T(8,128)(2,1)S(1)} %get-tuple-element.44), channel_id=1, source_target_pairs={{0,2},{4,6},{1,3},{5,7},{2,0},{6,4},{3,1},{7,5},{8,10},{12,14},{9,... | collective-permute-start | bytes 294920 | tf_op jit(solution)/shard_map/ppermute | solution.py:38
  28.8 4.4 %collective-permute-start.6 = (bf16[2,16,1536]{2,1,0:T(8,128)(2,1)S(1)}, bf16[2,16,1536]{2,1,0:T(8,128)(2,1)S(1)}, u32[]{:S(2)}, u32[]{:S(2)}) collective-permute-start(bf16[2,16,1536]{2,1,0:T(8,128)(2,1)S(1)} %get-tuple-element.45), channel_id=1, source_target_pairs={{2,4},{3,5},{0,1},{6,7},{4,2},{5,3},{1,0},{7,6},{10,12},{11,13},{8... | collective-permute-start | bytes 294920 | tf_op jit(solution)/shard_map/ppermute | solution.py:38
  29.8 8.7 %collective-permute-start.15 = (bf16[2,16,1536]{2,1,0:T(8,128)(2,1)S(1)}, bf16[2,16,1536]{2,1,0:T(8,128)(2,1)S(1)}, u32[]{:S(2)}, u32[]{:S(2)}) collective-permute-start(bf16[2,16,1536]{2,1,0:T(8,128)(2,1)S(1)} %kv_far.1), channel_id=1, source_target_pairs={{0,1},{1,0},{2,3},{3,2},{4,5},{5,4},{6,7},{7,6},{8,9},{9,8},{10,11... | collective-permute-start | bytes 294920 | tf_op jit(solution)/shard_map/ppermute | solution.py:38
  33.2 19.5 %collective-permute-start.7 = (bf16[2,16,1536]{2,1,0:T(8,128)(2,1)S(1)}, bf16[2,16,1536]{2,1,0:T(8,128)(2,1)S(1)}, u32[]{:S(2)}, u32[]{:S(2)}) collective-permute-start(bf16[2,16,1536]{2,1,0:T(8,128)(2,1)S(1)} %qd_far.1), channel_id=1, source_target_pairs={{0,1},{1,0},{2,3},{3,2},{4,5},{5,4},{6,7},{7,6},{8,9},{9,8},{10,11... | collective-permute-start | bytes 294920 | tf_op jit(solution)/shard_map/ppermute | solution.py:38
  41.1 2.7 %collective-permute-start.16 = (f32[1,32,128]{2,1,0:T(8,128)S(1)}, f32[1,32,128]{2,1,0:T(8,128)S(1)}, u32[]{:S(2)}, u32[]{:S(2)}) collective-permute-start(f32[1,32,128]{2,1,0:T(8,128)S(1)} %get-tuple-element.61), channel_id=1, source_target_pairs={{0,8},{16,24},{1,9},{17,25},{8,0},{24,16},{9,1},{25,17},{2,10},{18... | collective-permute-start | bytes 49160 | tf_op jit(solution)/shard_map/ppermute | solution.py:38
  42.5 2.6 %collective-permute-start.17 = (f32[1,32,128]{2,1,0:T(8,128)S(1)}, f32[1,32,128]{2,1,0:T(8,128)S(1)}, u32[]{:S(2)}, u32[]{:S(2)}) collective-permute-start(f32[1,32,128]{2,1,0:T(8,128)S(1)} %get-tuple-element.62), channel_id=1, source_target_pairs={{8,16},{9,17},{0,1},{24,25},{16,8},{17,9},{1,0},{25,24},{10,18},{1... | collective-permute-start | bytes 49160 | tf_op jit(solution)/shard_map/ppermute | solution.py:38
  45.1 2.7 %collective-permute-start.19 = (f32[1,48,128]{2,1,0:T(8,128)S(1)}, f32[1,48,128]{2,1,0:T(8,128)S(1)}, u32[]{:S(2)}, u32[]{:S(2)}) collective-permute-start(f32[1,48,128]{2,1,0:T(8,128)S(1)} %get-tuple-element.63), channel_id=1, source_target_pairs={{0,2},{4,6},{1,3},{5,7},{2,0},{6,4},{3,1},{7,5},{8,10},{12,14},{9,... | collective-permute-start | bytes 73736 | tf_op jit(solution)/shard_map/ppermute | solution.py:38
  45.2 3.6 %collective-permute-start.20 = (f32[1,48,128]{2,1,0:T(8,128)S(1)}, f32[1,48,128]{2,1,0:T(8,128)S(1)}, u32[]{:S(2)}, u32[]{:S(2)}) collective-permute-start(f32[1,48,128]{2,1,0:T(8,128)S(1)} %get-tuple-element.64), channel_id=1, source_target_pairs={{2,4},{3,5},{0,1},{6,7},{4,2},{5,3},{1,0},{7,6},{10,12},{11,13},{8... | collective-permute-start | bytes 73736 | tf_op jit(solution)/shard_map/ppermute | solution.py:38
  45.4 8.8 %collective-permute-start.18 = (f32[1,96,128]{2,1,0:T(8,128)S(1)}, f32[1,96,128]{2,1,0:T(8,128)S(1)}, u32[]{:S(2)}, u32[]{:S(2)}) collective-permute-start(f32[1,96,128]{2,1,0:T(8,128)S(1)} %st_near.1), channel_id=1, source_target_pairs={{0,1},{1,0},{2,3},{3,2},{4,5},{5,4},{6,7},{7,6},{8,9},{9,8},{10,11... | collective-permute-start | bytes 147464 | tf_op jit(solution)/shard_map/ppermute | solution.py:38
  48.8 5.4 %collective-permute-start.21 = (f32[1,48,128]{2,1,0:T(8,128)S(1)}, f32[1,48,128]{2,1,0:T(8,128)S(1)}, u32[]{:S(2)}, u32[]{:S(2)}) collective-permute-start(f32[1,48,128]{2,1,0:T(8,128)S(1)} %st_far.1), channel_id=1, source_target_pairs={{0,1},{1,0},{2,3},{3,2},{4,5},{5,4},{6,7},{7,6},{8,9},{9,8},{10,11... | collective-permute-start | bytes 73736 | tf_op jit(solution)/shard_map/ppermute | solution.py:38

commit v6 on v5

--- a/solution.py
+++ b/solution.py
@@ -340,54 +340,28 @@
         m_ref[h, 2:3, :] = jnp.sum(part, axis=0, keepdims=True)
 
 
-def query_kernel(cfg, block, faces, closed_ref, code_ref, near_s_ref, near_g_ref, near_m_ref, *rest):
-    heads, depth, pads, counts = cfg
-    qd_ref, rest = rest[0], rest[1:]
-    kv, rest = rest[: sum(counts)], rest[sum(counts) :]
-    near, far = (kv[: counts[0]], pads[0]), (kv[counts[0] :], pads[1])
-    dq_ref, stat_ref = rest[:2]
-    first_refs = rest[2 : 2 + faces]
-    s_ref, g_ref, d_ref, stat_rows = rest[2 + faces :]
-    scale = 1.0 / math.sqrt(depth)
-    wide = near_s_ref.shape[1]
-    total_rows = code_ref.shape[0]
+def statistics_kernel(cfg, block, faces, closed_ref, code_ref, near_m_ref, qd_ref, *rest):
+    heads, depth, wide, pad, count = cfg
+    far, rest = [(rest[:count], pad)], rest[count:]
+    s_ref, g_ref, stat_rows, stat_ref = rest[:4]
+    first_refs = rest[4:]
     stat_rows[...] = jnp.zeros(stat_rows.shape, jnp.float32)
-
-    def columns(h):
-        return slice(h * depth, (h + 1) * depth)
-
-    def products(h):
-        cols = columns(h)
-        scores = dot(gather([far], 0, cols), qd_ref[0, :, cols], NT) * (scale * LOG2E)
+    for h in range(heads):
+        cols = slice(h * depth, (h + 1) * depth)
+        scores = dot(gather(far, 0, cols), qd_ref[0, :, cols], NT) * (LOG2E / math.sqrt(depth))
+        grads = dot(gather(far, 1, cols), qd_ref[1, :, cols], NT)
         allowed = (code_ref[wide:, :] & closed_ref[0:1, h : h + 1]) == 0
-        s_ref[h % 2] = jnp.where(allowed, scores, NEG)
-        g_ref[h % 2] = dot(gather([far], 1, cols), qd_ref[1, :, cols], NT)
-
-    products(0)
-    for h in range(heads):
-        if h + 1 < heads:
-            products(h + 1)
+        scores = jnp.where(allowed, scores, NEG)
+        s_ref[h] = scores
+        g_ref[h] = grads
         near_peak = near_m_ref[h, 0:1, :]
-        scores, grads = s_ref[h % 2], g_ref[h % 2]
         peak = jnp.maximum(near_peak, jnp.max(scores, axis=0, keepdims=True))
         raised = jnp.exp2(scores - peak)
         lower = jnp.exp2(near_peak - peak)
         total = near_m_ref[h, 1:2, :] * lower + jnp.sum(raised, axis=0, keepdims=True)
         part = near_m_ref[h, 2:3, :] * lower + jnp.sum(raised * grads, axis=0, keepdims=True)
-        drift = part / total
-        logsum = peak + jnp.log2(total)
-        stat_rows[h : h + 1, :] = logsum
-        stat_rows[heads + h : heads + h + 1, :] = drift
-        for r in range(0, total_rows, STEP):
-            if r < wide:
-                scores, grads = near_s_ref[h, r : r + STEP, :], near_g_ref[h, r : r + STEP, :]
-            else:
-                at = slice(r - wide, r - wide + STEP)
-                scores, grads = s_ref[h % 2, at, :], g_ref[h % 2, at, :]
-            attention = jnp.exp2(scores - logsum)
-            d_ref[h % 2, r : r + STEP, :] = (attention * (grads - drift)).astype(jnp.bfloat16)
-        cols = columns(h)
-        put_tiles(dq_ref, dot(d_ref[h % 2], gather([near, far], 0, cols), TN) * scale, cols)
+        stat_rows[h : h + 1, :] = peak + jnp.log2(total)
+        stat_rows[heads + h : heads + h + 1, :] = part / total
     stat_ref[0] = stat_rows[...].T
     T, H, W, C = block
 
@@ -397,6 +371,25 @@
             first_refs[k][0, w * H * C : (w + 1) * H * C, :] = stat_ref[0, r : r + H * C, :]
 
     by_parity("ta", faces, T, put)
+
+
+def query_kernel(cfg, near_s_ref, near_g_ref, far_s_ref, far_g_ref, stat_rows, *rest):
+    heads, depth, pads, counts = cfg
+    near, far = (rest[: counts[0]], pads[0]), (rest[counts[0] : sum(counts)], pads[1])
+    dq_ref, d_ref = rest[sum(counts) :]
+    wide, total_rows = near_s_ref.shape[1], d_ref.shape[1]
+    for h in range(heads):
+        cols = slice(h * depth, (h + 1) * depth)
+        logsum = stat_rows[h : h + 1, :]
+        drift = stat_rows[heads + h : heads + h + 1, :]
+        for r in range(0, total_rows, STEP):
+            i, s_ref, g_ref = (r, near_s_ref, near_g_ref) if r < wide else (r - wide, far_s_ref, far_g_ref)
+            attention = jnp.exp2(s_ref[h, i : i + STEP, :] - logsum)
+            d_ref[h % 2, r : r + STEP, :] = (
+                attention * (g_ref[h, i : i + STEP, :] - drift)
+            ).astype(jnp.bfloat16)
+        product = dot(d_ref[h % 2], gather([near, far], 0, cols), TN) / math.sqrt(depth)
+        put_tiles(dq_ref, product, cols)
 
 
 def statistics_rows(st, pads, block, counts):
@@ -538,18 +531,26 @@
         [closed, query_code, qd] + near,
         name="query_products",
     )
-    kcfg = (heads, depth, pads, (len(near), len(far)))
+    near_s, near_g, near_m = near_products
     made = local(
-        functools.partial(query_kernel, kcfg, block, counts[0]),
-        [pltpu.VMEM(queries.shape, jnp.bfloat16), pltpu.VMEM((1, rows, lanes), jnp.float32)]
+        functools.partial(
+            statistics_kernel, (heads, depth, wide, pads[1], len(far)), block, counts[0]
+        ),
+        [pltpu.VMEM((heads, all_wide - wide, rows), jnp.float32)] * 2
+        + [pltpu.VMEM((lanes, rows), jnp.float32), pltpu.VMEM((1, rows, lanes), jnp.float32)]
         + [pltpu.VMEM((1, W * H * C, lanes), jnp.float32)] * counts[0],
-        [closed, query_code] + near_products + [qd] + near + far,
-        scratch_shapes=[pltpu.VMEM((2, all_wide - wide, rows), jnp.float32)] * 2
-        + [pltpu.VMEM((2, all_wide, rows), jnp.bfloat16), pltpu.VMEM((lanes, rows), jnp.float32)],
+        [closed, query_code, near_m, qd] + far,
+        name="query_statistics",
+    )
+    far_s, far_g, stat_rows, stats = made[:4]
+    (query_gradient,) = local(
+        functools.partial(query_kernel, (heads, depth, pads, (len(near), len(far)))),
+        [pltpu.VMEM(queries.shape, jnp.bfloat16)],
+        [near_s, near_g, far_s, far_g, stat_rows] + near + far,
+        scratch_shapes=[pltpu.VMEM((2, all_wide, rows), jnp.bfloat16)],
         name="query_side",
     )
-    query_gradient, stats = made[:2]
-    st_ta = swap("ta", made[2:])
+    st_ta = swap("ta", made[4:])
     stat_pieces = sum(spread(stats, st_ta, block, counts, "st"), [])
     products = []
     for i, pieces in enumerate((qd_near, qd_far)):

time: 56.9 us -> 56 us (0.984)
  Pallas kernels: 13.8 us -> 13 us
    pallas_call x18 -> x19, Pallas kernels: 13.8 us -> 13 us  [local(): pl.pallas_call(kernel, out_shape=out_shape, in_specs=[place] * len(operan...]
  transfers between devices with their start and end apart: 22 -> 22, of which waited for: 10 -> 10; matrix products, arithmetic and copies ran while one was open for 0% -> 0% of each run, Pallas kernels for 18% -> 17%
where the time goes in v6:
time: 56 us; the launch traced here: 55.7 us
  starting transfers between devices  21.9 us (39%)
  waiting for transfers between devices  20 us (36%)
  Pallas kernels  13 us (23%)
  between operations  0.81 us (1%)
    ppermute x22, starting transfers between devices, swap(): got.append(lax.ppermute(sends[k], axes, pairs))  21.9 us
    ppermute x22, waiting for transfers between devices, swap(): got.append(lax.ppermute(sends[k], axes, pairs))  20 us
    pallas_call x19, Pallas kernels, local(): pl.pallas_call(kernel, out_shape=out_shape, in_specs=[place] * len(operan...  13 us
  transfers between devices with their start and end apart: 22, of which 10 were waited for; matrix products, arithmetic and copies ran while one was open for 0% of the time, Pallas kernels for 17%

profile of v6, /device:TPU:21, one launch (start us, length us, event | category | flops | bytes accessed | tf_op | source)
XLA Modules:
  0.0 55.7 jit_solution(5033924551983029958)
XLA Ops:
  0.6 1.4 %kv_prepare.1 = (bf16[2,32,1536]{2,1,0:T(8,128)(2,1)S(1)}, bf16[2,32,1536]{2,1,0:T(8,128)(2,1)S(1)}, bf16[2,32,1536]{2,1,0:T(8,128)(2,1)S(1)}, bf16[2,32,1536]{2,1,0:T(8,128)(2,1)S(1)}, bf16[2,128,1536]{2,1,0:T(8,128)(2,1)S(1)}) custom-call(bf16[4,4,2,4,1536]{4,3,2,1,0:T(4,128)(2,1)} %refs_0_.4, bf16[4,4,2,4,1536]{4,3,2,1,0:T(4,128)(2,1)} %refs_1_.4), custom_call_target="tpu_custom_call" | custom-call | tf_op jit(solution)/shard_map/kv_prepare/pallas_call | solution.py:146
  2.0 1.3 %collective-permute-start.8 = (bf16[2,32,1536]{2,1,0:T(8,128)(2,1)S(1)}, bf16[2,32,1536]{2,1,0:T(8,128)(2,1)S(1)}, u32[]{:S(2)}, u32[]{:S(2)}) collective-permute-start(bf16[2,32,1536]{2,1,0:T(8,128)(2,1)S(1)} %get-tuple-element.52), channel_id=1, source_target_pairs={{0,2},{4,6},{1,3},{5,7},{2,0},{6,4},{3,1},{7,5},{8,10},{12,14},{9,... | collective-permute-start | bytes 589832 | tf_op jit(solution)/shard_map/ppermute | solution.py:38
  3.3 0.2 collective-permute-start.9
  3.5 1.3 %collective-permute-start.10 = (bf16[2,32,1536]{2,1,0:T(8,128)(2,1)S(1)}, bf16[2,32,1536]{2,1,0:T(8,128)(2,1)S(1)}, u32[]{:S(2)}, u32[]{:S(2)}) collective-permute-start(bf16[2,32,1536]{2,1,0:T(8,128)(2,1)S(1)} %get-tuple-element.54), channel_id=1, source_target_pairs={{0,8},{16,24},{1,9},{17,25},{8,0},{24,16},{9,1},{25,17},{2,10},{18... | collective-permute-start | bytes 589832 | tf_op jit(solution)/shard_map/ppermute | solution.py:38
  4.8 0.0 collective-permute-start.11
  4.8 1.4 %qd_prepare.1 = (bf16[2,32,1536]{2,1,0:T(8,128)(2,1)S(1)}, bf16[2,32,1536]{2,1,0:T(8,128)(2,1)S(1)}, bf16[2,32,1536]{2,1,0:T(8,128)(2,1)S(1)}, bf16[2,32,1536]{2,1,0:T(8,128)(2,1)S(1)}, bf16[2,128,1536]{2,1,0:T(8,128)(2,1)S(1)}) custom-call(bf16[4,4,2,4,1536]{4,3,2,1,0:T(4,128)(2,1)} %refs_0_.5, bf16[4,4,2,4,1536]{4,3,2,1,0:T(4,128)(2,1)} %refs_1_.5), custom_call_target="tpu_custom_call" | custom-call | tf_op jit(solution)/shard_map/qd_prepare/pallas_call | solution.py:146
  6.1 1.7 %collective-permute-start.2 = (bf16[2,32,1536]{2,1,0:T(8,128)(2,1)S(1)}, bf16[2,32,1536]{2,1,0:T(8,128)(2,1)S(1)}, u32[]{:S(2)}, u32[]{:S(2)}) collective-permute-start(bf16[2,32,1536]{2,1,0:T(8,128)(2,1)S(1)} %get-tuple-element.42), channel_id=1, source_target_pairs={{0,8},{16,24},{1,9},{17,25},{8,0},{24,16},{9,1},{25,17},{2,10},{18... | collective-permute-start | bytes 589832 | tf_op jit(solution)/shard_map/ppermute | solution.py:38
  7.9 0.0 collective-permute-done.8.refs_1_.rest_1_.refs_0_
  7.9 0.2 collective-permute-start.3
  8.1 3.9 %collective-permute-done.9.refs_2_.rest_2_.refs_1_ = bf16[2,32,1536]{2,1,0:T(8,128)(2,1)S(1)} collective-permute-done((bf16[2,32,1536]{2,1,0:T(8,128)(2,1)S(1)}, bf16[2,32,1536]{2,1,0:T(8,128)(2,1)S(1)}, u32[]{:S(2)}, u32[]{:S(2)}) %collective-permute-start.9) | collective-permute-done | bytes 196640 | tf_op jit(solution)/shard_map/ppermute | solution.py:38
  12.0 0.0 collective-permute-start
  12.0 0.0 collective-permute-done.10.refs_3_.rest_3_
  12.0 2.2 %collective-permute-start.1 = (bf16[2,32,1536]{2,1,0:T(8,128)(2,1)S(1)}, bf16[2,32,1536]{2,1,0:T(8,128)(2,1)S(1)}, u32[]{:S(2)}, u32[]{:S(2)}) collective-permute-start(bf16[2,32,1536]{2,1,0:T(8,128)(2,1)S(1)} %get-tuple-element.41), channel_id=1, source_target_pairs={{2,4},{3,5},{0,1},{6,7},{4,2},{5,3},{1,0},{7,6},{10,12},{11,13},{8... | collective-permute-start | bytes 589832 | tf_op jit(solution)/shard_map/ppermute | solution.py:38
  14.2 0.0 collective-permute-done.11.refs_4_.rest_4_
  14.2 0.1 kv_near.1
  14.2 1.9 %collective-permute-start.12 = (bf16[2,128,1536]{2,1,0:T(8,128)(2,1)S(1)}, bf16[2,128,1536]{2,1,0:T(8,128)(2,1)S(1)}, u32[]{:S(2)}, u32[]{:S(2)}) collective-permute-start(bf16[2,128,1536]{2,1,0:T(8,128)(2,1)S(1)} %kv_near.1), channel_id=1, source_target_pairs={{0,1},{1,0},{2,3},{3,2},{4,5},{5,4},{6,7},{7,6},{8,9},{9,8},{10,11... | collective-permute-start | bytes 2359304 | tf_op jit(solution)/shard_map/ppermute | solution.py:38
  16.1 0.0 collective-permute-done.2.refs_3_.rest_3_.refs_0_.refs_8_
  16.1 0.0 collective-permute-done.3.refs_4_.rest_4_.refs_1_.refs_9_
  16.1 0.8 %collective-permute-done.refs_1_.rest_1_.refs_6_ = bf16[2,32,1536]{2,1,0:T(8,128)(2,1)S(1)} collective-permute-done((bf16[2,32,1536]{2,1,0:T(8,128)(2,1)S(1)}, bf16[2,32,1536]{2,1,0:T(8,128)(2,1)S(1)}, u32[]{:S(2)}, u32[]{:S(2)}) %collective-permute-start) | collective-permute-done | bytes 196640 | tf_op jit(solution)/shard_map/ppermute | solution.py:38
  16.9 5.2 %collective-permute-done.1.refs_2_.rest_2_.refs_7_ = bf16[2,32,1536]{2,1,0:T(8,128)(2,1)S(1)} collective-permute-done((bf16[2,32,1536]{2,1,0:T(8,128)(2,1)S(1)}, bf16[2,32,1536]{2,1,0:T(8,128)(2,1)S(1)}, u32[]{:S(2)}, u32[]{:S(2)}) %collective-permute-start.1) | collective-permute-done | bytes 196640 | tf_op jit(solution)/shard_map/ppermute | solution.py:38
  22.1 0.1 qd_near.1
  22.2 2.2 %collective-permute-start.4 = (bf16[2,128,1536]{2,1,0:T(8,128)(2,1)S(1)}, bf16[2,128,1536]{2,1,0:T(8,128)(2,1)S(1)}, u32[]{:S(2)}, u32[]{:S(2)}) collective-permute-start(bf16[2,128,1536]{2,1,0:T(8,128)(2,1)S(1)} %qd_near.1), channel_id=1, source_target_pairs={{0,1},{1,0},{2,3},{3,2},{4,5},{5,4},{6,7},{7,6},{8,9},{9,8},{10,11... | collective-permute-start | bytes 2359304 | tf_op jit(solution)/shard_map/ppermute | solution.py:38
  24.4 0.1 kv_corner.1
  24.4 1.4 %collective-permute-start.13 = (bf16[2,16,1536]{2,1,0:T(8,128)(2,1)S(1)}, bf16[2,16,1536]{2,1,0:T(8,128)(2,1)S(1)}, u32[]{:S(2)}, u32[]{:S(2)}) collective-permute-start(bf16[2,16,1536]{2,1,0:T(8,128)(2,1)S(1)} %get-tuple-element.59), channel_id=1, source_target_pairs={{0,8},{16,24},{1,9},{17,25},{8,0},{24,16},{9,1},{25,17},{2,10},{18... | collective-permute-start | bytes 294920 | tf_op jit(solution)/shard_map/ppermute | solution.py:38
  25.8 0.0 collective-permute-start.14
  25.8 0.1 qd_corner.1
  25.9 0.1 collective-permute-start.5
  25.9 2.9 %collective-permute-done.13.refs_0_.rest_0_.rest_6_ = bf16[2,16,1536]{2,1,0:T(8,128)(2,1)S(1)} collective-permute-done((bf16[2,16,1536]{2,1,0:T(8,128)(2,1)S(1)}, bf16[2,16,1536]{2,1,0:T(8,128)(2,1)S(1)}, u32[]{:S(2)}, u32[]{:S(2)}) %collective-permute-start.13) | collective-permute-done | bytes 98336 | tf_op jit(solution)/shard_map/ppermute | solution.py:38
  28.8 0.2 collective-permute-start.6
  29.0 0.8 %collective-permute-done.14.refs_1_.rest_1_.rest_7_ = bf16[2,16,1536]{2,1,0:T(8,128)(2,1)S(1)} collective-permute-done((bf16[2,16,1536]{2,1,0:T(8,128)(2,1)S(1)}, bf16[2,16,1536]{2,1,0:T(8,128)(2,1)S(1)}, u32[]{:S(2)}, u32[]{:S(2)}) %collective-permute-start.14) | collective-permute-done | bytes 98336 | tf_op jit(solution)/shard_map/ppermute | solution.py:38
  29.8 1.2 %collective-permute-start.15 = (bf16[2,16,1536]{2,1,0:T(8,128)(2,1)S(1)}, bf16[2,16,1536]{2,1,0:T(8,128)(2,1)S(1)}, u32[]{:S(2)}, u32[]{:S(2)}) collective-permute-start(bf16[2,16,1536]{2,1,0:T(8,128)(2,1)S(1)} %kv_far.1), channel_id=1, source_target_pairs={{0,1},{1,0},{2,3},{3,2},{4,5},{5,4},{6,7},{7,6},{8,9},{9,8},{10,11... | collective-permute-start | bytes 294920 | tf_op jit(solution)/shard_map/ppermute | solution.py:38
  31.1 0.0 collective-permute-done.5.refs_0_.rest_0_.refs_11_
  31.1 2.1 %collective-permute-done.6.refs_1_.rest_1_.refs_12_ = bf16[2,16,1536]{2,1,0:T(8,128)(2,1)S(1)} collective-permute-done((bf16[2,16,1536]{2,1,0:T(8,128)(2,1)S(1)}, bf16[2,16,1536]{2,1,0:T(8,128)(2,1)S(1)}, u32[]{:S(2)}, u32[]{:S(2)}) %collective-permute-start.6) | collective-permute-done | bytes 98336 | tf_op jit(solution)/shard_map/ppermute | solution.py:38
  33.2 2.1 %collective-permute-start.7 = (bf16[2,16,1536]{2,1,0:T(8,128)(2,1)S(1)}, bf16[2,16,1536]{2,1,0:T(8,128)(2,1)S(1)}, u32[]{:S(2)}, u32[]{:S(2)}) collective-permute-start(bf16[2,16,1536]{2,1,0:T(8,128)(2,1)S(1)} %qd_far.1), channel_id=1, source_target_pairs={{0,1},{1,0},{2,3},{3,2},{4,5},{5,4},{6,7},{7,6},{8,9},{9,8},{10,11... | collective-permute-start | bytes 294920 | tf_op jit(solution)/shard_map/ppermute | solution.py:38
  35.3 1.9 %query_codes.1 = (s32[512,128]{1,0:T(8,128)S(1)}, s32[8,12]{1,0:T(8,128)S(1)}) custom-call(s32[8,128]{1,0:T(8,128)} %constant.6.clone.refs_0_, s32[8,512]{1,0:T(8,128)} %constant.7.clone.refs_1_, s32[16,4,16]{2,1,0:T(4,128)} %bitcast.2, s32[3,12]{1,0:T(4,128)} %bitcast.4), custom_call_target="tpu_custom_call" | custom-call | tf_op jit(solution)/shard_map/query_codes/pallas_call | solution.py:146
  37.3 0.0 collective-permute-done.12.rest_5_
  37.3 1.3 %query_products.1 = (f32[12,384,128]{2,1,0:T(8,128)S(1)}, f32[12,384,128]{2,1,0:T(8,128)S(1)}, f32[12,8,128]{2,1,0:T(8,128)S(1)}) custom-call(s32[8,12]{1,0:T(8,128)S(1)} %get-tuple-element.50.closed_ref, s32[512,128]{1,0:T(8,128)S(1)} %get-tuple-element.51.code_ref, bf16[2,128,1536]{2,1,0:T(8,128)(2,1)S(1)} %get-tuple-element.39.refs_0_.rest_0_.own_ref.qd_ref.refs_5_, ...), custom_call_target="tpu_custom_call" | custom-call | tf_op jit(solution)/shard_map/query_products/pallas_call | solution.py:146
  38.5 0.0 collective-permute-done.15.rest_2_.rest_8_
  38.6 0.8 %query_statistics.1 = (f32[12,128,128]{2,1,0:T(8,128)S(1)}, f32[12,128,128]{2,1,0:T(8,128)S(1)}, f32[128,128]{1,0:T(8,128)S(1)}, f32[1,128,128]{2,1,0:T(8,128)S(...) custom-call(s32[8,12]{1,0:T(8,128)S(1)} %get-tuple-element.50.closed_ref, ...), custom_call_target="tpu_custom_call" | custom-call | tf_op jit(solution)/shard_map/query_statistics/pallas_call | solution.py:146
  39.4 1.3 %collective-permute-start.16 = (f32[1,32,128]{2,1,0:T(8,128)S(1)}, f32[1,32,128]{2,1,0:T(8,128)S(1)}, u32[]{:S(2)}, u32[]{:S(2)}) collective-permute-start(f32[1,32,128]{2,1,0:T(8,128)S(1)} %get-tuple-element.65), channel_id=1, source_target_pairs={{0,8},{16,24},{1,9},{17,25},{8,0},{24,16},{9,1},{25,17},{2,10},{18... | collective-permute-start | bytes 49160 | tf_op jit(solution)/shard_map/ppermute | solution.py:38
  40.8 0.0 collective-permute-start.17
  40.8 1.3 %collective-permute-done.16.refs_1_.refs_0_.refs_15_ = f32[1,32,128]{2,1,0:T(8,128)S(1)} collective-permute-done((f32[1,32,128]{2,1,0:T(8,128)S(1)}, f32[1,32,128]{2,1,0:T(8,128)S(1)}, u32[]{:S(2)}, u32[]{:S(2)}) %collective-permute-start.16) | collective-permute-done | bytes 16416 | tf_op jit(solution)/shard_map/ppermute | solution.py:38
  42.1 1.3 %collective-permute-done.17.refs_2_.refs_1_.refs_16_ = f32[1,32,128]{2,1,0:T(8,128)S(1)} collective-permute-done((f32[1,32,128]{2,1,0:T(8,128)S(1)}, f32[1,32,128]{2,1,0:T(8,128)S(1)}, u32[]{:S(2)}, u32[]{:S(2)}) %collective-permute-start.17) | collective-permute-done | bytes 16416 | tf_op jit(solution)/shard_map/ppermute | solution.py:38
  43.4 0.1 collective-permute-start.19
  43.4 0.3 collective-permute-start.20
  43.7 1.7 %collective-permute-start.18 = (f32[1,96,128]{2,1,0:T(8,128)S(1)}, f32[1,96,128]{2,1,0:T(8,128)S(1)}, u32[]{:S(2)}, u32[]{:S(2)}) collective-permute-start(f32[1,96,128]{2,1,0:T(8,128)S(1)} %st_near.1), channel_id=1, source_target_pairs={{0,1},{1,0},{2,3},{3,2},{4,5},{5,4},{6,7},{7,6},{8,9},{9,8},{10,11... | collective-permute-start | bytes 147464 | tf_op jit(solution)/shard_map/ppermute | solution.py:38
  45.4 0.7 %collective-permute-done.19.refs_0_.refs_18_ = f32[1,48,128]{2,1,0:T(8,128)S(1)} collective-permute-done((f32[1,48,128]{2,1,0:T(8,128)S(1)}, f32[1,48,128]{2,1,0:T(8,128)S(1)}, u32[]{:S(2)}, u32[]{:S(2)}) %collective-permute-start.19) | collective-permute-done | bytes 24608 | tf_op jit(solution)/shard_map/ppermute | solution.py:38
  46.1 1.0 %collective-permute-done.20.refs_1_.refs_19_ = f32[1,48,128]{2,1,0:T(8,128)S(1)} collective-permute-done((f32[1,48,128]{2,1,0:T(8,128)S(1)}, f32[1,48,128]{2,1,0:T(8,128)S(1)}, u32[]{:S(2)}, u32[]{:S(2)}) %collective-permute-start.20) | collective-permute-done | bytes 24608 | tf_op jit(solution)/shard_map/ppermute | solution.py:38
  47.1 2.6 %collective-permute-start.21 = (f32[1,48,128]{2,1,0:T(8,128)S(1)}, f32[1,48,128]{2,1,0:T(8,128)S(1)}, u32[]{:S(2)}, u32[]{:S(2)}) collective-permute-start(f32[1,48,128]{2,1,0:T(8,128)S(1)} %st_far.1), channel_id=1, source_target_pairs={{0,1},{1,0},{2,3},{3,2},{4,5},{5,4},{6,7},{7,6},{8,9},{9,8},{10,11... | collective-permute-start | bytes 73736 | tf_op jit(solution)/shard_map/ppermute | solution.py:38
  49.7 1.3 %key_codes.1 = (s32[128,512]{1,0:T(8,128)S(1)}, s32[8,12]{1,0:T(8,128)S(1)}) custom-call(s32[8,128]{1,0:T(8,128)} %constant.6.clone.refs_0_, s32[8,512]{1,0:T(8,128)} %constant.8.clone.refs_1_, s32[16,4,16]{2,1,0:T(4,128)} %bitcast.3, s32[3,12]{1,0:T(4,128)} %bitcast.5), custom_call_target="tpu_custom_call" | custom-call | tf_op jit(solution)/shard_map/key_codes/pallas_call | solution.py:146
  51.0 0.0 collective-permute-done.7.rest_2_.refs_13_
  51.0 0.4 key_products_1.1
  51.4 0.0 collective-permute-done.4.rest_5_.refs_10_
  51.4 1.1 %key_products_0.1 = (f32[12,128,384]{2,1,0:T(8,128)S(1)}, f32[12,128,384]{2,1,0:T(8,128)S(1)}) custom-call(s32[8,12]{1,0:T(8,128)S(1)} %get-tuple-element.36.closed_ref, s32[128,512]{1,0:T(8,128)S(1)} %get-tuple-element.37.code_ref, bf16[2,128,1536]{2,1,0:T(8,128)(2,1)S(1)} %get-tuple-element.38.own_ref.refs_0_.rest_0_, ...), custom_call_target="tpu_custom_call" | custom-call | tf_op jit(solution)/shard_map/key_products_0/pallas_call | solution.py:146
  52.5 0.9 %query_side.1.refs_4_ = bf16[4,4,2,4,1536]{4,3,2,1,0:T(4,128)(2,1)S(1)} custom-call(f32[12,384,128]{2,1,0:T(8,128)S(1)} %get-tuple-element.56.near_s_ref, f32[12,384,128]{2,1,0:T(8,128)S(1)} %get-tuple-element.57.near_g_ref, f32[12,128,128]{2,1,0:T(8,128)S(1)} %get-tuple-element.61.far_s_ref, f32[12,128,128]{2,1,0:T(8,128)S(1)} %get-tuple-element.62.far_g_ref, ...), custom_call_target="tpu_custom_call" | custom-call | tf_op jit(solution)/shard_map/query_side/pallas_call | solution.py:146
  53.4 0.0 collective-permute-done.21.refs_20_
  53.4 0.0 collective-permute-done.18.refs_17_
  53.4 2.3 %key_side.1 = (bf16[4,4,2,4,1536]{4,3,2,1,0:T(4,128)(2,1)}, bf16[4,4,2,4,1536]{4,3,2,1,0:T(4,128)(2,1)}, bf16[4,4,2,4,1536]{4,3,2,1,0:T(4,128)(2,1)}) custom-call(f32[12,128,384]{2,1,0:T(8,128)S(1)} %get-tuple-element.44.refs_0_, f32[12,128,384]{2,1,0:T(8,128)S(1)} %get-tuple-element.45.refs_1_, f32[12,128,128]{2,1,0:T(8,128)S(1)} %get-tuple-element.48.refs_2_, ...), custom_call_target="tpu_custom_call" | custom-call | tf_op jit(solution)/shard_map/key_side/pallas_call | solution.py:146
  (5 shorter events, 0.0 us)
Async XLA Ops:
  2.0 5.9 %collective-permute-start.8 = (bf16[2,32,1536]{2,1,0:T(8,128)(2,1)S(1)}, bf16[2,32,1536]{2,1,0:T(8,128)(2,1)S(1)}, u32[]{:S(2)}, u32[]{:S(2)}) collective-permute-start(bf16[2,32,1536]{2,1,0:T(8,128)(2,1)S(1)} %get-tuple-element.52), channel_id=1, source_target_pairs={{0,2},{4,6},{1,3},{5,7},{2,0},{6,4},{3,1},{7,5},{8,10},{12,14},{9,... | collective-permute-start | bytes 589832 | tf_op jit(solution)/shard_map/ppermute | solution.py:38
  3.3 8.7 %collective-permute-start.9 = (bf16[2,32,1536]{2,1,0:T(8,128)(2,1)S(1)}, bf16[2,32,1536]{2,1,0:T(8,128)(2,1)S(1)}, u32[]{:S(2)}, u32[]{:S(2)}) collective-permute-start(bf16[2,32,1536]{2,1,0:T(8,128)(2,1)S(1)} %get-tuple-element.53), channel_id=1, source_target_pairs={{2,4},{3,5},{0,1},{6,7},{4,2},{5,3},{1,0},{7,6},{10,12},{11,13},{8... | collective-permute-start | bytes 589832 | tf_op jit(solution)/shard_map/ppermute | solution.py:38
  3.5 8.5 %collective-permute-start.10 = (bf16[2,32,1536]{2,1,0:T(8,128)(2,1)S(1)}, bf16[2,32,1536]{2,1,0:T(8,128)(2,1)S(1)}, u32[]{:S(2)}, u32[]{:S(2)}) collective-permute-start(bf16[2,32,1536]{2,1,0:T(8,128)(2,1)S(1)} %get-tuple-element.54), channel_id=1, source_target_pairs={{0,8},{16,24},{1,9},{17,25},{8,0},{24,16},{9,1},{25,17},{2,10},{18... | collective-permute-start | bytes 589832 | tf_op jit(solution)/shard_map/ppermute | solution.py:38
  4.8 9.4 %collective-permute-start.11 = (bf16[2,32,1536]{2,1,0:T(8,128)(2,1)S(1)}, bf16[2,32,1536]{2,1,0:T(8,128)(2,1)S(1)}, u32[]{:S(2)}, u32[]{:S(2)}) collective-permute-start(bf16[2,32,1536]{2,1,0:T(8,128)(2,1)S(1)} %get-tuple-element.55), channel_id=1, source_target_pairs={{8,16},{9,17},{0,1},{24,25},{16,8},{17,9},{1,0},{25,24},{10,18},{1... | collective-permute-start | bytes 589832 | tf_op jit(solution)/shard_map/ppermute | solution.py:38
  6.1 10.0 %collective-permute-start.2 = (bf16[2,32,1536]{2,1,0:T(8,128)(2,1)S(1)}, bf16[2,32,1536]{2,1,0:T(8,128)(2,1)S(1)}, u32[]{:S(2)}, u32[]{:S(2)}) collective-permute-start(bf16[2,32,1536]{2,1,0:T(8,128)(2,1)S(1)} %get-tuple-element.42), channel_id=1, source_target_pairs={{0,8},{16,24},{1,9},{17,25},{8,0},{24,16},{9,1},{25,17},{2,10},{18... | collective-permute-start | bytes 589832 | tf_op jit(solution)/shard_map/ppermute | solution.py:38
  7.9 8.2 %collective-permute-start.3 = (bf16[2,32,1536]{2,1,0:T(8,128)(2,1)S(1)}, bf16[2,32,1536]{2,1,0:T(8,128)(2,1)S(1)}, u32[]{:S(2)}, u32[]{:S(2)}) collective-permute-start(bf16[2,32,1536]{2,1,0:T(8,128)(2,1)S(1)} %get-tuple-element.43), channel_id=1, source_target_pairs={{8,16},{9,17},{0,1},{24,25},{16,8},{17,9},{1,0},{25,24},{10,18},{1... | collective-permute-start | bytes 589832 | tf_op jit(solution)/shard_map/ppermute | solution.py:38
  12.0 4.9 %collective-permute-start = (bf16[2,32,1536]{2,1,0:T(8,128)(2,1)S(1)}, bf16[2,32,1536]{2,1,0:T(8,128)(2,1)S(1)}, u32[]{:S(2)}, u32[]{:S(2)}) collective-permute-start(bf16[2,32,1536]{2,1,0:T(8,128)(2,1)S(1)} %get-tuple-element.40), channel_id=1, source_target_pairs={{0,2},{4,6},{1,3},{5,7},{2,0},{6,4},{3,1},{7,5},{8,10},{12,14},{9,... | collective-permute-start | bytes 589832 | tf_op jit(solution)/shard_map/ppermute | solution.py:38
  12.0 10.1 %collective-permute-start.1 = (bf16[2,32,1536]{2,1,0:T(8,128)(2,1)S(1)}, bf16[2,32,1536]{2,1,0:T(8,128)(2,1)S(1)}, u32[]{:S(2)}, u32[]{:S(2)}) collective-permute-start(bf16[2,32,1536]{2,1,0:T(8,128)(2,1)S(1)} %get-tuple-element.41), channel_id=1, source_target_pairs={{2,4},{3,5},{0,1},{6,7},{4,2},{5,3},{1,0},{7,6},{10,12},{11,13},{8... | collective-permute-start | bytes 589832 | tf_op jit(solution)/shard_map/ppermute | solution.py:38
  14.2 23.0 %collective-permute-start.12 = (bf16[2,128,1536]{2,1,0:T(8,128)(2,1)S(1)}, bf16[2,128,1536]{2,1,0:T(8,128)(2,1)S(1)}, u32[]{:S(2)}, u32[]{:S(2)}) collective-permute-start(bf16[2,128,1536]{2,1,0:T(8,128)(2,1)S(1)} %kv_near.1), channel_id=1, source_target_pairs={{0,1},{1,0},{2,3},{3,2},{4,5},{5,4},{6,7},{7,6},{8,9},{9,8},{10,11... | collective-permute-start | bytes 2359304 | tf_op jit(solution)/shard_map/ppermute | solution.py:38
  22.2 29.2 %collective-permute-start.4 = (bf16[2,128,1536]{2,1,0:T(8,128)(2,1)S(1)}, bf16[2,128,1536]{2,1,0:T(8,128)(2,1)S(1)}, u32[]{:S(2)}, u32[]{:S(2)}) collective-permute-start(bf16[2,128,1536]{2,1,0:T(8,128)(2,1)S(1)} %qd_near.1), channel_id=1, source_target_pairs={{0,1},{1,0},{2,3},{3,2},{4,5},{5,4},{6,7},{7,6},{8,9},{9,8},{10,11... | collective-permute-start | bytes 2359304 | tf_op jit(solution)/shard_map/ppermute | solution.py:38
  24.4 4.4 %collective-permute-start.13 = (bf16[2,16,1536]{2,1,0:T(8,128)(2,1)S(1)}, bf16[2,16,1536]{2,1,0:T(8,128)(2,1)S(1)}, u32[]{:S(2)}, u32[]{:S(2)}) collective-permute-start(bf16[2,16,1536]{2,1,0:T(8,128)(2,1)S(1)} %get-tuple-element.59), channel_id=1, source_target_pairs={{0,8},{16,24},{1,9},{17,25},{8,0},{24,16},{9,1},{25,17},{2,10},{18... | collective-permute-start | bytes 294920 | tf_op jit(solution)/shard_map/ppermute | solution.py:38
  25.8 4.0 %collective-permute-start.14 = (bf16[2,16,1536]{2,1,0:T(8,128)(2,1)S(1)}, bf16[2,16,1536]{2,1,0:T(8,128)(2,1)S(1)}, u32[]{:S(2)}, u32[]{:S(2)}) collective-permute-start(bf16[2,16,1536]{2,1,0:T(8,128)(2,1)S(1)} %get-tuple-element.60), channel_id=1, source_target_pairs={{8,16},{9,17},{0,1},{24,25},{16,8},{17,9},{1,0},{25,24},{10,18},{1... | collective-permute-start | bytes 294920 | tf_op jit(solution)/shard_map/ppermute | solution.py:38
  25.9 5.2 %collective-permute-start.5 = (bf16[2,16,1536]{2,1,0:T(8,128)(2,1)S(1)}, bf16[2,16,1536]{2,1,0:T(8,128)(2,1)S(1)}, u32[]{:S(2)}, u32[]{:S(2)}) collective-permute-start(bf16[2,16,1536]{2,1,0:T(8,128)(2,1)S(1)} %get-tuple-element.46), channel_id=1, source_target_pairs={{0,2},{4,6},{1,3},{5,7},{2,0},{6,4},{3,1},{7,5},{8,10},{12,14},{9,... | collective-permute-start | bytes 294920 | tf_op jit(solution)/shard_map/ppermute | solution.py:38
  28.8 4.4 %collective-permute-start.6 = (bf16[2,16,1536]{2,1,0:T(8,128)(2,1)S(1)}, bf16[2,16,1536]{2,1,0:T(8,128)(2,1)S(1)}, u32[]{:S(2)}, u32[]{:S(2)}) collective-permute-start(bf16[2,16,1536]{2,1,0:T(8,128)(2,1)S(1)} %get-tuple-element.47), channel_id=1, source_target_pairs={{2,4},{3,5},{0,1},{6,7},{4,2},{5,3},{1,0},{7,6},{10,12},{11,13},{8... | collective-permute-start | bytes 294920 | tf_op jit(solution)/shard_map/ppermute | solution.py:38
  29.8 8.7 %collective-permute-start.15 = (bf16[2,16,1536]{2,1,0:T(8,128)(2,1)S(1)}, bf16[2,16,1536]{2,1,0:T(8,128)(2,1)S(1)}, u32[]{:S(2)}, u32[]{:S(2)}) collective-permute-start(bf16[2,16,1536]{2,1,0:T(8,128)(2,1)S(1)} %kv_far.1), channel_id=1, source_target_pairs={{0,1},{1,0},{2,3},{3,2},{4,5},{5,4},{6,7},{7,6},{8,9},{9,8},{10,11... | collective-permute-start | bytes 294920 | tf_op jit(solution)/shard_map/ppermute | solution.py:38
  33.2 17.7 %collective-permute-start.7 = (bf16[2,16,1536]{2,1,0:T(8,128)(2,1)S(1)}, bf16[2,16,1536]{2,1,0:T(8,128)(2,1)S(1)}, u32[]{:S(2)}, u32[]{:S(2)}) collective-permute-start(bf16[2,16,1536]{2,1,0:T(8,128)(2,1)S(1)} %qd_far.1), channel_id=1, source_target_pairs={{0,1},{1,0},{2,3},{3,2},{4,5},{5,4},{6,7},{7,6},{8,9},{9,8},{10,11... | collective-permute-start | bytes 294920 | tf_op jit(solution)/shard_map/ppermute | solution.py:38
  39.4 2.7 %collective-permute-start.16 = (f32[1,32,128]{2,1,0:T(8,128)S(1)}, f32[1,32,128]{2,1,0:T(8,128)S(1)}, u32[]{:S(2)}, u32[]{:S(2)}) collective-permute-start(f32[1,32,128]{2,1,0:T(8,128)S(1)} %get-tuple-element.65), channel_id=1, source_target_pairs={{0,8},{16,24},{1,9},{17,25},{8,0},{24,16},{9,1},{25,17},{2,10},{18... | collective-permute-start | bytes 49160 | tf_op jit(solution)/shard_map/ppermute | solution.py:38
  40.8 2.6 %collective-permute-start.17 = (f32[1,32,128]{2,1,0:T(8,128)S(1)}, f32[1,32,128]{2,1,0:T(8,128)S(1)}, u32[]{:S(2)}, u32[]{:S(2)}) collective-permute-start(f32[1,32,128]{2,1,0:T(8,128)S(1)} %get-tuple-element.66), channel_id=1, source_target_pairs={{8,16},{9,17},{0,1},{24,25},{16,8},{17,9},{1,0},{25,24},{10,18},{1... | collective-permute-start | bytes 49160 | tf_op jit(solution)/shard_map/ppermute | solution.py:38
  43.4 2.7 %collective-permute-start.19 = (f32[1,48,128]{2,1,0:T(8,128)S(1)}, f32[1,48,128]{2,1,0:T(8,128)S(1)}, u32[]{:S(2)}, u32[]{:S(2)}) collective-permute-start(f32[1,48,128]{2,1,0:T(8,128)S(1)} %get-tuple-element.67), channel_id=1, source_target_pairs={{0,2},{4,6},{1,3},{5,7},{2,0},{6,4},{3,1},{7,5},{8,10},{12,14},{9,... | collective-permute-start | bytes 73736 | tf_op jit(solution)/shard_map/ppermute | solution.py:38
  43.4 3.6 %collective-permute-start.20 = (f32[1,48,128]{2,1,0:T(8,128)S(1)}, f32[1,48,128]{2,1,0:T(8,128)S(1)}, u32[]{:S(2)}, u32[]{:S(2)}) collective-permute-start(f32[1,48,128]{2,1,0:T(8,128)S(1)} %get-tuple-element.68), channel_id=1, source_target_pairs={{2,4},{3,5},{0,1},{6,7},{4,2},{5,3},{1,0},{7,6},{10,12},{11,13},{8... | collective-permute-start | bytes 73736 | tf_op jit(solution)/shard_map/ppermute | solution.py:38
  43.7 9.7 %collective-permute-start.18 = (f32[1,96,128]{2,1,0:T(8,128)S(1)}, f32[1,96,128]{2,1,0:T(8,128)S(1)}, u32[]{:S(2)}, u32[]{:S(2)}) collective-permute-start(f32[1,96,128]{2,1,0:T(8,128)S(1)} %st_near.1), channel_id=1, source_target_pairs={{0,1},{1,0},{2,3},{3,2},{4,5},{5,4},{6,7},{7,6},{8,9},{9,8},{10,11... | collective-permute-start | bytes 147464 | tf_op jit(solution)/shard_map/ppermute | solution.py:38
  47.1 6.3 %collective-permute-start.21 = (f32[1,48,128]{2,1,0:T(8,128)S(1)}, f32[1,48,128]{2,1,0:T(8,128)S(1)}, u32[]{:S(2)}, u32[]{:S(2)}) collective-permute-start(f32[1,48,128]{2,1,0:T(8,128)S(1)} %st_far.1), channel_id=1, source_target_pairs={{0,1},{1,0},{2,3},{3,2},{4,5},{5,4},{6,7},{7,6},{8,9},{9,8},{10,11... | collective-permute-start | bytes 73736 | tf_op jit(solution)/shard_map/ppermute | solution.py:38
